TPU v7x, 32 devices: a whole 2x2x4 slice. The times are simulated.
32 devices in a mesh: dp: 8 (over y, x, core), tensor: 4 (over z).
Axes of the slice: x: 2, y: 2, z: 4, core: 2. Of those that a mesh axis runs over, the one named last changes fastest.
Arguments:
- tokens: bfloat16 [8192, 2048], P('dp', 'tensor'), may hold values from -6 to 6
- cotangent: bfloat16 [8192, 2048], P('dp', 'tensor'), may hold values from -6 to 6
- first_gain: bfloat16 [2048], P('dp'), may hold values from 0.099609375 to 1.8984375
- first_shift: bfloat16 [2048], P('dp'), may hold values from -1.75 to 1.75
- attention_in: bfloat16 [3, 2048, 2048], P(None, 'dp', 'tensor'), may hold values from -0.125 to 0.125
- attention_bias: bfloat16 [2, 32, 64], P(None, 'tensor', 'dp'), may hold values from -3 to 3
- attention_out: bfloat16 [2048, 2048], P('tensor', 'dp'), may hold values from -0.5 to 0.5
- out_bias: bfloat16 [2048], P('dp'), may hold values from -1.75 to 1.75
- second_gain: bfloat16 [2048], P('dp'), may hold values from 0.099609375 to 1.8984375
- second_shift: bfloat16 [2048], P('dp'), may hold values from -1.75 to 1.75
- up_weight: bfloat16 [2048, 8192], P('dp', 'tensor'), may hold values from -0.125 to 0.125
- up_bias: bfloat16 [32, 256], P('tensor', 'dp'), may hold values from -3 to 3
- down_weight: bfloat16 [8192, 2048], P('tensor', 'dp'), may hold values from -0.0625 to 0.0625
- down_bias: bfloat16 [2048], P('dp'), may hold values from -1.75 to 1.75
- source_block: int32 [64], P('dp'), may hold values from 0 to 63, as said below
- target_block: int32 [64], P('dp'), may hold values from 0 to 63, as said below
- block_fill: int32 [64], P('dp'), may hold values from 1 to 128, as said below
- block_start: int32 [64], P('dp'), may hold values from 0 to 0, as said below
Outputs:
- output: bfloat16 [8192, 2048], P('dp', 'tensor')
- input_grad: bfloat16 [8192, 2048], P('dp', 'tensor')
- first_gain_grad: float32 [2048], P('dp')
- first_shift_grad: float32 [2048], P('dp')
- attention_in_grad: float32 [3, 2048, 2048], P(None, 'dp', 'tensor')
- attention_bias_grad: float32 [2, 32, 64], P(None, 'tensor', 'dp')
- attention_out_grad: float32 [2048, 2048], P('tensor', 'dp')
- out_bias_grad: float32 [2048], P('dp')
- second_gain_grad: float32 [2048], P('dp')
- second_shift_grad: float32 [2048], P('dp')
- up_weight_grad: float32 [2048, 8192], P('dp', 'tensor')
- up_bias_grad: float32 [32, 256], P('tensor', 'dp')
- down_weight_grad: float32 [8192, 2048], P('tensor', 'dp')
- down_bias_grad: float32 [2048], P('dp')
Inputs may be any that keep to these rules, and one draw needn't show every extreme that they name: `source_block`: a permutation of the 64 anchor blocks. `target_block`: the inverse permutation of source_block. `block_fill`: 128 in every block but the last of a sequence; a sequence has 128 to 1024 tokens; the first sequence of every bin has 1024 tokens. `block_start`: every bin holds whole sequences of consecutive blocks, each of 1 to 8 blocks; blocks of one sequence share this value and the sequence's first block equals it; where a bin has more than 8 blocks, its last block is a sequence of its own.
All inputs are finite; a program needn't handle non-finite values.
Results may differ from a plain program's by a relative error of at most 0.024.
Values may be sent and summed in bfloat16 or wider, within the bound.
No kernel may reach another device: no remote copies, remote signals or barrier semaphores. Data moves between devices by JAX's collectives and lax.ppermute only.
A program may use at most 256 MiB of HBM per device.

v0:
```python
import jax
import jax.numpy as jnp
from jax import lax
from jax.sharding import PartitionSpec as P

H = 32
BLK = 128
MAXLEN = 1024
QB = 512


norm_eps = 1e-05
masked_score = -1e30
density_scale = 0.3989422804014327
root_half = 0.7071067811865476


def normalize(rows):
    mean = jnp.mean(rows, axis=-1, keepdims=True)
    centred = rows - mean
    variance = jnp.mean(centred * centred, axis=-1, keepdims=True)
    scale = lax.rsqrt(variance + norm_eps)
    return (centred * scale, scale)


def norm_back(grad_norm, unit, scale, gain):
    grad_unit = grad_norm * gain
    mean_grad = jnp.mean(grad_unit, axis=-1, keepdims=True)
    mean_dot = jnp.mean(grad_unit * unit, axis=-1, keepdims=True)
    return scale * (grad_unit - mean_grad - unit * mean_dot)


def spread(table):
    return jnp.broadcast_to(table[:, None], (table.shape[0], BLK)).reshape(-1)


def bins_move(first_rows, second_rows, wanted):
    empty = (jnp.zeros_like(first_rows), jnp.zeros_like(second_rows))
    pieces = (
        lax.all_gather(first_rows, "dp", axis=0, tiled=True),
        lax.all_gather(second_rows, "dp", axis=0, tiled=True),
    )
    piece_rows = pieces[0].shape[0]
    inside = (wanted >= 0) & (wanted < piece_rows)
    clipped = jnp.clip(wanted, 0, piece_rows - 1)
    return (
        jnp.where(inside[:, None], pieces[0][clipped], empty[0]),
        jnp.where(inside[:, None], pieces[1][clipped], empty[1]),
    )


def gather_rows(value):
    return lax.all_gather(value, "tensor", axis=0, tiled=True)


def sum_rows(value):
    return lax.psum_scatter(
        value.astype(jnp.bfloat16), "tensor", scatter_dimension=0, tiled=True
    ).astype(jnp.float32)


def on_device(
    tokens,
    cotangent,
    first_gain,
    first_shift,
    attention_in,
    attention_bias,
    attention_out,
    out_bias,
    second_gain,
    second_shift,
    up_weight,
    up_bias,
    down_weight,
    down_bias,
    source_block,
    target_block,
    block_fill,
    block_start,
):
    f32 = jnp.float32
    bf16 = jnp.bfloat16
    tensor_count = lax.axis_size("tensor")
    tensor_rank = lax.axis_index("tensor")
    bin_slots = tokens.shape[0]
    row_count = bin_slots // tensor_count
    offset = jnp.arange(bin_slots, dtype=jnp.int32) % BLK
    block_of = jnp.arange(bin_slots, dtype=jnp.int32) // BLK
    segment = spread(block_start)
    valid_slot = offset < spread(block_fill)
    place = (block_of - segment) * BLK + offset
    anchor_rows = spread(source_block) * BLK + offset
    bin_rows = spread(target_block) * BLK + offset
    valid_rows = lax.dynamic_slice_in_dim(valid_slot, tensor_rank * row_count, row_count)
    gathered = bins_move(tokens, cotangent, anchor_rows)
    rows_in, grad_in = (
        lax.all_to_all(gathered[0], "tensor", split_axis=0, concat_axis=1, tiled=True),
        lax.all_to_all(gathered[1], "tensor", split_axis=0, concat_axis=1, tiled=True),
    )
    full = (
        lax.all_gather(first_gain, "dp", axis=0, tiled=True),
        lax.all_gather(first_shift, "dp", axis=0, tiled=True),
        lax.all_gather(attention_in, "dp", axis=1, tiled=True),
        lax.all_gather(attention_bias, "dp", axis=2, tiled=True),
        lax.all_gather(attention_out, "dp", axis=1, tiled=True),
        lax.all_gather(out_bias, "dp", axis=0, tiled=True),
        lax.all_gather(second_gain, "dp", axis=0, tiled=True),
        lax.all_gather(second_shift, "dp", axis=0, tiled=True),
        lax.all_gather(up_weight, "dp", axis=0, tiled=True),
        lax.all_gather(up_bias, "dp", axis=1, tiled=True),
        lax.all_gather(down_weight, "dp", axis=1, tiled=True),
        lax.all_gather(down_bias, "dp", axis=0, tiled=True),
    )
    (
        gain_one,
        shift_one,
        in_proj,
        attn_bias,
        out_proj,
        out_shift,
        gain_two,
        shift_two,
        up_full,
        up_shift,
        down_full,
        down_shift,
    ) = full
    rows_x = rows_in.astype(f32)
    unit_one, scale_one = normalize(rows_x)
    norm_one = (unit_one * gain_one.astype(f32) + shift_one.astype(f32)).astype(bf16)
    norm_all = gather_rows(norm_one)
    query = (
        jnp.dot(norm_all, in_proj[0], preferred_element_type=f32)
        + attn_bias[0].reshape(-1).astype(f32)
    ).astype(bf16)
    keys = jnp.dot(norm_all, in_proj[1], preferred_element_type=f32).astype(bf16)
    values = (
        jnp.dot(norm_all, in_proj[2], preferred_element_type=f32)
        + attn_bias[1].reshape(-1).astype(f32)
    ).astype(bf16)
    heads_here = attn_bias.shape[1]
    head_size = attn_bias.shape[2]
    width = heads_here * head_size
    head_ids = tensor_rank * heads_here + jnp.arange(heads_here, dtype=jnp.int32)
    slopes = jnp.exp2(-8.0 * (head_ids + 1).astype(f32) / H)
    keys_pad = jnp.concatenate([jnp.zeros((MAXLEN, width), bf16), keys])
    values_pad = jnp.concatenate([jnp.zeros((MAXLEN, width), bf16), values])
    segment_pad = jnp.concatenate([jnp.full((MAXLEN,), -1, jnp.int32), segment])
    place_pad = jnp.concatenate([jnp.zeros((MAXLEN,), jnp.int32), place])
    valid_pad = jnp.concatenate([jnp.zeros((MAXLEN,), dtype=bool), valid_slot])
    window = QB + MAXLEN
    block_count = bin_slots // QB

    def block_scores(begin):
        query_block = lax.dynamic_slice_in_dim(query, begin, QB).reshape(QB, heads_here, head_size)
        key_block = lax.dynamic_slice_in_dim(keys_pad, begin, window).reshape(
            window, heads_here, head_size
        )
        value_block = lax.dynamic_slice_in_dim(values_pad, begin, window).reshape(
            window, heads_here, head_size
        )
        query_segment = lax.dynamic_slice_in_dim(segment, begin, QB)
        query_place = lax.dynamic_slice_in_dim(place, begin, QB)
        key_segment = lax.dynamic_slice_in_dim(segment_pad, begin, window)
        key_place = lax.dynamic_slice_in_dim(place_pad, begin, window)
        key_valid = lax.dynamic_slice_in_dim(valid_pad, begin, window)
        raw = jnp.einsum("qhe,khe->hqk", query_block, key_block, preferred_element_type=f32) * 0.125
        distance = (query_place[:, None] - key_place[None, :]).astype(f32)
        raw = raw - slopes[:, None, None] * distance[None]
        allowed = (
            (query_segment[:, None] == key_segment[None, :])
            & (key_place[None, :] <= query_place[:, None])
            & key_valid[None, :]
        )
        return (jnp.where(allowed[None], raw, masked_score), query_block, key_block, value_block)

    def forward_block(index, carry):
        attended_now, log_now = carry
        begin = index * QB
        scores, query_block, key_block, value_block = block_scores(begin)
        top = jnp.max(scores, axis=-1, keepdims=True)
        total = jnp.sum(jnp.exp(scores - top), axis=-1, keepdims=True)
        block_log = top + jnp.log(total)
        weights = jnp.exp(scores - block_log).astype(bf16)
        mixed = jnp.einsum(
            "hqk,khe->qhe", weights, value_block, preferred_element_type=f32
        ).reshape(QB, width)
        attended_now = lax.dynamic_update_slice_in_dim(attended_now, mixed.astype(bf16), begin, 0)
        log_now = lax.dynamic_update_slice_in_dim(log_now, block_log, begin, 1)
        return (attended_now, log_now)

    attended, log_total = lax.fori_loop(
        0,
        block_count,
        forward_block,
        (jnp.zeros((bin_slots, width), bf16), jnp.zeros((heads_here, bin_slots, 1), f32)),
    )
    attn_rows = sum_rows(jnp.dot(attended, out_proj, preferred_element_type=f32))
    resid = rows_x + attn_rows + out_shift.astype(f32)
    unit_two, scale_two = normalize(resid)
    norm_two = (unit_two * gain_two.astype(f32) + shift_two.astype(f32)).astype(bf16)
    norm_two_all = gather_rows(norm_two)
    before = jnp.dot(norm_two_all, up_full, preferred_element_type=f32) + up_shift.reshape(
        -1
    ).astype(f32)
    hidden = jax.nn.gelu(before, approximate=False).astype(bf16)
    branch_rows = sum_rows(jnp.dot(hidden, down_full, preferred_element_type=f32))
    result = resid + branch_rows + down_shift.astype(f32)
    output_rows = jnp.where(valid_rows[:, None], result, 0.0).astype(bf16)
    full = (
        lax.all_gather(first_gain, "dp", axis=0, tiled=True),
        lax.all_gather(first_shift, "dp", axis=0, tiled=True),
        lax.all_gather(attention_in, "dp", axis=1, tiled=True),
        lax.all_gather(attention_bias, "dp", axis=2, tiled=True),
        lax.all_gather(attention_out, "dp", axis=1, tiled=True),
        lax.all_gather(out_bias, "dp", axis=0, tiled=True),
        lax.all_gather(second_gain, "dp", axis=0, tiled=True),
        lax.all_gather(second_shift, "dp", axis=0, tiled=True),
        lax.all_gather(up_weight, "dp", axis=0, tiled=True),
        lax.all_gather(up_bias, "dp", axis=1, tiled=True),
        lax.all_gather(down_weight, "dp", axis=1, tiled=True),
        lax.all_gather(down_bias, "dp", axis=0, tiled=True),
    )
    (
        gain_one,
        shift_one,
        in_proj,
        attn_bias,
        out_proj,
        out_shift,
        gain_two,
        shift_two,
        up_full,
        up_shift,
        down_full,
        down_shift,
    ) = full
    grad_rows = jnp.where(valid_rows[:, None], grad_in.astype(f32), 0.0)
    down_bias_grad = jnp.sum(grad_rows, axis=0)
    grad_branch = gather_rows(grad_rows.astype(bf16))
    down_weight_grad = jnp.einsum("tf,td->fd", hidden, grad_branch, preferred_element_type=f32)
    grad_hidden = jnp.einsum("td,fd->tf", grad_branch, down_full, preferred_element_type=f32)
    gelu_slope = (
        0.5 * (1.0 + jax.scipy.special.erf(before * root_half))
        + before * jnp.exp(-0.5 * before * before) * density_scale
    )
    grad_before = (grad_hidden * gelu_slope).astype(bf16)
    up_bias_grad = jnp.sum(grad_before, axis=0, dtype=f32).reshape(heads_here, -1)
    up_weight_grad = jnp.einsum("td,tf->df", norm_two_all, grad_before, preferred_element_type=f32)
    grad_norm_two = sum_rows(
        jnp.einsum("tf,df->td", grad_before, up_full, preferred_element_type=f32)
    )
    second_gain_grad = jnp.sum(grad_norm_two * unit_two, axis=0)
    second_shift_grad = jnp.sum(grad_norm_two, axis=0)
    grad_resid = grad_rows + norm_back(grad_norm_two, unit_two, scale_two, gain_two.astype(f32))
    out_bias_grad = jnp.sum(grad_resid, axis=0)
    grad_attn = gather_rows(grad_resid.astype(bf16))
    attention_out_grad = jnp.einsum("tc,td->cd", attended, grad_attn, preferred_element_type=f32)
    grad_attended = jnp.einsum("td,cd->tc", grad_attn, out_proj, preferred_element_type=f32).astype(
        bf16
    )

    def backward_block(index, carry):
        grad_query, grad_keys, grad_values = carry
        begin = index * QB
        scores, query_block, key_block, value_block = block_scores(begin)
        block_log = lax.dynamic_slice_in_dim(log_total, begin, QB, 1)
        probs = jnp.exp(scores - block_log)
        grad_block = lax.dynamic_slice_in_dim(grad_attended, begin, QB).reshape(
            QB, heads_here, head_size
        )
        grad_probs = jnp.einsum("qhe,khe->hqk", grad_block, value_block, preferred_element_type=f32)
        inner = jnp.sum(probs * grad_probs, axis=-1, keepdims=True)
        grad_scores = (probs * (grad_probs - inner)).astype(bf16)
        query_part = (
            jnp.einsum("hqk,khe->qhe", grad_scores, key_block, preferred_element_type=f32) * 0.125
        )
        key_part = (
            jnp.einsum("hqk,qhe->khe", grad_scores, query_block, preferred_element_type=f32) * 0.125
        )
        value_part = jnp.einsum(
            "hqk,qhe->khe", probs.astype(bf16), grad_block, preferred_element_type=f32
        )
        grad_query = lax.dynamic_update_slice_in_dim(
            grad_query, query_part.reshape(QB, width), begin, 0
        )
        old_keys = lax.dynamic_slice_in_dim(grad_keys, begin, window)
        grad_keys = lax.dynamic_update_slice_in_dim(
            grad_keys, old_keys + key_part.reshape(window, width), begin, 0
        )
        old_values = lax.dynamic_slice_in_dim(grad_values, begin, window)
        grad_values = lax.dynamic_update_slice_in_dim(
            grad_values, old_values + value_part.reshape(window, width), begin, 0
        )
        return (grad_query, grad_keys, grad_values)

    padded_zero = jnp.zeros((MAXLEN + bin_slots, width), f32)
    grad_query, grad_keys, grad_values = lax.fori_loop(
        0,
        block_count,
        backward_block,
        (jnp.zeros((bin_slots, width), f32), padded_zero, padded_zero),
    )
    grad_query = grad_query.astype(bf16)
    grad_keys = grad_keys[MAXLEN:].astype(bf16)
    grad_values = grad_values[MAXLEN:].astype(bf16)
    attention_in_grad = jnp.stack(
        [
            jnp.einsum("td,tc->dc", norm_all, grad_query, preferred_element_type=f32),
            jnp.einsum("td,tc->dc", norm_all, grad_keys, preferred_element_type=f32),
            jnp.einsum("td,tc->dc", norm_all, grad_values, preferred_element_type=f32),
        ]
    )
    attention_bias_grad = jnp.stack(
        [jnp.sum(grad_query, axis=0, dtype=f32), jnp.sum(grad_values, axis=0, dtype=f32)]
    ).reshape(2, heads_here, head_size)
    grad_norm_partial = jnp.einsum("tc,dc->td", grad_query, in_proj[0], preferred_element_type=f32)
    grad_norm_partial = grad_norm_partial + jnp.einsum(
        "tc,dc->td", grad_keys, in_proj[1], preferred_element_type=f32
    )
    grad_norm_partial = grad_norm_partial + jnp.einsum(
        "tc,dc->td", grad_values, in_proj[2], preferred_element_type=f32
    )
    grad_norm_one = sum_rows(grad_norm_partial)
    first_gain_grad = jnp.sum(grad_norm_one * unit_one, axis=0)
    first_shift_grad = jnp.sum(grad_norm_one, axis=0)
    grad_tokens = grad_resid + norm_back(grad_norm_one, unit_one, scale_one, gain_one.astype(f32))
    input_rows = grad_tokens.astype(bf16)
    (
        first_gain_grad,
        first_shift_grad,
        out_bias_grad,
        second_gain_grad,
        second_shift_grad,
        down_bias_grad,
    ) = (
        lax.psum(first_gain_grad.astype(jnp.bfloat16), "tensor").astype(jnp.float32),
        lax.psum(first_shift_grad.astype(jnp.bfloat16), "tensor").astype(jnp.float32),
        lax.psum(out_bias_grad.astype(jnp.bfloat16), "tensor").astype(jnp.float32),
        lax.psum(second_gain_grad.astype(jnp.bfloat16), "tensor").astype(jnp.float32),
        lax.psum(second_shift_grad.astype(jnp.bfloat16), "tensor").astype(jnp.float32),
        lax.psum(down_bias_grad.astype(jnp.bfloat16), "tensor").astype(jnp.float32),
    )
    reduced = (
        lax.psum_scatter(
            first_gain_grad.astype(jnp.bfloat16), "dp", scatter_dimension=0, tiled=True
        ).astype(jnp.float32),
        lax.psum_scatter(
            first_shift_grad.astype(jnp.bfloat16), "dp", scatter_dimension=0, tiled=True
        ).astype(jnp.float32),
        lax.psum_scatter(
            attention_in_grad.astype(jnp.bfloat16), "dp", scatter_dimension=1, tiled=True
        ).astype(jnp.float32),
        lax.psum_scatter(
            attention_bias_grad.astype(jnp.bfloat16), "dp", scatter_dimension=2, tiled=True
        ).astype(jnp.float32),
        lax.psum_scatter(
            attention_out_grad.astype(jnp.bfloat16), "dp", scatter_dimension=1, tiled=True
        ).astype(jnp.float32),
        lax.psum_scatter(
            out_bias_grad.astype(jnp.bfloat16), "dp", scatter_dimension=0, tiled=True
        ).astype(jnp.float32),
        lax.psum_scatter(
            second_gain_grad.astype(jnp.bfloat16), "dp", scatter_dimension=0, tiled=True
        ).astype(jnp.float32),
        lax.psum_scatter(
            second_shift_grad.astype(jnp.bfloat16), "dp", scatter_dimension=0, tiled=True
        ).astype(jnp.float32),
        lax.psum_scatter(
            up_weight_grad.astype(jnp.bfloat16), "dp", scatter_dimension=0, tiled=True
        ).astype(jnp.float32),
        lax.psum_scatter(
            up_bias_grad.astype(jnp.bfloat16), "dp", scatter_dimension=1, tiled=True
        ).astype(jnp.float32),
        lax.psum_scatter(
            down_weight_grad.astype(jnp.bfloat16), "dp", scatter_dimension=1, tiled=True
        ).astype(jnp.float32),
        lax.psum_scatter(
            down_bias_grad.astype(jnp.bfloat16), "dp", scatter_dimension=0, tiled=True
        ).astype(jnp.float32),
    )
    gain_one_grad = reduced[0]
    shift_one_grad = reduced[1]
    out_shift_grad = reduced[5]
    gain_two_grad = reduced[6]
    shift_two_grad = reduced[7]
    down_shift_grad = reduced[11]
    columns = (
        lax.all_to_all(output_rows, "tensor", split_axis=1, concat_axis=0, tiled=True),
        lax.all_to_all(input_rows, "tensor", split_axis=1, concat_axis=0, tiled=True),
    )
    final = bins_move(columns[0], columns[1], bin_rows)
    return (
        final[0],
        final[1],
        gain_one_grad,
        shift_one_grad,
        reduced[2],
        reduced[3],
        reduced[4],
        out_shift_grad,
        gain_two_grad,
        shift_two_grad,
        reduced[8],
        reduced[9],
        reduced[10],
        down_shift_grad,
    )


def solution(mesh):
    return jax.shard_map(
        on_device,
        mesh=mesh,
        in_specs=(
            P("dp", "tensor"),
            P("dp", "tensor"),
            P("dp"),
            P("dp"),
            P(None, "dp", "tensor"),
            P(None, "tensor", "dp"),
            P("tensor", "dp"),
            P("dp"),
            P("dp"),
            P("dp"),
            P("dp", "tensor"),
            P("tensor", "dp"),
            P("tensor", "dp"),
            P("dp"),
            P("dp"),
            P("dp"),
            P("dp"),
            P("dp"),
        ),
        out_specs=(
            P("dp", "tensor"),
            P("dp", "tensor"),
            P("dp"),
            P("dp"),
            P(None, "dp", "tensor"),
            P(None, "tensor", "dp"),
            P("tensor", "dp"),
            P("dp"),
            P("dp"),
            P("dp"),
            P("dp", "tensor"),
            P("tensor", "dp"),
            P("tensor", "dp"),
            P("dp"),
        ),
        check_vma=False,
    )
```

profile of v0, /device:TPU:0, one launch (start us, length us, event | category | flops | bytes accessed | tf_op | source)
XLA Modules:
  0.0 1712.6 jit_solution(3325952922458523042)
XLA Ops:
  10.3 56.5 %all-gather.36.cloned.1.call-done = bf16[8192,512]{1,0:T(8,128)(2,1)} async-done(((bf16[1024,512]{1,0:T(8,128)(2,1)}), bf16[8192,512]{1,0:T(8,128)(2,1)}) %all-gather.36.cloned.1.call-update) | async-done | bytes 8388624 | tf_op jit(solution)/shard_map/all_gather | solution.py:41
  66.9 8.4 gather_fusion.2
  75.3 47.7 %all-gather.20.cloned.1.call-done = bf16[8192,512]{1,0:T(8,128)(2,1)} async-done(((bf16[1024,512]{1,0:T(8,128)(2,1)}), bf16[8192,512]{1,0:T(8,128)(2,1)}) %all-gather.20.cloned.1.call-update) | async-done | bytes 8388624 | tf_op jit(solution)/shard_map/all_gather | solution.py:40
  123.1 8.4 gather_fusion
  137.7 9.0 all-gather.1
  146.8 8.2 all-gather
  154.9 8.9 all-to-all-done
  168.1 9.1 all_gather.71
  177.6 75.6 %all-gather.22.cloned.1.call-done = bf16[1024,2048]{1,0:T(8,128)(2,1)} async-done(((bf16[256,2048]{1,0:T(8,128)(2,1)}), bf16[1024,2048]{1,0:T(8,128)(2,1)}) %all-gather.22.cloned.1.call-update) | async-done | bytes 4194320 | tf_op jit(solution)/shard_map/all_gather | solution.py:53
  277.8 74.9 %while.34 = (s32[]{:T(128)}, bf16[1024,512]{0,1:T(8,128)(2,1)}, f32[8,1024,1]{1,0,2:T(8,128)S(1)}, bf16[2048,512]{0,1:T(8,128)(2,1)S(1)}, s32[1024]{0:T(1024)S(1...) while((s32[]{:T(128)}, bf16[1024,512]{0,1:T(8,128)(2,1)}, ...), condition=%wide.region_5.6_spmd.clone, body=%wide.region_2.5_spmd.clone.sunk | while | flops 1672212480 | bytes 112915352 | solution.py:193
  279.6 12.7 fusion.137
  292.3 11.3 exponential_reduce_fusion.2
  303.6 10.4 fusion.138
  316.9 12.7 fusion.137
  329.6 11.3 exponential_reduce_fusion.2
  340.9 10.4 fusion.138
  352.8 6.4 convolution_convert_fusion.4
  360.1 8.9 all-gather.4
  369.0 8.9 all-gather.3
  377.9 8.0 all-gather.2
  385.9 48.6 %reduce-scatter.13.cloned.1.call-done = bf16[256,2048]{1,0:T(8,128)(2,1)} async-done(((bf16[1024,2048]{1,0:T(8,128)(2,1)}), bf16[256,2048]{1,0:T(8,128)(2,1)}) %reduce-scatter.13.cloned.1.call-update) | async-done | bytes 1048592 | tf_op jit(solution)/shard_map/reduce_scatter | solution.py:57
  444.8 26.2 %all-to-all-done.2 = bf16[4,256,512]{2,1,0:T(8,128)(2,1)} async-done(((bf16[4,256,512]{2,1,0:T(8,128)(2,1)}), bf16[4,256,512]{2,1,0:T(8,128)(2,1)}, u32[]{:S(2)}, u32[]{:S(2)}) %all-to-all-start.2) | async-done | bytes 1048608 | tf_op jit(solution)/shard_map/all_to_all | solution.py:99
  475.3 9.2 all-gather.5
  484.6 6.7 all-gather.30.cloned.1.call-done
  491.3 82.9 %all-gather.28.cloned.1.call-done = bf16[1024,2048]{1,0:T(8,128)(2,1)} async-done(((bf16[256,2048]{1,0:T(8,128)(2,1)}), bf16[1024,2048]{1,0:T(8,128)(2,1)}) %all-gather.28.cloned.1.call-update) | async-done | bytes 4194320 | tf_op jit(solution)/shard_map/all_gather | solution.py:53
  574.2 30.8 %fusion.11 = (bf16[1024,2048]{1,0:T(8,128)(2,1)}, f32[1024,2048]{1,0:T(8,128)}) fusion(f32[2048]{0:T(1024)S(1)} %bitcast.250, bf16[1024,2048]{1,0:T(8,128)(2,1)} %all-gather.28.cloned.1.call-done, bf16[2048,2048]{1,0:T(8,128)(2,1)} %all-gather.30.cloned.1.call-done), kind=kOutput, calls=%fused_computation.45 | convolution fusion | flops 8728346624 | bytes 25174016 | tf_op jit(solution)/shard_map/dot_general | solution.py:204
  605.0 25.5 %all-gather.32.cloned.1.call-done = bf16[2048,2048]{1,0:T(8,128)(2,1)} async-done(((bf16[2048,256]{1,0:T(8,128)(2,1)}), bf16[2048,2048]{1,0:T(8,128)(2,1)}) %all-gather.32.cloned.1.call-update) | async-done | bytes 8388624 | tf_op jit(solution)/shard_map/all_gather | solution.py:112
  630.5 82.8 %all-gather.38.cloned.1.call-done = bf16[1024,2048]{1,0:T(8,128)(2,1)} async-done(((bf16[256,2048]{1,0:T(8,128)(2,1)}), bf16[1024,2048]{1,0:T(8,128)(2,1)}) %all-gather.38.cloned.1.call-update) | async-done | bytes 4194320 | tf_op jit(solution)/shard_map/all_gather | solution.py:53
  713.2 17.0 fusion.77
  732.2 10.7 convolution_convert_fusion.2
  742.9 13.9 convolution_convert_fusion.3
  757.5 8.9 all-gather.6
  766.4 51.9 %reduce-scatter.17.cloned.1.call-done = bf16[256,2048]{1,0:T(8,128)(2,1)} async-done(((bf16[1024,2048]{1,0:T(8,128)(2,1)}), bf16[256,2048]{1,0:T(8,128)(2,1)}) %reduce-scatter.17.cloned.1.call-update) | async-done | bytes 1048592 | tf_op jit(solution)/shard_map/reduce_scatter | solution.py:57
  821.7 76.1 %reduce-scatter.15.cloned.1.call-done = bf16[256,2048]{1,0:T(8,128)(2,1)} async-done(((bf16[1024,2048]{1,0:T(8,128)(2,1)}), bf16[256,2048]{1,0:T(8,128)(2,1)}) %reduce-scatter.15.cloned.1.call-update) | async-done | bytes 1048592 | tf_op jit(solution)/shard_map/reduce_scatter | solution.py:57
  905.9 81.4 %all-gather.40.cloned.1.call-done = bf16[1024,2048]{1,0:T(8,128)(2,1)} async-done(((bf16[256,2048]{1,0:T(8,128)(2,1)}), bf16[1024,2048]{1,0:T(8,128)(2,1)}) %all-gather.40.cloned.1.call-update) | async-done | bytes 4194320 | tf_op jit(solution)/shard_map/all_gather | solution.py:53
  987.2 6.2 convolution_convert_fusion.9
  999.7 172.5 %while.35 = (s32[]{:T(128)}, bf16[1024,512]{0,1:T(8,128)(2,1)}, f32[2048,512]{0,1:T(8,128)}, f32[2048,512]{0,1:T(8,128)}, bf16[2048,512]{0,1:T(8,128)(2,1)}, /*i...) while((s32[]{:T(128)}, bf16[1024,512]{0,1:T(8,128)(2,1)}, ...), condition=%wide.region_15.16_spmd.clone, body=%wide.region_13.15_spmd.clone.sunk | while | flops 4103335936 | bytes 300561568 | solution.py:299
  1009.1 10.1 fusion.149
  1019.2 21.5 %multiply_reduce_fusion.3 = (f32[8,512]{1,0:T(8,128)S(1)}, f32[8,512,1536]{2,1,0:T(8,128)}) fusion(f32[8,512,1536]{2,1,0:T(8,128)} %fusion.149, f32[8,512]{1,0:T(8,128)S(1)} %dynamic-slice_bitcast_fusion.2, f32[512,1536]{1,0:T(8,128)} %subtract_convert_fusion.5, f32[8]{0:T(128)S(1)} %multiply_exponential_fusion.5, ...), kind=kOutput, calls=%fused_computation.22.clone.1 | convolution fusion | flops 849342464 | bytes 56393760 | tf_op jit(solution)/shard_map/while/body/eval_jaxpr/qhe,khe->hqk/dot_general | solution.py:168
  1040.7 16.4 multiply_convert_fusion.2
  1057.0 12.1 fusion.150
  1069.1 6.1 convolution_multiply_fusion.4
  1079.5 6.5 constant_dynamic-update-slice_fusion.9
  1095.0 10.1 fusion.149
  1105.1 21.5 %multiply_reduce_fusion.3 = (f32[8,512]{1,0:T(8,128)S(1)}, f32[8,512,1536]{2,1,0:T(8,128)}) fusion(f32[8,512,1536]{2,1,0:T(8,128)} %fusion.149, f32[8,512]{1,0:T(8,128)S(1)} %dynamic-slice_bitcast_fusion.2, f32[512,1536]{1,0:T(8,128)} %subtract_convert_fusion.5, f32[8]{0:T(128)S(1)} %multiply_exponential_fusion.5, ...), kind=kOutput, calls=%fused_computation.22.clone.1 | convolution fusion | flops 849342464 | bytes 56393760 | tf_op jit(solution)/shard_map/while/body/eval_jaxpr/qhe,khe->hqk/dot_general | solution.py:168
  1126.6 16.4 multiply_convert_fusion.2
  1143.0 12.1 fusion.150
  1165.5 6.5 constant_dynamic-update-slice_fusion.9
  1176.8 7.7 fusion.49
  1184.6 8.8 add_convert_fusion
  1194.9 14.1 convolution_convert_fusion
  1209.1 14.3 convolution_convert_fusion.1
  1245.3 45.7 %all_to_all.58 = bf16[256,4,512]{2,0,1:T(8,128)(2,1)} all-to-all(bf16[256,4,512]{2,0,1:T(8,128)(2,1)S(1)} %bitcast.227), channel_id=1, replica_groups=mesh['dp'=8,'tensor'=4] {'tensor'}, dimensions={1} | all-to-all | bytes 2097152 | tf_op jit(solution)/shard_map/all_to_all | solution.py:390
  1295.6 29.3 %all_to_all.59 = bf16[256,4,512]{2,0,1:T(8,128)(2,1)} all-to-all(bf16[256,4,512]{2,0,1:T(8,128)(2,1)S(1)} %bitcast.228), channel_id=1, replica_groups=mesh['dp'=8,'tensor'=4] {'tensor'}, dimensions={1} | all-to-all | bytes 2097152 | tf_op jit(solution)/shard_map/all_to_all | solution.py:391
  1330.1 68.8 %reduce-scatter.27.cloned.1.call-done = bf16[2048,256]{1,0:T(8,128)(2,1)} async-done(((bf16[2048,2048]{1,0:T(8,128)(2,1)}), bf16[2048,256]{1,0:T(8,128)(2,1)}) %reduce-scatter.27.cloned.1.call-update) | async-done | bytes 1048592 | tf_op jit(solution)/shard_map/reduce_scatter | solution.py:376
  1401.6 72.1 %reduce-scatter.25.cloned.1.call-done = bf16[256,2048]{1,0:T(8,128)(2,1)} async-done(((bf16[2048,2048]{1,0:T(8,128)(2,1)}), bf16[256,2048]{1,0:T(8,128)(2,1)}) %reduce-scatter.25.cloned.1.call-update) | async-done | bytes 1048592 | tf_op jit(solution)/shard_map/reduce_scatter | solution.py:370
  1479.9 38.1 %reduce-scatter.23.cloned.1.call-done = bf16[512,256]{1,0:T(8,128)(2,1)} async-done(((bf16[512,2048]{1,0:T(8,128)(2,1)}), bf16[512,256]{1,0:T(8,128)(2,1)}) %reduce-scatter.23.cloned.1.call-update) | async-done | bytes 262160 | tf_op jit(solution)/shard_map/reduce_scatter | solution.py:358
  1520.0 23.4 %all-reduce.12 = (bf16[2048]{0:T(1024)(128)(2,1)S(1)}, bf16[2048]{0:T(1024)(128)(2,1)S(1)}, bf16[2,8,64]{2,1,0:T(8,128)(2,1)S(1)}, bf16[2048]{0:T(1024)(128)(2,1...) all-reduce(bf16[2048]{0:T(1024)(128)(2,1)S(1)} %get-tuple-element.6, ...), channel_id=6, replica_groups=mesh['dp'=8,'tensor'=4] {'dp'}, use_global_device_ids=true, to_apply=%region_21.22.clone | all-reduce | flops 13312 | bytes 53248
  1543.9 11.7 all-reduce.13
  1559.6 23.5 %reduce-scatter.21.cloned.1.call-done = bf16[3,256,512]{2,1,0:T(8,128)(2,1)} async-done(((bf16[3,2048,512]{2,1,0:T(8,128)(2,1)}), bf16[3,256,512]{2,1,0:T(8,128)(2,1)}) %reduce-scatter.21.cloned.1.call-update) | async-done | bytes 786448 | tf_op jit(solution)/shard_map/reduce_scatter | solution.py:352
  1585.6 53.5 %all-gather.34.cloned.1.call-done = bf16[8192,512]{1,0:T(8,128)(2,1)} async-done(((bf16[1024,512]{1,0:T(8,128)(2,1)}), bf16[8192,512]{1,0:T(8,128)(2,1)}) %all-gather.34.cloned.1.call-update) | async-done | bytes 8388624 | tf_op jit(solution)/shard_map/all_gather | solution.py:40
  1639.1 8.4 gather_fusion.1
  1647.6 47.7 %all-gather.42.cloned.1.call-done = bf16[8192,512]{1,0:T(8,128)(2,1)} async-done(((bf16[1024,512]{1,0:T(8,128)(2,1)}), bf16[8192,512]{1,0:T(8,128)(2,1)}) %all-gather.42.cloned.1.call-update) | async-done | bytes 8388624 | tf_op jit(solution)/shard_map/all_gather | solution.py:41
  1695.3 8.4 gather_fusion.3
  (360 shorter events, 168.0 us)
Async XLA Ops:
  7.2 59.7 %all-gather.36.cloned.1.call-start = ((), (), s32[]{:S(2)}) async-start(), calls=%async_computation.23 | async-start | bytes 9437184 | tf_op jit(solution)/shard_map/all_gather | solution.py:41
  7.9 115.2 %all-gather.20.cloned.1.call-start = ((), (), s32[]{:S(2)}) async-start(), calls=%async_computation.13 | async-start | bytes 9437184 | tf_op jit(solution)/shard_map/all_gather | solution.py:40
  8.7 168.9 %all-gather.24.cloned.1.call-start = ((), (), s32[]{:S(2)}) async-start(), calls=%async_computation.15 | async-start | bytes 7077888 | tf_op jit(solution)/shard_map/all_gather | solution.py:104
  131.5 6.2 copy-start.45
  131.5 6.2 copy-start.46
  133.1 30.7 %all-to-all-start = ((bf16[4,256,512]{2,1,0:T(8,128)(2,1)}), bf16[4,256,512]{2,1,0:T(8,128)(2,1)S(1)}, u32[]{:S(2)}, u32[]{:S(2)}) async-start(bf16[4,256,512]{2,1,0:T(8,128)(2,1)} %get-tuple-element.753), calls=%async_computation | async-start | bytes 2097152 | tf_op jit(solution)/shard_map/all_to_all | solution.py:98
  137.7 115.5 %all-gather.22.cloned.1.call-start = ((), (), s32[]{:S(2)}) async-start(), calls=%async_computation.14 | async-start | bytes 5242880 | tf_op jit(solution)/shard_map/all_gather | solution.py:53
  154.9 10.2 copy-start.27
  164.4 3.5 copy-start.47
  164.4 3.6 copy-start.37
  167.1 185.7 %all-gather.26.cloned.1.call-start = ((), (), s32[]{:S(2)}) async-start(), calls=%async_computation.16 | async-start | bytes 2359296 | tf_op jit(solution)/shard_map/all_gather | solution.py:106
  167.7 266.8 %reduce-scatter.13.cloned.1.call-start = ((), (), s32[]{:S(2)}) async-start(), calls=%async_computation.17 | async-start | bytes 5242880 | tf_op jit(solution)/shard_map/reduce_scatter | solution.py:57
  168.0 9.6 copy-start.41
  303.6 10.4 copy-start.24
  340.9 10.4 copy-start.24
  359.2 132.1 %all-gather.30.cloned.1.call-start = ((), (), s32[]{:S(2)}) async-start(), calls=%async_computation.19 | async-start | bytes 9437184 | tf_op jit(solution)/shard_map/all_gather | solution.py:110
  359.9 214.3 %all-gather.28.cloned.1.call-start = ((), (), s32[]{:S(2)}) async-start(), calls=%async_computation.18 | async-start | bytes 5242880 | tf_op jit(solution)/shard_map/all_gather | solution.py:53
  437.1 7.6 copy-start.42
  439.6 190.8 %all-gather.32.cloned.1.call-start = ((), (), s32[]{:S(2)}) async-start(), calls=%async_computation.20 | async-start | bytes 9437184 | tf_op jit(solution)/shard_map/all_gather | solution.py:112
  440.4 30.6 %all-to-all-start.2 = ((bf16[4,256,512]{2,1,0:T(8,128)(2,1)}), bf16[4,256,512]{2,1,0:T(8,128)(2,1)}, u32[]{:S(2)}, u32[]{:S(2)}) async-start(bf16[4,256,512]{2,1,0:T(8,128)(2,1)} %get-tuple-element.752), calls=%async_computation.4 | async-start | bytes 2097152 | tf_op jit(solution)/shard_map/all_to_all | solution.py:99
  444.7 268.6 %all-gather.38.cloned.1.call-start = ((), (), s32[]{:S(2)}) async-start(), calls=%async_computation.24 | async-start | bytes 5242880 | tf_op jit(solution)/shard_map/all_gather | solution.py:53
  444.8 453.0 %copy-start.35 = (pred[256]{0:T(512)(128)(4,1)}, pred[256]{0:T(512)(128)(4,1)S(1)}, u32[]{:S(2)}) copy-start(pred[256]{0:T(512)(128)(4,1)S(1)} %dynamic_slice.143) | copy-start | bytes 772
  475.2 343.1 %reduce-scatter.17.cloned.1.call-start = ((), (), s32[]{:S(2)}) async-start(), calls=%async_computation.25 | async-start | bytes 5242880 | tf_op jit(solution)/shard_map/reduce_scatter | solution.py:57
  713.2 19.0 %copy-start.43 = (bf16[2048,2048]{1,0:T(8,128)(2,1)S(1)}, bf16[2048,2048]{1,0:T(8,128)(2,1)}, u32[]{:S(2)}) copy-start(bf16[2048,2048]{1,0:T(8,128)(2,1)} %all-gather.30.cloned.1.call-done) | copy-start | bytes 25165828
  742.9 154.9 %reduce-scatter.15.cloned.1.call-start = ((), (), s32[]{:S(2)}) async-start(), calls=%async_computation.21 | async-start | bytes 5242880 | tf_op jit(solution)/shard_map/reduce_scatter | solution.py:57
  756.9 230.3 %all-gather.40.cloned.1.call-start = ((), (), s32[]{:S(2)}) async-start(), calls=%async_computation.26 | async-start | bytes 5242880 | tf_op jit(solution)/shard_map/all_gather | solution.py:53
  905.8 385.2 %reduce-scatter.19.cloned.1.call-start = ((), (), s32[]{:S(2)}) async-start(), calls=%async_computation.27 | async-start | bytes 5242880 | tf_op jit(solution)/shard_map/reduce_scatter | solution.py:57
  1003.1 6.0 copy-start.1
  1003.1 3.7 copy-start.7
  1004.4 14.7 copy-start.13
  1006.9 12.2 copy-start.3
  1040.6 16.4 copy-start.2
  1075.2 4.3 copy-start
  1079.5 6.5 copy-start.5
  1079.5 6.5 copy-start.17
  1089.0 6.0 copy-start.1
  1089.1 3.7 copy-start.7
  1090.4 14.7 copy-start.13
  1092.8 12.2 copy-start.3
  1126.6 16.4 copy-start.2
  1161.1 4.4 copy-start
  1165.5 6.5 copy-start.5
  1165.5 6.5 copy-start.17
  1176.8 7.8 copy-start.8
  1193.4 135.1 %reduce-scatter.29.cloned.1.call-start = ((), (), s32[]{:S(2)}) async-start(), calls=%async_computation.33 | async-start | bytes 73728
  1194.9 204.0 %reduce-scatter.27.cloned.1.call-start = ((), (), s32[]{:S(2)}) async-start(), calls=%async_computation.32 | async-start | bytes 9437184 | tf_op jit(solution)/shard_map/reduce_scatter | solution.py:376
  1209.0 264.7 %reduce-scatter.25.cloned.1.call-start = ((), (), s32[]{:S(2)}) async-start(), calls=%async_computation.31 | async-start | bytes 9437184 | tf_op jit(solution)/shard_map/reduce_scatter | solution.py:370
  1223.4 294.6 %reduce-scatter.23.cloned.1.call-start = ((), (), s32[]{:S(2)}) async-start(), calls=%async_computation.30 | async-start | bytes 2359296 | tf_op jit(solution)/shard_map/reduce_scatter | solution.py:358
  1230.5 352.6 %reduce-scatter.21.cloned.1.call-start = ((), (), s32[]{:S(2)}) async-start(), calls=%async_computation.29 | async-start | bytes 7077888 | tf_op jit(solution)/shard_map/reduce_scatter | solution.py:352
  1230.6 5.1 copy-start.10
  1230.6 5.1 copy-start.44
  1244.0 47.1 %copy-start.12 = (f32[4,32,8,512]{3,2,0,1:T(8,128)S(1)}, f32[4,32,8,512]{3,2,0,1:T(8,128)}, u32[]{:S(2)}) copy-start(f32[4,32,8,512]{3,2,0,1:T(8,128)} %copy-done.11) | copy-start | bytes 6291460
  1244.0 47.1 %copy-start.28 = (f32[8,1,256]{2,1,0:T(1,128)S(1)}, f32[8,1,256]{2,1,0:T(1,128)}, u32[]{:S(2)}) copy-start(f32[8,1,256]{2,1,0:T(1,128)} %copy-done.27) | copy-start | bytes 24580
  1244.0 47.1 %copy-start.30 = (f32[256]{0:T(256)S(1)}, f32[256]{0:T(256)}, u32[]{:S(2)}) copy-start(f32[256]{0:T(256)} %copy-done.29) | copy-start | bytes 3076
  1244.0 47.1 %copy-start.34 = (f32[256]{0:T(256)S(1)}, f32[256]{0:T(256)}, u32[]{:S(2)}) copy-start(f32[256]{0:T(256)} %copy-done.33) | copy-start | bytes 3076
  1244.0 395.1 %all-gather.34.cloned.1.call-start = ((), (), s32[]{:S(2)}) async-start(), calls=%async_computation.22 | async-start | bytes 9437184 | tf_op jit(solution)/shard_map/all_gather | solution.py:40
  1291.0 404.4 %all-gather.42.cloned.1.call-start = ((), (), s32[]{:S(2)}) async-start(), calls=%async_computation.28 | async-start | bytes 9437184 | tf_op jit(solution)/shard_map/all_gather | solution.py:41
  1295.5 29.4 %copy-start.53 = (u32[32]{0:T(128)S(1)}, u32[32]{0:T(128)}, u32[]{:S(2)}) copy-start(u32[32]{0:T(128)} %constant.274) | copy-start | bytes 388
  1295.5 31.3 %copy-start.52 = (s32[8]{0:T(128)S(1)}, s32[8]{0:T(128)}, u32[]{:S(2)}) copy-start(s32[8]{0:T(128)} %param.37) | copy-start | bytes 100
  1295.5 31.5 %copy-start.36 = (pred[256]{0:T(512)(128)(4,1)S(1)}, pred[256]{0:T(512)(128)(4,1)}, u32[]{:S(2)}) copy-start(pred[256]{0:T(512)(128)(4,1)} %copy-done.35) | copy-start | bytes 772
  1295.5 34.4 %copy-start.22 = (bf16[256,2048]{1,0:T(8,128)(2,1)S(1)}, bf16[256,2048]{1,0:T(8,128)(2,1)}, u32[]{:S(2)}) copy-start(bf16[256,2048]{1,0:T(8,128)(2,1)} %reduce-scatter.17.cloned.1.call-done) | copy-start | bytes 3145732
  1330.1 189.7 %copy-start.21 = (bf16[256,2048]{1,0:T(8,128)(2,1)S(1)}, bf16[256,2048]{1,0:T(8,128)(2,1)}, u32[]{:S(2)}) copy-start(bf16[256,2048]{1,0:T(8,128)(2,1)} %reduce-scatter.19.cloned.1.call-done) | copy-start | bytes 3145732
  1401.6 118.4 %copy-start.31 = (bf16[2048]{0:T(1024)(128)(2,1)S(1)}, bf16[2048]{0:T(1024)(128)(2,1)}, u32[]{:S(2)}) copy-start(bf16[2048]{0:T(1024)(128)(2,1)} %get-tuple-element.660) | copy-start | bytes 12292
  1401.6 118.4 %copy-start.32 = (bf16[2048]{0:T(1024)(128)(2,1)S(1)}, bf16[2048]{0:T(1024)(128)(2,1)}, u32[]{:S(2)}) copy-start(bf16[2048]{0:T(1024)(128)(2,1)} %get-tuple-element.735) | copy-start | bytes 12292
  (28 other events, 43.8 us)
Sparse Core Ops, SparseCore 0:
  9.9 56.9 all-gather.35
  68.8 54.2 all-gather.19
  125.0 45.3 all-gather.23
  172.4 80.7 all-gather.21
  254.9 26.5 all-gather.25
  359.3 75.1 reduce-scatter.12
  436.4 54.8 all-gather.29
  493.4 80.7 all-gather.27
  576.1 54.3 all-gather.31
  632.5 80.7 all-gather.37
  743.0 75.2 reduce-scatter.16
  820.5 77.2 reduce-scatter.14
  905.9 81.2 all-gather.39
  1193.6 90.1 reduce-scatter.18
  1287.2 37.0 reduce-scatter.28
  1327.6 71.2 reduce-scatter.26
  1402.2 71.4 reduce-scatter.24
  1476.9 41.1 reduce-scatter.22
  1521.4 61.6 reduce-scatter.20
  1584.8 54.2 all-gather.33
  1641.0 54.2 all-gather.41
where the time goes:
time: 1720 us; the launch traced here: 1710 us
  waiting for transfers between devices  979 us (57%)
  matrix products  319 us (19%)
  blocking collectives  180 us (10%)
  other arithmetic  127 us (7%)
  local copies, waits for them, and re-layouts  80.4 us (5%)
    all_gather x4, waiting for transfers between devices, gather_rows(): return lax.all_gather(value, 'tensor', axis=0, tiled=True)  323 us
    reduce_scatter x4, waiting for transfers between devices, sum_rows(): lax.psum_scatter(value.astype(jnp.bfloat16), 'tensor', scatter_dimension=...  177 us
    all_gather x2, waiting for transfers between devices, bins_move(): lax.all_gather(second_rows, 'dp', axis=0, tiled=True)  104 us
    all_gather x2, waiting for transfers between devices, bins_move(): lax.all_gather(first_rows, 'dp', axis=0, tiled=True)  101 us
    reduce_scatter x1, waiting for transfers between devices, on_device(): lax.psum_scatter(up_weight_grad.astype(jnp.bfloat16), 'dp', scatter_dimen...  72.1 us
    reduce_scatter x1, waiting for transfers between devices, on_device(): lax.psum_scatter(down_weight_grad.astype(jnp.bfloat16), 'dp', scatter_dim...  68.8 us
    dot_general x4, matrix products, block_scores(): jnp.einsum('qhe,khe->hqk', query_block, key_block, preferred_element_type...  68.3 us
    all_to_all x1, blocking collectives, on_device(): lax.all_to_all(output_rows, 'tensor', split_axis=1, concat_axis=0, tiled=...  45.7 us
  transfers between devices with their start and end apart: 23, of which 19 were waited for; matrix products, arithmetic and copies ran while one was open for 15% of the time, Pallas kernels for 0%

commit v1 on v0

v1 whole, which is shorter than its diff:
```python
import jax
import jax.numpy as jnp
from jax import lax
from jax.experimental import pallas as pl
from jax.experimental.pallas import tpu as pltpu
from jax.sharding import PartitionSpec as P

H = 32
BLK = 128
MAXLEN = 1024
QB = 512
TILE = 256

norm_eps = 1e-05
masked_score = -1e30
density_scale = 0.3989422804014327
root_half = 0.7071067811865476

f32 = jnp.float32
bf16 = jnp.bfloat16


def normalize(rows):
    mean = jnp.mean(rows, axis=-1, keepdims=True)
    centred = rows - mean
    variance = jnp.mean(centred * centred, axis=-1, keepdims=True)
    scale = lax.rsqrt(variance + norm_eps)
    return (centred * scale, scale)


def norm_back(grad_norm, unit, scale, gain):
    grad_unit = grad_norm * gain
    mean_grad = jnp.mean(grad_unit, axis=-1, keepdims=True)
    mean_dot = jnp.mean(grad_unit * unit, axis=-1, keepdims=True)
    return scale * (grad_unit - mean_grad - unit * mean_dot)


def spread(table):
    return jnp.broadcast_to(table[:, None], (table.shape[0], BLK)).reshape(-1)


def swap(value, k):
    count = lax.axis_size("dp")
    return lax.ppermute(value, "dp", [(i, i ^ k) for i in range(count)])


def turn(value, r):
    count = lax.axis_size("tensor")
    return lax.ppermute(value, "tensor", [(i, (i + r) % count) for i in range(count)])


def after(values, others):
    return lax.optimization_barrier((values, others))[0]


def near_kinds():
    count = lax.axis_size("dp")
    return [0, 2, 6, 4] if count == 8 else list(range(0, count, 2))


def plane_gather(rows):
    if lax.axis_size("dp") == 8:
        half = rows.shape[1] // 2
        a = swap(rows, 2)
        b = swap(rows, 4)
        corner = [swap(a[:, :half], 4), swap(b[:, half:], 2)]
        pieces = [rows, a, jnp.concatenate(corner, axis=1), b]
    else:
        pieces = [swap(rows, k) if k else rows for k in near_kinds()]
    near = jnp.concatenate(pieces, axis=0)
    return near, swap(near, 1)


def plane_sum(near, far, weight, dim):
    count = lax.axis_size("dp")
    step = near.shape[0] * 2 // count
    other = swap(contract(far, weight, 1, dim).astype(bf16), 1)
    both = (contract(near, weight, 1, dim) + other.astype(f32)).astype(bf16)
    if count == 8:
        half = both.shape[1] // 2
        a = swap(both[step : 3 * step, :half], 2)
        b = swap(both[2 * step :, half:], 4)
        c = both[3 * step :, :half].astype(f32) + a[step:].astype(f32)
        d = both[step : 2 * step, half:].astype(f32) + b[:step].astype(f32)
        c = swap(c.astype(bf16), 4)
        d = swap(d.astype(bf16), 2)
        left = both[:step, :half].astype(f32) + a[:step].astype(f32) + c.astype(f32)
        right = both[:step, half:].astype(f32) + b[step:].astype(f32) + d.astype(f32)
        return jnp.concatenate([left, right], axis=1)
    total = both[:step].astype(f32)
    for j, k in enumerate(near_kinds()):
        if k:
            total = total + swap(both[j * step : (j + 1) * step], k).astype(f32)
    return total


def small_gather(value):
    count = lax.axis_size("dp")
    value = value.reshape(1, -1)
    k = 1
    while k < count:
        value = jnp.concatenate([value, swap(value, k)], axis=0)
        k *= 2
    return jnp.take(value, jnp.arange(count, dtype=jnp.int32) ^ lax.axis_index("dp"), axis=0)


def pick_blocks(near, far, owner, local, blocks):
    rank = lax.axis_index("dp")
    near = near.reshape(-1, BLK, near.shape[-1])
    far = far.reshape(-1, BLK, far.shape[-1])
    kinds = near_kinds()
    piece = jnp.array([kinds.index(2 * j) for j in range(len(kinds))], jnp.int32)
    k = owner ^ rank
    at = piece[k // 2] * blocks + local
    picked = []
    for i in range(owner.shape[0]):
        a = lax.dynamic_index_in_dim(near, at[i], 0, keepdims=True)
        b = lax.dynamic_index_in_dim(far, at[i], 0, keepdims=True)
        picked.append(jnp.where(k[i] % 2 == 0, a, b))
    return jnp.concatenate(picked, axis=0)


def to_bins(blocks, here):
    count = lax.axis_size("tensor")
    z = lax.axis_index("tensor")
    wide = blocks.shape[-1]
    out = jnp.zeros((here, BLK, wide * count), blocks.dtype)
    for r in range(count):
        piece = lax.dynamic_slice_in_dim(blocks, ((z + r) % count) * here, here, 0)
        if r:
            piece = turn(piece, r)
        out = lax.dynamic_update_slice(out, piece, (0, 0, ((z - r) % count) * wide))
    return out


def from_bins(rows):
    count = lax.axis_size("tensor")
    z = lax.axis_index("tensor")
    here = rows.shape[0]
    wide = rows.shape[-1] // count
    out = jnp.zeros((here * count, BLK, wide), rows.dtype)
    for r in range(count):
        piece = lax.dynamic_slice_in_dim(rows, ((z + r) % count) * wide, wide, 2)
        if r:
            piece = turn(piece, r)
        out = lax.dynamic_update_slice(out, piece, (((z - r) % count) * here, 0, 0))
    return out


def contract(a, b, left, right):
    return lax.dot_general(a, b, (((left,), (right,)), ((), ())), preferred_element_type=f32)


def attend_kernel(heads, head_size, where, slopes, near, far, out_near, out_far, qkv, mixed):
    width = heads * head_size
    blocks = near.shape[0] // BLK
    for j in range(2 * blocks):
        source, i = (near, j) if j < blocks else (far, j - blocks)
        at = pl.multiple_of(where[j] * BLK, BLK)
        for part in range(3):
            for h in range(heads):
                lo = part * width + h * head_size
                piece = source[i * BLK : (i + 1) * BLK, lo : lo + head_size]
                if part == 0:
                    piece = (piece.astype(f32) * 0.125).astype(bf16)
                qkv[part, h, pl.ds(at, BLK), :] = piece
    slots = 2 * blocks * BLK

    def one_head(h, carry):
        slope = slopes[h]
        for t in range(slots // TILE):
            lo, hi = t * TILE, (t + 1) * TILE
            query = qkv[0, h, lo:hi, :]
            scores = contract(query, qkv[1, h, 0:hi, :], 1, 1)
            column = lax.broadcasted_iota(jnp.int32, (1, hi), 1)
            scores = scores + slope * (column - hi).astype(f32)
            diagonal = scores[:, lo:hi]
            rows = lax.broadcasted_iota(jnp.int32, (TILE, TILE), 0)
            columns = lax.broadcasted_iota(jnp.int32, (TILE, TILE), 1)
            diagonal = jnp.where(columns <= rows, diagonal, masked_score)
            scores = jnp.concatenate([scores[:, :lo], diagonal], axis=1) if t else diagonal
            top = jnp.max(scores, axis=1, keepdims=True)
            weights = jnp.exp(scores - top)
            total = jnp.sum(weights, axis=1, keepdims=True)
            result = contract(weights.astype(bf16), qkv[2, h, 0:hi, :], 1, 0) / total
            mixed[h, lo:hi, :] = result.astype(bf16)
        return carry

    lax.fori_loop(0, heads, one_head, 0)
    for j in range(2 * blocks):
        target, i = (out_near, j) if j < blocks else (out_far, j - blocks)
        at = pl.multiple_of(where[j] * BLK, BLK)
        for h in range(heads):
            target[i * BLK : (i + 1) * BLK, h * head_size : (h + 1) * head_size] = mixed[
                h, pl.ds(at, BLK), :
            ]


def attend_back_kernel(
    heads, head_size, where, slopes, near, far, grad_near, grad_far, out_near, out_far, qkvg, sums, parts
):
    width = heads * head_size
    blocks = near.shape[0] // BLK
    for j in range(2 * blocks):
        source, grad, i = (near, grad_near, j) if j < blocks else (far, grad_far, j - blocks)
        at = pl.multiple_of(where[j] * BLK, BLK)
        for part in range(4):
            for h in range(heads):
                lo = part * width + h * head_size
                if part < 3:
                    piece = source[i * BLK : (i + 1) * BLK, lo : lo + head_size]
                else:
                    piece = grad[i * BLK : (i + 1) * BLK, h * head_size : (h + 1) * head_size]
                if part == 0:
                    piece = (piece.astype(f32) * 0.125).astype(bf16)
                qkvg[part, h, pl.ds(at, BLK), :] = piece
    slots = 2 * blocks * BLK

    def one_head(h, carry):
        slope = slopes[h]
        sums[...] = jnp.zeros_like(sums)
        for t in range(slots // TILE):
            lo, hi = t * TILE, (t + 1) * TILE
            query = qkvg[0, h, lo:hi, :]
            grad = qkvg[3, h, lo:hi, :]
            keys = qkvg[1, h, 0:hi, :]
            scores = contract(keys, query, 1, 1)
            key_place = lax.broadcasted_iota(jnp.int32, (hi, 1), 0)
            scores = scores + slope * (key_place - hi).astype(f32)
            diagonal = scores[lo:hi, :]
            rows = lax.broadcasted_iota(jnp.int32, (TILE, TILE), 0)
            columns = lax.broadcasted_iota(jnp.int32, (TILE, TILE), 1)
            diagonal = jnp.where(rows <= columns, diagonal, masked_score)
            scores = jnp.concatenate([scores[:lo, :], diagonal], axis=0) if t else diagonal
            top = jnp.max(scores, axis=0, keepdims=True)
            weights = jnp.exp(scores - top)
            total = jnp.sum(weights, axis=0, keepdims=True)
            probs = weights * (1.0 / total)
            grad_probs = contract(qkvg[2, h, 0:hi, :], grad, 1, 1)
            inner = jnp.sum(probs * grad_probs, axis=0, keepdims=True)
            grad_scores = (probs * (grad_probs - inner)).astype(bf16)
            sums[0, 0:hi, :] += contract(grad_scores, query, 1, 0)
            sums[1, 0:hi, :] += contract(probs.astype(bf16), grad, 1, 0)
            grad_query = contract(grad_scores, keys, 0, 0) * 0.125
            parts[0, h, lo:hi, :] = grad_query.astype(bf16)
        parts[1, h] = sums[0].astype(bf16)
        parts[2, h] = sums[1].astype(bf16)
        return carry

    lax.fori_loop(0, heads, one_head, 0)
    for j in range(2 * blocks):
        target, i = (out_near, j) if j < blocks else (out_far, j - blocks)
        at = pl.multiple_of(where[j] * BLK, BLK)
        for part in range(3):
            for h in range(heads):
                lo = part * width + h * head_size
                target[i * BLK : (i + 1) * BLK, lo : lo + head_size] = parts[part, h, pl.ds(at, BLK), :]


def smem():
    return pl.BlockSpec(memory_space=pltpu.SMEM)


def vmem():
    return pl.BlockSpec(memory_space=pltpu.VMEM)


def attend_one(near, far, where, slopes, heads, head_size):
    slots = 2 * near.shape[0]
    width = heads * head_size
    half = jax.ShapeDtypeStruct((near.shape[0], width), bf16)

    def body(*refs):
        attend_kernel(heads, head_size, *refs)

    return pl.pallas_call(
        body,
        out_shape=(half, half),
        in_specs=[smem(), smem(), vmem(), vmem()],
        out_specs=(vmem(), vmem()),
        scratch_shapes=[
            pltpu.VMEM((3, heads, slots, head_size), bf16),
            pltpu.VMEM((heads, slots, head_size), bf16),
        ],
        cost_estimate=pl.CostEstimate(
            flops=2 * slots * slots * width, transcendentals=slots * slots * heads // 2, bytes_accessed=8 * slots * width
        ),
        name="attend",
    )(where, slopes, near, far)


def attend_one_back(near, far, grad_near, grad_far, where, slopes, heads, head_size):
    slots = 2 * near.shape[0]
    half = jax.ShapeDtypeStruct(near.shape, bf16)

    def body(*refs):
        attend_back_kernel(heads, head_size, *refs)

    return pl.pallas_call(
        body,
        out_shape=(half, half),
        in_specs=[smem(), smem(), vmem(), vmem(), vmem(), vmem()],
        out_specs=(vmem(), vmem()),
        scratch_shapes=[
            pltpu.VMEM((4, heads, slots, head_size), bf16),
            pltpu.VMEM((2, slots, head_size), f32),
            pltpu.VMEM((3, heads, slots, head_size), bf16),
        ],
        cost_estimate=pl.CostEstimate(
            flops=5 * slots * slots * heads * head_size,
            transcendentals=slots * slots * heads // 2,
            bytes_accessed=16 * slots * heads * head_size,
        ),
        name="attend_back",
    )(where, slopes, near, far, grad_near, grad_far)


def reorder(near, far, order):
    pieces = jnp.concatenate([near, far], axis=0).reshape(-1, BLK, near.shape[-1])
    return jnp.take(pieces, order, axis=0).reshape(-1, near.shape[-1])


def block_view(query, keys, values, segment, place, valid, slopes, heads, head_size):
    width = heads * head_size
    keys_pad = jnp.concatenate([jnp.zeros((MAXLEN, width), bf16), keys])
    values_pad = jnp.concatenate([jnp.zeros((MAXLEN, width), bf16), values])
    segment_pad = jnp.concatenate([jnp.full((MAXLEN,), -1, jnp.int32), segment])
    place_pad = jnp.concatenate([jnp.zeros((MAXLEN,), jnp.int32), place])
    valid_pad = jnp.concatenate([jnp.zeros((MAXLEN,), dtype=bool), valid])
    window = QB + MAXLEN

    def block_scores(begin):
        query_block = lax.dynamic_slice_in_dim(query, begin, QB).reshape(QB, heads, head_size)
        key_block = lax.dynamic_slice_in_dim(keys_pad, begin, window).reshape(window, heads, head_size)
        value_block = lax.dynamic_slice_in_dim(values_pad, begin, window).reshape(window, heads, head_size)
        query_segment = lax.dynamic_slice_in_dim(segment, begin, QB)
        query_place = lax.dynamic_slice_in_dim(place, begin, QB)
        key_segment = lax.dynamic_slice_in_dim(segment_pad, begin, window)
        key_place = lax.dynamic_slice_in_dim(place_pad, begin, window)
        key_valid = lax.dynamic_slice_in_dim(valid_pad, begin, window)
        raw = jnp.einsum("qhe,khe->hqk", query_block, key_block, preferred_element_type=f32) * 0.125
        distance = (query_place[:, None] - key_place[None, :]).astype(f32)
        raw = raw - slopes[:, None, None] * distance[None]
        allowed = (
            (query_segment[:, None] == key_segment[None, :])
            & (key_place[None, :] <= query_place[:, None])
            & key_valid[None, :]
        )
        return (jnp.where(allowed[None], raw, masked_score), query_block, key_block, value_block)

    return block_scores, window


def attend_any(query, keys, values, segment, place, valid, slopes, heads, head_size):
    slots, width = query.shape
    block_scores, _ = block_view(query, keys, values, segment, place, valid, slopes, heads, head_size)

    def forward_block(index, attended):
        begin = index * QB
        scores, _, _, value_block = block_scores(begin)
        weights = jax.nn.softmax(scores, axis=-1).astype(bf16)
        mixed = jnp.einsum("hqk,khe->qhe", weights, value_block, preferred_element_type=f32)
        return lax.dynamic_update_slice_in_dim(attended, mixed.reshape(QB, width).astype(bf16), begin, 0)

    return lax.fori_loop(0, slots // QB, forward_block, jnp.zeros((slots, width), bf16))


def attend_any_back(query, keys, values, grad, segment, place, valid, slopes, heads, head_size):
    slots, width = query.shape
    block_scores, window = block_view(query, keys, values, segment, place, valid, slopes, heads, head_size)

    def backward_block(index, carry):
        grad_query, grad_keys, grad_values = carry
        begin = index * QB
        scores, query_block, key_block, value_block = block_scores(begin)
        probs = jax.nn.softmax(scores, axis=-1)
        grad_block = lax.dynamic_slice_in_dim(grad, begin, QB).reshape(QB, heads, head_size)
        grad_probs = jnp.einsum("qhe,khe->hqk", grad_block, value_block, preferred_element_type=f32)
        inner = jnp.sum(probs * grad_probs, axis=-1, keepdims=True)
        grad_scores = (probs * (grad_probs - inner)).astype(bf16)
        query_part = jnp.einsum("hqk,khe->qhe", grad_scores, key_block, preferred_element_type=f32) * 0.125
        key_part = jnp.einsum("hqk,qhe->khe", grad_scores, query_block, preferred_element_type=f32) * 0.125
        value_part = jnp.einsum("hqk,qhe->khe", probs.astype(bf16), grad_block, preferred_element_type=f32)
        grad_query = lax.dynamic_update_slice_in_dim(grad_query, query_part.reshape(QB, width), begin, 0)
        old_keys = lax.dynamic_slice_in_dim(grad_keys, begin, window)
        grad_keys = lax.dynamic_update_slice_in_dim(
            grad_keys, old_keys + key_part.reshape(window, width), begin, 0
        )
        old_values = lax.dynamic_slice_in_dim(grad_values, begin, window)
        grad_values = lax.dynamic_update_slice_in_dim(
            grad_values, old_values + value_part.reshape(window, width), begin, 0
        )
        return (grad_query, grad_keys, grad_values)

    padded_zero = jnp.zeros((MAXLEN + slots, width), f32)
    grad_query, grad_keys, grad_values = lax.fori_loop(
        0, slots // QB, backward_block, (jnp.zeros((slots, width), f32), padded_zero, padded_zero)
    )
    return jnp.concatenate([grad_query, grad_keys[MAXLEN:], grad_values[MAXLEN:]], axis=1).astype(bf16)


def on_device(
    tokens,
    cotangent,
    first_gain,
    first_shift,
    attention_in,
    attention_bias,
    attention_out,
    out_bias,
    second_gain,
    second_shift,
    up_weight,
    up_bias,
    down_weight,
    down_bias,
    source_block,
    target_block,
    block_fill,
    block_start,
):
    n = lax.axis_size("dp")
    nz = lax.axis_size("tensor")
    p = lax.axis_index("dp")
    z = lax.axis_index("tensor")
    bin_slots, columns = tokens.shape
    blocks = bin_slots // BLK
    assert blocks == n and n % nz == 0 and n % 2 == 0
    here = n // nz
    shard = first_gain.shape[0]
    d = shard * n
    head_size = attention_bias.shape[2] * n
    heads_z = attention_bias.shape[1]
    heads = H // n
    width = heads * head_size
    units_z = up_weight.shape[1]
    units = units_z // n
    even_heads = heads_z % n == 0

    small = [first_gain, first_shift, out_bias, second_gain, second_shift, down_bias]
    small = small + [attention_bias.reshape(-1), up_bias.reshape(-1)]
    small = small + [t.astype(bf16) for t in (source_block, target_block, block_fill, block_start)]
    packed = small_gather(jnp.concatenate(small))
    at = 6 * shard
    vectors = packed[:, :at].reshape(n, 6, shard).transpose(1, 0, 2).reshape(6, 1, d).astype(f32)
    gain_one, shift_one, out_shift, gain_two, shift_two, down_shift = [vectors[i] for i in range(6)]
    size = attention_bias.size
    bias_z = packed[:, at : at + size].reshape(n, 2, heads_z, head_size // n)
    bias_z = bias_z.transpose(1, 2, 0, 3).reshape(2, heads_z * head_size)
    at = at + size
    size = up_bias.size
    up_z = packed[:, at : at + size].reshape(n, up_bias.shape[0], up_bias.shape[1])
    up_z = up_z.transpose(1, 0, 2).reshape(n, units)
    tables = packed[:, at + size :].reshape(n, 4, blocks).transpose(1, 0, 2).astype(jnp.int32)
    source, target, fill, start = [tables[i] for i in range(4)]
    if even_heads:
        bias_z = lax.dynamic_slice_in_dim(bias_z, p * (width // nz), width // nz, 1)
        head_ids = jnp.arange(nz, dtype=jnp.int32)[:, None] * heads_z + p * (heads_z // n)
        head_ids = (head_ids + jnp.arange(heads_z // n, dtype=jnp.int32)[None, :]).reshape(-1)
    else:
        head_ids = p * heads + jnp.arange(heads, dtype=jnp.int32)
    up_z = lax.dynamic_index_in_dim(up_z, p, 0, keepdims=False)
    bias_size = bias_z.size
    both_z = jnp.concatenate([bias_z.reshape(-1), up_z])
    every = jnp.zeros((nz, both_z.shape[0]), bf16)
    for r in range(nz):
        piece = turn(both_z, r) if r else both_z
        every = lax.dynamic_update_slice(every, piece[None], ((z - r) % nz, 0))
    mine = every[:, :bias_size].reshape(nz, 2, -1).transpose(1, 0, 2).reshape(2, -1)
    if not even_heads:
        mine = lax.dynamic_slice_in_dim(mine, p * width, width, 1)
    qkv_bias = jnp.concatenate([mine[0], jnp.zeros((width,), bf16), mine[1]]).astype(f32)[None]
    up_shift = every[:, bias_size:].reshape(1, nz * units).astype(f32)
    slopes = jnp.exp2(-8.0 * (head_ids + 1).astype(f32) / H)

    def spread_out(value, split, join):
        return lax.all_to_all(value, "dp", split_axis=split, concat_axis=join, tiled=True)

    def over_bins(value, axis):
        return lax.all_gather(value, "tensor", axis=axis, tiled=True)

    wanted = lax.dynamic_index_in_dim(source, p, 1, keepdims=False)
    near, far = plane_gather(tokens)
    out_weight, up_weight, down_weight, cotangent = after(
        (attention_out, up_weight, down_weight, cotangent), (near, far)
    )
    rows_in = to_bins(pick_blocks(near, far, wanted // blocks, wanted % blocks, blocks), here)
    near, far = plane_gather(after(cotangent, rows_in))
    grad_in = to_bins(pick_blocks(near, far, wanted // blocks, wanted % blocks, blocks), here)

    if even_heads:
        in_rows = over_bins(spread_out(attention_in.transpose(0, 2, 1), 1, 2), 1)
        out_rows = over_bins(spread_out(out_weight, 0, 1), 0)
    else:
        in_rows = spread_out(over_bins(attention_in, 2).transpose(0, 2, 1), 1, 2)
        out_rows = spread_out(over_bins(out_weight, 0), 0, 1)
    in_rows = in_rows.reshape(3 * width, d)
    up_part = over_bins(spread_out(up_weight, 1, 0), 1)
    down_part = over_bins(spread_out(down_weight, 0, 1), 0)

    first_bin = z * here
    kinds = near_kinds() + [k + 1 for k in near_kinds()]
    where = jnp.array(kinds, jnp.int32) ^ p
    single = bin_slots == MAXLEN
    offset = jnp.arange(bin_slots, dtype=jnp.int32) % BLK
    block_of = jnp.arange(bin_slots, dtype=jnp.int32) // BLK

    def bin_tables(g):
        bin_start = lax.dynamic_index_in_dim(start, first_bin + g, 0, keepdims=False)
        bin_fill = lax.dynamic_index_in_dim(fill, first_bin + g, 0, keepdims=False)
        segment = spread(bin_start)
        valid = offset < spread(bin_fill)
        place = (block_of - segment) * BLK + offset
        valid_rows = jnp.arange(BLK, dtype=jnp.int32) < lax.dynamic_index_in_dim(bin_fill, p, 0)
        return segment, place, valid, valid_rows[:, None]

    inverse = [kinds.index(k) for k in range(n)]
    order = jnp.array(inverse, jnp.int32)[jnp.arange(n, dtype=jnp.int32) ^ p]

    def split_rows(rows):
        back = jnp.take(rows.reshape(n, BLK, -1), where, axis=0).reshape(rows.shape)
        return back[: bin_slots // 2], back[bin_slots // 2 :]

    def attend(near, far, g):
        if single:
            return attend_one(near, far, where, slopes, heads, head_size)
        segment, place, valid, _ = bin_tables(g)
        rows = reorder(near, far, order)
        query, keys, values = rows[:, :width], rows[:, width : 2 * width], rows[:, 2 * width :]
        return split_rows(
            attend_any(query, keys, values, segment, place, valid, slopes, heads, head_size)
        )

    def attend_back(near, far, grad_near, grad_far, g):
        if single:
            return attend_one_back(near, far, grad_near, grad_far, where, slopes, heads, head_size)
        segment, place, valid, _ = bin_tables(g)
        rows = reorder(near, far, order)
        grad = reorder(grad_near, grad_far, order)
        query, keys, values = rows[:, :width], rows[:, width : 2 * width], rows[:, 2 * width :]
        return split_rows(
            attend_any_back(query, keys, values, grad, segment, place, valid, slopes, heads, head_size)
        )

    streams = []
    for g in range(here):
        s = {}
        s["valid"] = bin_tables(g)[3]
        s["x"] = rows_in[g].astype(f32)
        s["grad"] = jnp.where(s["valid"], grad_in[g].astype(f32), 0.0)
        s["unit_one"], s["scale_one"] = normalize(s["x"])
        norm_one = (s["unit_one"] * gain_one + shift_one).astype(bf16)
        s["one"] = plane_gather(norm_one)
        s["qkv"] = [(contract(v, in_rows, 1, 1) + qkv_bias).astype(bf16) for v in s["one"]]
        s["att"] = attend(*s["qkv"], g)
        resid = s["x"] + plane_sum(*s["att"], out_rows, 0) + out_shift
        s["unit_two"], s["scale_two"] = normalize(resid)
        norm_two = (s["unit_two"] * gain_two + shift_two).astype(bf16)
        s["two"] = plane_gather(norm_two)
        s["hidden"], s["slope"] = [], []
        for v in s["two"]:
            before = jnp.dot(v, up_part, preferred_element_type=f32) + up_shift
            share = 0.5 * (1.0 + lax.erf(before * root_half))
            s["hidden"].append((before * share).astype(bf16))
            density = jnp.exp(-0.5 * before * before) * density_scale
            s["slope"].append((share + before * density).astype(bf16))
        s["resid"] = resid
        s["branch"] = plane_gather(s["grad"].astype(bf16))
        streams.append(s)

    def pairs_sum(left, right):
        a = jnp.concatenate([v for s in streams for v in s[left]], axis=0)
        b = jnp.concatenate([v for s in streams for v in s[right]], axis=0)
        return contract(a, b, 0, 0)

    down_grad = pairs_sum("hidden", "branch").astype(bf16)
    branches = after([s["branch"] for s in streams], down_grad)
    down_grad = lax.psum_scatter(down_grad, "tensor", scatter_dimension=0, tiled=True)
    down_grad = spread_out(down_grad, 1, 0).astype(f32)
    for s, branch in zip(streams, branches):
        s["before"] = [
            (contract(v, down_part, 1, 1) * slope.astype(f32)).astype(bf16)
            for v, slope in zip(branch, s["slope"])
        ]
    up_grad = pairs_sum("two", "before").astype(bf16)
    up_grad = lax.psum_scatter(up_grad, "tensor", scatter_dimension=1, tiled=True)
    up_grad = spread_out(up_grad, 0, 1).astype(f32)
    up_bias_grad = sum(jnp.sum(v.astype(f32), axis=0) for s in streams for v in s["before"])
    for g, s in enumerate(streams):
        grad_two = plane_sum(*s["before"], up_part, 1)
        s["gain_two"] = jnp.sum(grad_two * s["unit_two"], axis=0)
        s["shift_two"] = jnp.sum(grad_two, axis=0)
        s["grad_resid"] = s["grad"] + norm_back(grad_two, s["unit_two"], s["scale_two"], gain_two)
        s["attn"] = plane_gather(s["grad_resid"].astype(bf16))
        grad_att = [contract(v, out_rows, 1, 1).astype(bf16) for v in s["attn"]]
        s["grad_qkv"] = attend_back(*s["qkv"], *grad_att, g)
    results = []
    for s in streams:
        result = s["resid"] + plane_sum(*s["hidden"], down_part, 0) + down_shift
        results.append(jnp.where(s["valid"], result, 0.0).astype(bf16))
    output = from_bins(jnp.stack(results))
    out_grad = pairs_sum("att", "attn").astype(bf16)
    if even_heads:
        out_grad = lax.psum_scatter(out_grad, "tensor", scatter_dimension=0, tiled=True)
        out_grad = spread_out(out_grad, 1, 0).astype(f32)
    else:
        out_grad = spread_out(out_grad, 1, 0)
        out_grad = lax.psum_scatter(out_grad, "tensor", scatter_dimension=0, tiled=True).astype(f32)
    in_grad = pairs_sum("grad_qkv", "one").astype(bf16).reshape(3, width, d)
    if even_heads:
        in_grad = in_grad.reshape(3, nz, width // nz, d).transpose(1, 0, 2, 3).reshape(-1, d)
        in_grad = lax.psum_scatter(in_grad, "tensor", scatter_dimension=0, tiled=True)
        in_grad = spread_out(in_grad.reshape(3, width // nz, d), 2, 1)
    else:
        in_grad = spread_out(in_grad, 2, 1)
        in_grad = lax.psum_scatter(in_grad, "tensor", scatter_dimension=1, tiled=True)
    in_grad = in_grad.transpose(0, 2, 1).astype(f32)
    bias_grad = sum(jnp.sum(v.astype(f32), axis=0) for s in streams for v in s["grad_qkv"])
    bias_grad = jnp.stack([bias_grad[:width], bias_grad[2 * width :]])

    input_rows = []
    for s in streams:
        grad_one = plane_sum(*s["grad_qkv"], in_rows, 0)
        s["gain_one"] = jnp.sum(grad_one * s["unit_one"], axis=0)
        s["shift_one"] = jnp.sum(grad_one, axis=0)
        grad_x = s["grad_resid"] + norm_back(grad_one, s["unit_one"], s["scale_one"], gain_one)
        input_rows.append(grad_x.astype(bf16))
    input_grad = from_bins(jnp.stack(input_rows))

    wanted = lax.dynamic_index_in_dim(target, p, 0, keepdims=False)

    def to_anchor(blocks_here):
        near, far = plane_gather(blocks_here.reshape(n * BLK, columns))
        return pick_blocks(near, far, wanted % blocks, wanted // blocks, n).reshape(bin_slots, columns)

    output = to_anchor(output)
    input_grad = to_anchor(input_grad)

    def over_streams(name):
        return sum(s[name] for s in streams)

    vectors = jnp.stack(
        [
            over_streams("gain_one"),
            over_streams("shift_one"),
            sum(jnp.sum(s["grad_resid"], axis=0) for s in streams),
            over_streams("gain_two"),
            over_streams("shift_two"),
            sum(jnp.sum(s["grad"], axis=0) for s in streams),
        ]
    ).reshape(6, n, shard).transpose(1, 0, 2).reshape(n, -1)
    if even_heads:
        bias_full = jnp.zeros((2, nz, n, width // nz), f32)
        bias_full = lax.dynamic_update_slice(
            bias_full, bias_grad.reshape(2, nz, 1, width // nz), (0, 0, p, 0)
        )
    else:
        bias_full = jnp.zeros((2, n, width), f32)
        bias_full = lax.dynamic_update_slice(bias_full, bias_grad.reshape(2, 1, width), (0, p, 0))
    bias_full = bias_full.reshape(2, nz, heads_z * n, head_size // n)
    up_full = jnp.zeros((nz, n, units), f32)
    up_full = lax.dynamic_update_slice(up_full, up_bias_grad.reshape(nz, 1, units), (0, p, 0))
    rows_z = up_bias.shape[0]
    bias_full = bias_full.reshape(2, nz, heads_z, n, head_size // n).transpose(1, 3, 0, 2, 4)
    up_full = up_full.reshape(nz, rows_z, n, up_bias.shape[1]).transpose(0, 2, 1, 3)
    by_slice = jnp.concatenate([bias_full.reshape(nz, n, -1), up_full.reshape(nz, n, -1)], axis=2)

    def for_slice(r):
        return jnp.concatenate(
            [vectors, lax.dynamic_index_in_dim(by_slice, (z + r) % nz, 0, keepdims=False)], axis=1
        )

    table = for_slice(0)
    for r in range(1, nz):
        table = table + turn(for_slice(r), r)
    mine = lax.dynamic_index_in_dim(table, p, 0, keepdims=False)
    for k in range(1, n):
        mine = mine + swap(lax.dynamic_index_in_dim(table, p ^ k, 0, keepdims=False), k)
    vectors = mine[: 6 * shard].reshape(6, shard)
    at = 6 * shard + attention_bias.size
    bias_grad = mine[6 * shard : at].reshape(attention_bias.shape)
    up_bias_grad = mine[at:].reshape(up_bias.shape)
    return (
        output,
        input_grad,
        vectors[0],
        vectors[1],
        in_grad,
        bias_grad,
        out_grad,
        vectors[2],
        vectors[3],
        vectors[4],
        up_grad,
        up_bias_grad,
        down_grad,
        vectors[5],
    )


def solution(mesh):
    return jax.shard_map(
        on_device,
        mesh=mesh,
        in_specs=(
            P("dp", "tensor"),
            P("dp", "tensor"),
            P("dp"),
            P("dp"),
            P(None, "dp", "tensor"),
            P(None, "tensor", "dp"),
            P("tensor", "dp"),
            P("dp"),
            P("dp"),
            P("dp"),
            P("dp", "tensor"),
            P("tensor", "dp"),
            P("tensor", "dp"),
            P("dp"),
            P("dp"),
            P("dp"),
            P("dp"),
            P("dp"),
        ),
        out_specs=(
            P("dp", "tensor"),
            P("dp", "tensor"),
            P("dp"),
            P("dp"),
            P(None, "dp", "tensor"),
            P(None, "tensor", "dp"),
            P("tensor", "dp"),
            P("dp"),
            P("dp"),
            P("dp"),
            P("dp", "tensor"),
            P("tensor", "dp"),
            P("tensor", "dp"),
            P("dp"),
        ),
        check_vma=False,
    )
```

time: 1720 us -> 1130 us (0.66)
  waiting for transfers between devices: 979 us -> 346 us
  starting transfers between devices: 9.68 us -> 211 us
  blocking collectives: 180 us -> 0 us
  matrix products: 319 us -> 149 us
  between operations: 16.9 us -> 79.9 us
  Pallas kernels: 0 us -> 58.5 us
  local copies, waits for them, and re-layouts: 80.4 us -> 123 us
    all_gather x12 -> x4, waiting for transfers between devices: 560 us -> 0.03 us  [over_bins(): return lax.all_gather(value, 'tensor', axis=axis, tiled=True)]
    reduce_scatter x8 -> x4, waiting for transfers between devices: 379 us -> 0.04 us  [the longest x1 0.02 us: on_device(): lax.psum_scatter(down_grad, 'tensor', scatter_dimension=0, tiled=True)]
    ppermute x0 -> x128, waiting for transfers between devices: none -> 328 us  [the longest x110 243 us: swap(): return lax.ppermute(value, 'dp', [(i, i ^ k) for i in range(count)])]
    ppermute x0 -> x128, starting transfers between devices: none -> 181 us  [the longest x110 106 us: swap(): return lax.ppermute(value, 'dp', [(i, i ^ k) for i in range(count)])]
    dot_general x32 -> x36, matrix products: 319 us -> 149 us  [the longest x32 133 us: contract(): lax.dot_general(a, b, (((left,), (right,)), ((), ())), preferred_element_...]
    all_to_all x2 -> x0, blocking collectives: 74.9 us -> none  [the longest x1 45.7 us: on_device(): lax.all_to_all(output_rows, 'tensor', split_axis=1, concat_axis=0, tiled=...]
    all_gather x8 -> x0, blocking collectives: 70.2 us -> none  [the longest x1 9.21 us: on_device(): lax.all_gather(up_bias, 'dp', axis=1, tiled=True)]
    concatenate x0 -> x25, other arithmetic: none -> 68.6 us  [the longest x12 59.1 us: plane_gather(): near = jnp.concatenate(pieces, axis=0)]
  transfers between devices with their start and end apart: 23 -> 144, of which waited for: 19 -> 58; matrix products, arithmetic and copies ran while one was open for 15% -> 34% of each run, Pallas kernels for 0% -> 5%
where the time goes in v1:
time: 1130 us; the launch traced here: 1110 us
  waiting for transfers between devices  346 us (31%)
  starting transfers between devices  211 us (19%)
  matrix products  149 us (13%)
  other arithmetic  144 us (13%)
  local copies, waits for them, and re-layouts  123 us (11%)
  between operations  79.9 us (7%)
  Pallas kernels  58.5 us (5%)
    ppermute x110, waiting for transfers between devices, swap(): return lax.ppermute(value, 'dp', [(i, i ^ k) for i in range(count)])  243 us
    dot_general x32, matrix products, contract(): lax.dot_general(a, b, (((left,), (right,)), ((), ())), preferred_element_...  133 us
    ppermute x110, starting transfers between devices, swap(): return lax.ppermute(value, 'dp', [(i, i ^ k) for i in range(count)])  106 us
    ppermute x18, waiting for transfers between devices, turn(): lax.ppermute(value, 'tensor', [(i, (i + r) % count) for i in range(count)])  85.7 us
    ppermute x18, starting transfers between devices, turn(): lax.ppermute(value, 'tensor', [(i, (i + r) % count) for i in range(count)])  75.7 us
    concatenate x12, other arithmetic, plane_gather(): near = jnp.concatenate(pieces, axis=0)  59.1 us
    unnamed x385, local copies, waits for them, and re-layouts  56.6 us
    unnamed x40, other arithmetic  39.4 us
  transfers between devices with their start and end apart: 144, of which 58 were waited for; matrix products, arithmetic and copies ran while one was open for 34% of the time, Pallas kernels for 5%

profile of v1, /device:TPU:0, one launch (start us, length us, event | category | flops | bytes accessed | tf_op | source)
XLA Modules:
  0.0 1111.5 jit_solution(10090353320917886272)
XLA Ops:
  11.7 21.9 %collective-permute-done.3 = bf16[1024,512]{1,0:T(8,128)(2,1)S(1)} collective-permute-done((bf16[1024,512]{1,0:T(8,128)(2,1)}, bf16[1024,512]{1,0:T(8,128)(2,1)S(1)}, u32[]{:S(2)}, u32[]{:S(2)}) %collective-permute-start.3) | collective-permute-done | bytes 1048608 | tf_op jit(solution)/shard_map/ppermute | solution.py:44
  37.2 9.6 collective-permute-done.4
  60.9 11.4 %collective-permute-done.1 = bf16[2,1952]{1,0:T(2,128)(2,1)S(1)} collective-permute-done((bf16[2,1952]{1,0:T(2,128)(2,1)S(1)}, bf16[2,1952]{1,0:T(2,128)(2,1)S(1)}, u32[]{:S(2)}, u32[]{:S(2)}) %collective-permute-start.1) | collective-permute-done | bytes 7840 | tf_op jit(solution)/shard_map/ppermute | solution.py:44
  127.2 10.5 collective-permute-done.8
  137.7 18.6 %collective-permute-done.9 = bf16[2,128,512]{2,1,0:T(8,128)(2,1)S(1)} collective-permute-done((bf16[2,128,512]{2,1,0:T(8,128)(2,1)S(1)}, bf16[2,128,512]{2,1,0:T(8,128)(2,1)S(1)}, u32[]{:S(2)}, u32[]{:S(2)}) %collective-permute-start.9) | collective-permute-done | bytes 262176 | tf_op jit(solution)/shard_map/ppermute | solution.py:49
  165.6 6.2 collective-permute-done.11
  176.3 9.5 collective-permute-start.15
  193.8 5.2 pad_maximum_fusion.4
  203.1 9.3 collective-permute-done.62
  218.1 5.0 add_convert_fusion.11.refs_2_
  226.7 12.1 %pad_maximum_fusion.2 = bf16[4096,512]{1,0:T(8,128)(2,1)} fusion(bf16[1024,512]{1,0:T(8,128)(2,1)S(1)} %copy-done.58, bf16[1024,256]{1,0:T(8,128)(2,1)} %collective-permute-done.65, bf16[1024,256]{1,0:T(8,128)(2,1)} %collective-permute-done.63, bf16[1024,512]{1,0:T(8,128)(2,1)S(1)} %collective-permute-done.62, bf16[1024,512]{1,0:T(8,128)(2,1)S(1)} %copy-done.83), kind=kLoop, calls=%fused_computation.5 | loop fusion | flops 20971520 | bytes 8388608 | tf_op jit(solution)/shard_map/concatenate | solution.py:70
  245.4 4.3 add_convert_fusion.10.refs_3_
  249.7 10.2 attend.2
  277.3 10.9 all-to-all-done.2
  289.9 4.9 add_convert_fusion.9.refs_2_
  300.2 4.4 add_convert_fusion.8.refs_3_
  304.6 10.3 attend.3
  338.9 10.6 collective-permute-done.22
  349.5 5.0 collective-permute-done.21
  361.6 10.0 collective-permute-done.68
  381.3 8.5 collective-permute-done.40
  401.5 4.1 collective-permute-done.42
  405.6 5.6 collective-permute-done.41
  427.9 6.1 collective-permute-done.24
  442.1 4.2 pad_maximum_fusion.5
  450.1 11.6 %collective-permute-done.75 = bf16[128,2048]{1,0:T(8,128)(2,1)S(1)} collective-permute-done((bf16[128,2048]{1,0:T(8,128)(2,1)S(1)}, bf16[128,2048]{1,0:T(8,128)(2,1)S(1)}, u32[]{:S(2)}, u32[]{:S(2)}) %collective-permute-start.75) | collective-permute-done | bytes 524320 | tf_op jit(solution)/shard_map/ppermute | solution.py:44
  470.8 5.1 pad_maximum_fusion.9
  484.7 5.2 fusion.164
  490.8 6.2 collective-permute-done.44
  520.9 3.9 fusion.163
  524.9 5.2 multiply_convert_fusion.4
  532.1 11.0 fusion.19
  543.1 6.5 convert_reduce_fusion
  556.4 4.9 convert_reduce_fusion.1
  568.3 12.7 %fusion.16 = bf16[2048,1024]{1,0:T(8,128)(2,1)} fusion(bf16[2048,2048]{1,0:T(8,128)(2,1)} %constant_dynamic-update-slice_fusion.70, bf16[512,1024]{1,0:T(8,128)(2,1)S(1)} %get-tuple-element.290, bf16[512,1024]{1,0:T(8,128)(2,1)S(1)} %get-tuple-element.292, bf16[512,1024]{1,0:T(8,128)(2,1)S(1)} %get-tuple-element.296, ...), kind=kOutput, calls=%fused_computation.31 | convolution fusion | flops 8608808960 | bytes 16777216 | tf_op jit(solution)/shard_map/dot_general | solution.py:151
  581.3 5.0 convolution_convert_fusion.2
  592.4 4.0 add_convert_fusion.1
  605.8 5.5 collective-permute-done.96
  613.7 7.9 collective-permute-done.81
  624.2 5.5 collective-permute-done.97
  637.4 4.9 collective-permute-done.99
  642.4 3.9 collective-permute-done.84
  654.5 9.8 collective-permute-done.85
  669.2 6.4 collective-permute-done.50
  677.9 16.0 %collective-permute-done.86 = bf16[128,1024]{1,0:T(8,128)(2,1)S(1)} collective-permute-done((bf16[128,1024]{1,0:T(8,128)(2,1)S(1)}, bf16[128,1024]{1,0:T(8,128)(2,1)S(1)}, u32[]{:S(2)}, u32[]{:S(2)}) %collective-permute-start.86) | collective-permute-done | bytes 262176 | tf_op jit(solution)/shard_map/ppermute | solution.py:44
  704.4 5.3 collective-permute-done.33
  724.1 12.5 %collective-permute-start.54 = (bf16[2,128,512]{2,1,0:T(8,128)(2,1)S(1)}, bf16[2,128,512]{2,1,0:T(8,128)(2,1)S(1)}, u32[]{:S(2)}, u32[]{:S(2)}) collective-permute-start(bf16[2,128,512]{2,1,0:T(8,128)(2,1)S(1)} %get-tuple-element.211), channel_id=1, source_target_pairs={{0,1},{1,2},{2,3},{3,0},{4,5},{5,6},{6,7},{7,4},{8,9},{9,10},{10,1... | collective-permute-start | bytes 786440 | tf_op jit(solution)/shard_map/ppermute | solution.py:49
  745.3 5.4 collective-permute-start.56
  753.1 13.3 %collective-permute-done.55 = bf16[2,128,512]{2,1,0:T(8,128)(2,1)S(1)} collective-permute-done((bf16[2,128,512]{2,1,0:T(8,128)(2,1)S(1)}, bf16[2,128,512]{2,1,0:T(8,128)(2,1)S(1)}, u32[]{:S(2)}, u32[]{:S(2)}) %collective-permute-start.55) | collective-permute-done | bytes 262176 | tf_op jit(solution)/shard_map/ppermute | solution.py:49
  767.1 5.2 pad_maximum_fusion.11
  779.2 19.0 %attend_back.2 = (bf16[512,768]{1,0:T(8,128)(2,1)}, bf16[512,768]{1,0:T(8,128)(2,1)}) custom-call(s32[8]{0:T(128)} %broadcast_xor_fusion.refs_0_, f32[4]{0:T(128)} %multiply_exponential_fusion.refs_1_, bf16[512,768]{1,0:T(8,128)(2,1)} %add_convert_fusion.11.refs_2_, bf16[512,768]{1,0:T(8,128)(2,1)} %add_convert_fusion.10.refs_3_, ...), custom_call_target="tpu_custom_call" | custom-call | flops 1342177280 | bytes 4194304 | tf_op jit(solution)/shard_map/attend_back/pallas_call | solution.py:299
  798.2 5.3 convolution_convert_fusion.8
  818.1 18.9 %attend_back.3 = (bf16[512,768]{1,0:T(8,128)(2,1)}, bf16[512,768]{1,0:T(8,128)(2,1)}) custom-call(s32[8]{0:T(128)} %broadcast_xor_fusion.refs_0_, f32[4]{0:T(128)} %multiply_exponential_fusion.refs_1_, bf16[512,768]{1,0:T(8,128)(2,1)} %add_convert_fusion.9.refs_2_, bf16[512,768]{1,0:T(8,128)(2,1)} %add_convert_fusion.8.refs_3_, ...), custom_call_target="tpu_custom_call" | custom-call | flops 1342177280 | bytes 4194304 | tf_op jit(solution)/shard_map/attend_back/pallas_call | solution.py:299
  837.0 3.9 convolution_convert_fusion.7
  841.1 7.9 pad_maximum_fusion.1
  857.7 10.4 collective-permute-done.91
  882.1 7.6 collective-permute-done.106
  901.2 9.6 convolution_convert_fusion
  929.2 12.2 %collective-permute-done.110 = bf16[2,128,512]{2,1,0:T(8,128)(2,1)S(1)} collective-permute-done((bf16[2,128,512]{2,1,0:T(8,128)(2,1)S(1)}, bf16[2,128,512]{2,1,0:T(8,128)(2,1)S(1)}, u32[]{:S(2)}, u32[]{:S(2)}) %collective-permute-start.110) | collective-permute-done | bytes 262176 | tf_op jit(solution)/shard_map/ppermute | solution.py:49
  942.1 17.7 %collective-permute-done.111 = bf16[2,128,512]{2,1,0:T(8,128)(2,1)S(1)} collective-permute-done((bf16[2,128,512]{2,1,0:T(8,128)(2,1)S(1)}, bf16[2,128,512]{2,1,0:T(8,128)(2,1)S(1)}, u32[]{:S(2)}, u32[]{:S(2)}) %collective-permute-start.111) | collective-permute-done | bytes 262176 | tf_op jit(solution)/shard_map/ppermute | solution.py:49
  1011.4 7.4 pad_maximum_fusion.3
  1030.2 20.2 %collective-permute-start.118 = (f32[8,1920]{1,0:T(8,128)S(1)}, f32[8,1920]{1,0:T(8,128)S(1)}, u32[]{:S(2)}, u32[]{:S(2)}) collective-permute-start(f32[8,1920]{1,0:T(8,128)S(1)} %get-tuple-element.221), channel_id=1, source_target_pairs={{0,1},{1,2},{2,3},{3,0},{4,5},{5,6},{6,7},{7,4},{8,9},{9,10},{10,1... | collective-permute-start | bytes 184328 | tf_op jit(solution)/shard_map/ppermute | solution.py:49
  1056.2 4.1 all-to-all-start.5
  1084.2 6.5 all-to-all-done.4
  (948 shorter events, 479.7 us)
Async XLA Ops:
  7.2 26.4 %collective-permute-start.3 = (bf16[1024,512]{1,0:T(8,128)(2,1)}, bf16[1024,512]{1,0:T(8,128)(2,1)S(1)}, u32[]{:S(2)}, u32[]{:S(2)}) collective-permute-start(bf16[1024,512]{1,0:T(8,128)(2,1)} %param.23), channel_id=1, source_target_pairs={{0,8},{4,12},{8,0},{12,4},{16,24},{20,28},{24,16},{28,20},{1,9},{5... | collective-permute-start | bytes 3145736 | tf_op jit(solution)/shard_map/ppermute | solution.py:44
  10.2 25.2 %collective-permute-start.5 = (bf16[1024,512]{1,0:T(8,128)(2,1)}, bf16[1024,512]{1,0:T(8,128)(2,1)S(1)}, u32[]{:S(2)}, u32[]{:S(2)}) collective-permute-start(bf16[1024,512]{1,0:T(8,128)(2,1)} %param.23), channel_id=1, source_target_pairs={{0,16},{4,20},{8,24},{12,28},{16,0},{20,4},{24,8},{28,12},{1,17},{... | collective-permute-start | bytes 3145736 | tf_op jit(solution)/shard_map/ppermute | solution.py:44
  51.8 60.9 %collective-permute-start.7 = (bf16[4096,512]{1,0:T(8,128)(2,1)}, bf16[4096,512]{1,0:T(8,128)(2,1)}, u32[]{:S(2)}, u32[]{:S(2)}) collective-permute-start(bf16[4096,512]{1,0:T(8,128)(2,1)} %pad_maximum_fusion), channel_id=1, source_target_pairs={{0,4},{4,0},{8,12},{12,8},{16,20},{20,16},{24,28},{28,24},{1,5},{5... | collective-permute-start | bytes 12582920 | tf_op jit(solution)/shard_map/ppermute | solution.py:44
  54.2 23.0 %all-to-all-start = ((bf16[3,512,256]{2,0,1:T(4,128)(2,1)}), bf16[3,512,256]{2,0,1:T(4,128)(2,1)S(1)}, u32[]{:S(2)}, u32[]{:S(2)}) async-start(bf16[3,512,256]{2,0,1:T(4,128)(2,1)} %bitcast.28), calls=%async_computation | async-start | bytes 2097152 | tf_op jit(solution)/shard_map/all_to_all | solution.py:477
  57.8 160.4 %all-gather.5.cloned.1.call-start = ((), (), s32[]{:S(2)}) async-start(), calls=%async_computation.12 | async-start | bytes 3932160 | tf_op jit(solution)/shard_map/all_gather | solution.py:480
  122.7 33.6 %collective-permute-start.9 = (bf16[2,128,512]{2,1,0:T(8,128)(2,1)S(1)}, bf16[2,128,512]{2,1,0:T(8,128)(2,1)S(1)}, u32[]{:S(2)}, u32[]{:S(2)}) collective-permute-start(bf16[2,128,512]{2,1,0:T(8,128)(2,1)S(1)} %get-tuple-element.214), channel_id=1, source_target_pairs={{0,2},{1,3},{2,0},{3,1},{4,6},{5,7},{6,4},{7,5},{8,10},{9,11},{10,... | collective-permute-start | bytes 786440 | tf_op jit(solution)/shard_map/ppermute | solution.py:49
  125.3 31.0 %collective-permute-start.10 = (bf16[2,128,512]{2,1,0:T(8,128)(2,1)S(1)}, bf16[2,128,512]{2,1,0:T(8,128)(2,1)S(1)}, u32[]{:S(2)}, u32[]{:S(2)}) collective-permute-start(bf16[2,128,512]{2,1,0:T(8,128)(2,1)S(1)} %get-tuple-element.213), channel_id=1, source_target_pairs={{0,3},{1,0},{2,1},{3,2},{4,7},{5,4},{6,5},{7,6},{8,11},{9,8},{10,9... | collective-permute-start | bytes 786440 | tf_op jit(solution)/shard_map/ppermute | solution.py:49
  162.1 28.7 %all-to-all-start.1 = ((bf16[8,64,256]{2,1,0:T(8,128)(2,1)}), bf16[8,64,256]{2,1,0:T(8,128)(2,1)S(1)}, u32[]{:S(2)}, u32[]{:S(2)}) async-start(bf16[8,64,256]{2,1,0:T(8,128)(2,1)} %bitcast.35), calls=%async_computation.1 | async-start | bytes 524288 | tf_op jit(solution)/shard_map/all_to_all | solution.py:477
  165.5 94.4 %all-gather.7.cloned.1.call-start = ((), (), s32[]{:S(2)}) async-start(), calls=%async_computation.13 | async-start | bytes 1310720 | tf_op jit(solution)/shard_map/all_gather | solution.py:480
  192.3 23.1 %collective-permute-start.64 = (bf16[1024,512]{1,0:T(8,128)(2,1)}, bf16[1024,512]{1,0:T(8,128)(2,1)S(1)}, u32[]{:S(2)}, u32[]{:S(2)}) collective-permute-start(bf16[1024,512]{1,0:T(8,128)(2,1)} %param.24), channel_id=1, source_target_pairs={{0,16},{4,20},{8,24},{12,28},{16,0},{20,4},{24,8},{28,12},{1,17},{... | collective-permute-start | bytes 3145736 | tf_op jit(solution)/shard_map/ppermute | solution.py:44
  198.9 39.9 %collective-permute-start.18 = (bf16[512,2048]{1,0:T(8,128)(2,1)}, bf16[512,2048]{1,0:T(8,128)(2,1)}, u32[]{:S(2)}, u32[]{:S(2)}) collective-permute-start(bf16[512,2048]{1,0:T(8,128)(2,1)} %pad_maximum_fusion.4), channel_id=1, source_target_pairs={{0,4},{4,0},{8,12},{12,8},{16,20},{20,16},{24,28},{28,24},{1,5},{5... | collective-permute-start | bytes 6291464 | tf_op jit(solution)/shard_map/ppermute | solution.py:44
  238.8 87.9 %collective-permute-start.66 = (bf16[4096,512]{1,0:T(8,128)(2,1)}, bf16[4096,512]{1,0:T(8,128)(2,1)}, u32[]{:S(2)}, u32[]{:S(2)}) collective-permute-start(bf16[4096,512]{1,0:T(8,128)(2,1)} %pad_maximum_fusion.2), channel_id=1, source_target_pairs={{0,4},{4,0},{8,12},{12,8},{16,20},{20,16},{24,28},{28,24},{1,5},{5... | collective-permute-start | bytes 12582920 | tf_op jit(solution)/shard_map/ppermute | solution.py:44
  263.3 31.5 %collective-permute-start.19 = (bf16[512,2048]{1,0:T(8,128)(2,1)}, bf16[512,2048]{1,0:T(8,128)(2,1)}, u32[]{:S(2)}, u32[]{:S(2)}) collective-permute-start(bf16[512,2048]{1,0:T(8,128)(2,1)} %convolution_convert_fusion.6), channel_id=1, source_target_pairs={{0,4},{4,0},{8,12},{12,8},{16,20},{20,16},{24,28},{28,24},{1,5},{5... | collective-permute-start | bytes 6291464 | tf_op jit(solution)/shard_map/ppermute | solution.py:44
  272.8 211.9 %all-gather.9.cloned.1.call-start = ((), (), s32[]{:S(2)}) async-start(), calls=%async_computation.14 | async-start | bytes 5242880 | tf_op jit(solution)/shard_map/all_gather | solution.py:480
  277.3 22.9 %collective-permute-start.38 = (bf16[512,2048]{1,0:T(8,128)(2,1)}, bf16[512,2048]{1,0:T(8,128)(2,1)}, u32[]{:S(2)}, u32[]{:S(2)}) collective-permute-start(bf16[512,2048]{1,0:T(8,128)(2,1)} %pad_maximum_fusion.6), channel_id=1, source_target_pairs={{0,4},{4,0},{8,12},{12,8},{16,20},{20,16},{24,28},{28,24},{1,5},{5... | collective-permute-start | bytes 6291464 | tf_op jit(solution)/shard_map/ppermute | solution.py:44
  299.9 25.4 %collective-permute-start.20 = (bf16[256,1024]{1,0:T(8,128)(2,1)}, bf16[256,1024]{1,0:T(8,128)(2,1)}, u32[]{:S(2)}, u32[]{:S(2)}) collective-permute-start(bf16[256,1024]{1,0:T(8,128)(2,1)} %get-tuple-element.189), channel_id=1, source_target_pairs={{0,8},{4,12},{8,0},{12,4},{16,24},{20,28},{24,16},{28,20},{1,9},{5... | collective-permute-start | bytes 1572872 | tf_op jit(solution)/shard_map/ppermute | solution.py:44
  317.8 53.7 %collective-permute-start.39 = (bf16[512,2048]{1,0:T(8,128)(2,1)}, bf16[512,2048]{1,0:T(8,128)(2,1)}, u32[]{:S(2)}, u32[]{:S(2)}) collective-permute-start(bf16[512,2048]{1,0:T(8,128)(2,1)} %convolution_convert_fusion.4), channel_id=1, source_target_pairs={{0,4},{4,0},{8,12},{12,8},{16,20},{20,16},{24,28},{28,24},{1,5},{5... | collective-permute-start | bytes 6291464 | tf_op jit(solution)/shard_map/ppermute | solution.py:44
  319.8 72.7 %all-to-all-start.3 = ((bf16[8,256,256]{2,1,0:T(8,128)(2,1)}), bf16[8,256,256]{2,1,0:T(8,128)(2,1)S(1)}, u32[]{:S(2)}, u32[]{:S(2)}) async-start(bf16[8,256,256]{2,1,0:T(8,128)(2,1)} %bitcast.394), calls=%async_computation.3 | async-start | bytes 2097152 | tf_op jit(solution)/shard_map/all_to_all | solution.py:477
  323.4 219.7 %all-gather.11.cloned.1.call-start = ((), (), s32[]{:S(2)}) async-start(), calls=%async_computation.15 | async-start | bytes 5242880 | tf_op jit(solution)/shard_map/all_gather | solution.py:480
  323.4 26.1 %collective-permute-start.22 = (bf16[256,1024]{1,0:T(8,128)(2,1)}, bf16[256,1024]{1,0:T(8,128)(2,1)S(1)}, u32[]{:S(2)}, u32[]{:S(2)}) collective-permute-start(bf16[256,1024]{1,0:T(8,128)(2,1)} %get-tuple-element.190), channel_id=1, source_target_pairs={{0,16},{4,20},{8,24},{12,28},{16,0},{20,4},{24,8},{28,12},{1,17},{... | collective-permute-start | bytes 1572872 | tf_op jit(solution)/shard_map/ppermute | solution.py:44
  326.4 28.2 %collective-permute-start.21 = (bf16[128,1024]{1,0:T(8,128)(2,1)S(1)}, bf16[128,1024]{1,0:T(8,128)(2,1)S(1)}, u32[]{:S(2)}, u32[]{:S(2)}) collective-permute-start(bf16[128,1024]{1,0:T(8,128)(2,1)S(1)} %add_convert_fusion.29), channel_id=1, source_target_pairs={{0,16},{4,20},{8,24},{12,28},{16,0},{20,4},{24,8},{28,12},{1,17},{... | collective-permute-start | bytes 786440 | tf_op jit(solution)/shard_map/ppermute | solution.py:44
  335.1 26.5 %collective-permute-start.67 = (bf16[2,128,512]{2,1,0:T(8,128)(2,1)S(1)}, bf16[2,128,512]{2,1,0:T(8,128)(2,1)S(1)}, u32[]{:S(2)}, u32[]{:S(2)}) collective-permute-start(bf16[2,128,512]{2,1,0:T(8,128)(2,1)S(1)} %get-tuple-element.207), channel_id=1, source_target_pairs={{0,1},{1,2},{2,3},{3,0},{4,5},{5,6},{6,7},{7,4},{8,9},{9,10},{10,1... | collective-permute-start | bytes 786440 | tf_op jit(solution)/shard_map/ppermute | solution.py:49
  335.9 35.6 %collective-permute-start.68 = (bf16[2,128,512]{2,1,0:T(8,128)(2,1)S(1)}, bf16[2,128,512]{2,1,0:T(8,128)(2,1)S(1)}, u32[]{:S(2)}, u32[]{:S(2)}) collective-permute-start(bf16[2,128,512]{2,1,0:T(8,128)(2,1)S(1)} %get-tuple-element.206), channel_id=1, source_target_pairs={{0,2},{1,3},{2,0},{3,1},{4,6},{5,7},{6,4},{7,5},{8,10},{9,11},{10,... | collective-permute-start | bytes 786440 | tf_op jit(solution)/shard_map/ppermute | solution.py:49
  356.8 37.1 %collective-permute-start.23 = (bf16[128,1024]{1,0:T(8,128)(2,1)}, bf16[128,1024]{1,0:T(8,128)(2,1)S(1)}, u32[]{:S(2)}, u32[]{:S(2)}) collective-permute-start(bf16[128,1024]{1,0:T(8,128)(2,1)} %get-tuple-element.188), channel_id=1, source_target_pairs={{0,8},{4,12},{8,0},{12,4},{16,24},{20,28},{24,16},{28,20},{1,9},{5... | collective-permute-start | bytes 786440 | tf_op jit(solution)/shard_map/ppermute | solution.py:44
  381.1 24.6 %collective-permute-start.42 = (bf16[256,1024]{1,0:T(8,128)(2,1)}, bf16[256,1024]{1,0:T(8,128)(2,1)}, u32[]{:S(2)}, u32[]{:S(2)}) collective-permute-start(bf16[256,1024]{1,0:T(8,128)(2,1)} %get-tuple-element.182), channel_id=1, source_target_pairs={{0,16},{4,20},{8,24},{12,28},{16,0},{20,4},{24,8},{28,12},{1,17},{... | collective-permute-start | bytes 1572872 | tf_op jit(solution)/shard_map/ppermute | solution.py:44
  393.8 610.0 %reduce-scatter.9.cloned.1.call-start = ((), (), s32[]{:S(2)}) async-start(), calls=%async_computation.18 | async-start | bytes 5242880 | tf_op jit(solution)/shard_map/reduce_scatter | solution.py:586
  446.3 32.0 %collective-permute-start.28 = (bf16[512,2048]{1,0:T(8,128)(2,1)S(1)}, bf16[512,2048]{1,0:T(8,128)(2,1)S(1)}, u32[]{:S(2)}, u32[]{:S(2)}) collective-permute-start(bf16[512,2048]{1,0:T(8,128)(2,1)S(1)} %pad_maximum_fusion.5), channel_id=1, source_target_pairs={{0,4},{4,0},{8,12},{12,8},{16,20},{20,16},{24,28},{28,24},{1,5},{5... | collective-permute-start | bytes 6291464 | tf_op jit(solution)/shard_map/ppermute | solution.py:44
  476.0 33.7 %collective-permute-start.79 = (bf16[512,2048]{1,0:T(8,128)(2,1)}, bf16[512,2048]{1,0:T(8,128)(2,1)}, u32[]{:S(2)}, u32[]{:S(2)}) collective-permute-start(bf16[512,2048]{1,0:T(8,128)(2,1)} %pad_maximum_fusion.9), channel_id=1, source_target_pairs={{0,4},{4,0},{8,12},{12,8},{16,20},{20,16},{24,28},{28,24},{1,5},{5... | collective-permute-start | bytes 6291464 | tf_op jit(solution)/shard_map/ppermute | solution.py:44
  553.4 39.0 %collective-permute-start.95 = (bf16[512,2048]{1,0:T(8,128)(2,1)}, bf16[512,2048]{1,0:T(8,128)(2,1)}, u32[]{:S(2)}, u32[]{:S(2)}) collective-permute-start(bf16[512,2048]{1,0:T(8,128)(2,1)} %convolution_convert_fusion.1), channel_id=1, source_target_pairs={{0,4},{4,0},{8,12},{12,8},{16,20},{20,16},{24,28},{28,24},{1,5},{5... | collective-permute-start | bytes 6291464 | tf_op jit(solution)/shard_map/ppermute | solution.py:44
  581.1 426.5 %reduce-scatter.11.cloned.1.call-start = ((), (), s32[]{:S(2)}) async-start(), calls=%async_computation.19 | async-start | bytes 5242880 | tf_op jit(solution)/shard_map/reduce_scatter | solution.py:578
  591.8 43.1 %collective-permute-start.49 = (bf16[512,2048]{1,0:T(8,128)(2,1)S(1)}, bf16[512,2048]{1,0:T(8,128)(2,1)S(1)}, u32[]{:S(2)}, u32[]{:S(2)}) collective-permute-start(bf16[512,2048]{1,0:T(8,128)(2,1)S(1)} %convolution_convert_fusion.3), channel_id=1, source_target_pairs={{0,4},{4,0},{8,12},{12,8},{16,20},{20,16},{24,28},{28,24},{1,5},{5... | collective-permute-start | bytes 6291464 | tf_op jit(solution)/shard_map/ppermute | solution.py:44
  598.1 25.2 %collective-permute-start.98 = (bf16[256,1024]{1,0:T(8,128)(2,1)S(1)}, bf16[256,1024]{1,0:T(8,128)(2,1)S(1)}, u32[]{:S(2)}, u32[]{:S(2)}) collective-permute-start(bf16[256,1024]{1,0:T(8,128)(2,1)S(1)} %get-tuple-element.166), channel_id=1, source_target_pairs={{0,16},{4,20},{8,24},{12,28},{16,0},{20,4},{24,8},{28,12},{1,17},{... | collective-permute-start | bytes 1572872 | tf_op jit(solution)/shard_map/ppermute | solution.py:44
  602.3 28.2 %collective-permute-start.83 = (bf16[256,1024]{1,0:T(8,128)(2,1)S(1)}, bf16[256,1024]{1,0:T(8,128)(2,1)S(1)}, u32[]{:S(2)}, u32[]{:S(2)}) collective-permute-start(bf16[256,1024]{1,0:T(8,128)(2,1)S(1)} %get-tuple-element.174), channel_id=1, source_target_pairs={{0,16},{4,20},{8,24},{12,28},{16,0},{20,4},{24,8},{28,12},{1,17},{... | collective-permute-start | bytes 1572872 | tf_op jit(solution)/shard_map/ppermute | solution.py:44
  621.7 45.0 %collective-permute-start.30 = (bf16[256,1024]{1,0:T(8,128)(2,1)}, bf16[256,1024]{1,0:T(8,128)(2,1)}, u32[]{:S(2)}, u32[]{:S(2)}) collective-permute-start(bf16[256,1024]{1,0:T(8,128)(2,1)} %get-tuple-element.185), channel_id=1, source_target_pairs={{0,8},{4,12},{8,0},{12,4},{16,24},{20,28},{24,16},{28,20},{1,9},{5... | collective-permute-start | bytes 1572872 | tf_op jit(solution)/shard_map/ppermute | solution.py:44
  652.7 22.9 %collective-permute-start.50 = (bf16[256,1024]{1,0:T(8,128)(2,1)}, bf16[256,1024]{1,0:T(8,128)(2,1)}, u32[]{:S(2)}, u32[]{:S(2)}) collective-permute-start(bf16[256,1024]{1,0:T(8,128)(2,1)} %get-tuple-element.177), channel_id=1, source_target_pairs={{0,8},{4,12},{8,0},{12,4},{16,24},{20,28},{24,16},{28,20},{1,9},{5... | collective-permute-start | bytes 1572872 | tf_op jit(solution)/shard_map/ppermute | solution.py:44
  653.6 401.0 %reduce-scatter.7.cloned.1.call-start = ((), (), s32[]{:S(2)}) async-start(), calls=%async_computation.17 | async-start | bytes 1310720 | tf_op jit(solution)/shard_map/reduce_scatter | solution.py:604
  653.6 43.0 %collective-permute-start.32 = (bf16[256,1024]{1,0:T(8,128)(2,1)}, bf16[256,1024]{1,0:T(8,128)(2,1)S(1)}, u32[]{:S(2)}, u32[]{:S(2)}) collective-permute-start(bf16[256,1024]{1,0:T(8,128)(2,1)} %get-tuple-element.186), channel_id=1, source_target_pairs={{0,16},{4,20},{8,24},{12,28},{16,0},{20,4},{24,8},{28,12},{1,17},{... | collective-permute-start | bytes 1572872 | tf_op jit(solution)/shard_map/ppermute | solution.py:44
  664.2 37.2 %collective-permute-start.52 = (bf16[256,1024]{1,0:T(8,128)(2,1)}, bf16[256,1024]{1,0:T(8,128)(2,1)S(1)}, u32[]{:S(2)}, u32[]{:S(2)}) collective-permute-start(bf16[256,1024]{1,0:T(8,128)(2,1)} %get-tuple-element.178), channel_id=1, source_target_pairs={{0,16},{4,20},{8,24},{12,28},{16,0},{20,4},{24,8},{28,12},{1,17},{... | collective-permute-start | bytes 1572872 | tf_op jit(solution)/shard_map/ppermute | solution.py:44
  665.8 28.1 %collective-permute-start.86 = (bf16[128,1024]{1,0:T(8,128)(2,1)S(1)}, bf16[128,1024]{1,0:T(8,128)(2,1)S(1)}, u32[]{:S(2)}, u32[]{:S(2)}) collective-permute-start(bf16[128,1024]{1,0:T(8,128)(2,1)S(1)} %slice.928), channel_id=1, source_target_pairs={{0,16},{4,20},{8,24},{12,28},{16,0},{20,4},{24,8},{28,12},{1,17},{... | collective-permute-start | bytes 786440 | tf_op jit(solution)/shard_map/ppermute | solution.py:44
  666.7 28.1 %collective-permute-start.88 = (bf16[128,1024]{1,0:T(8,128)(2,1)S(1)}, bf16[128,1024]{1,0:T(8,128)(2,1)S(1)}, u32[]{:S(2)}, u32[]{:S(2)}) collective-permute-start(bf16[128,1024]{1,0:T(8,128)(2,1)S(1)} %slice.929), channel_id=1, source_target_pairs={{0,8},{4,12},{8,0},{12,4},{16,24},{20,28},{24,16},{28,20},{1,9},{5... | collective-permute-start | bytes 786440 | tf_op jit(solution)/shard_map/ppermute | solution.py:44
  675.6 23.9 %collective-permute-start.31 = (bf16[128,1024]{1,0:T(8,128)(2,1)S(1)}, bf16[128,1024]{1,0:T(8,128)(2,1)S(1)}, u32[]{:S(2)}, u32[]{:S(2)}) collective-permute-start(bf16[128,1024]{1,0:T(8,128)(2,1)S(1)} %add_convert_fusion.27), channel_id=1, source_target_pairs={{0,16},{4,20},{8,24},{12,28},{16,0},{20,4},{24,8},{28,12},{1,17},{... | collective-permute-start | bytes 786440 | tf_op jit(solution)/shard_map/ppermute | solution.py:44
  720.6 23.3 %collective-permute-start.102 = (bf16[128,2048]{1,0:T(8,128)(2,1)S(1)}, bf16[128,2048]{1,0:T(8,128)(2,1)S(1)}, u32[]{:S(2)}, u32[]{:S(2)}) collective-permute-start(bf16[128,2048]{1,0:T(8,128)(2,1)S(1)} %get-tuple-element.142), channel_id=1, source_target_pairs={{0,16},{4,20},{8,24},{12,28},{16,0},{20,4},{24,8},{28,12},{1,17},{... | collective-permute-start | bytes 1572872 | tf_op jit(solution)/shard_map/ppermute | solution.py:44
  724.1 28.3 %collective-permute-start.54 = (bf16[2,128,512]{2,1,0:T(8,128)(2,1)S(1)}, bf16[2,128,512]{2,1,0:T(8,128)(2,1)S(1)}, u32[]{:S(2)}, u32[]{:S(2)}) collective-permute-start(bf16[2,128,512]{2,1,0:T(8,128)(2,1)S(1)} %get-tuple-element.211), channel_id=1, source_target_pairs={{0,1},{1,2},{2,3},{3,0},{4,5},{5,6},{6,7},{7,4},{8,9},{9,10},{10,1... | collective-permute-start | bytes 786440 | tf_op jit(solution)/shard_map/ppermute | solution.py:49
  737.5 28.9 %collective-permute-start.55 = (bf16[2,128,512]{2,1,0:T(8,128)(2,1)S(1)}, bf16[2,128,512]{2,1,0:T(8,128)(2,1)S(1)}, u32[]{:S(2)}, u32[]{:S(2)}) collective-permute-start(bf16[2,128,512]{2,1,0:T(8,128)(2,1)S(1)} %get-tuple-element.212), channel_id=1, source_target_pairs={{0,2},{1,3},{2,0},{3,1},{4,6},{5,7},{6,4},{7,5},{8,10},{9,11},{10,... | collective-permute-start | bytes 786440 | tf_op jit(solution)/shard_map/ppermute | solution.py:49
  742.8 24.3 %collective-permute-start.101 = (bf16[128,1024]{1,0:T(8,128)(2,1)S(1)}, bf16[128,1024]{1,0:T(8,128)(2,1)S(1)}, u32[]{:S(2)}, u32[]{:S(2)}) collective-permute-start(bf16[128,1024]{1,0:T(8,128)(2,1)S(1)} %slice.950), channel_id=1, source_target_pairs={{0,16},{4,20},{8,24},{12,28},{16,0},{20,4},{24,8},{28,12},{1,17},{... | collective-permute-start | bytes 786440 | tf_op jit(solution)/shard_map/ppermute | solution.py:44
  744.0 23.2 %collective-permute-start.103 = (bf16[128,1024]{1,0:T(8,128)(2,1)S(1)}, bf16[128,1024]{1,0:T(8,128)(2,1)S(1)}, u32[]{:S(2)}, u32[]{:S(2)}) collective-permute-start(bf16[128,1024]{1,0:T(8,128)(2,1)S(1)} %slice.951), channel_id=1, source_target_pairs={{0,8},{4,12},{8,0},{12,4},{16,24},{20,28},{24,16},{28,20},{1,9},{5... | collective-permute-start | bytes 786440 | tf_op jit(solution)/shard_map/ppermute | solution.py:44
  745.3 27.0 %collective-permute-start.56 = (bf16[2,128,512]{2,1,0:T(8,128)(2,1)S(1)}, bf16[2,128,512]{2,1,0:T(8,128)(2,1)S(1)}, u32[]{:S(2)}, u32[]{:S(2)}) collective-permute-start(bf16[2,128,512]{2,1,0:T(8,128)(2,1)S(1)} %get-tuple-element.209), channel_id=1, source_target_pairs={{0,3},{1,0},{2,1},{3,2},{4,7},{5,4},{6,5},{7,6},{8,11},{9,8},{10,9... | collective-permute-start | bytes 786440 | tf_op jit(solution)/shard_map/ppermute | solution.py:49
  772.3 42.8 %collective-permute-start.104 = (bf16[512,2048]{1,0:T(8,128)(2,1)}, bf16[512,2048]{1,0:T(8,128)(2,1)}, u32[]{:S(2)}, u32[]{:S(2)}) collective-permute-start(bf16[512,2048]{1,0:T(8,128)(2,1)} %pad_maximum_fusion.11), channel_id=1, source_target_pairs={{0,4},{4,0},{8,12},{12,8},{16,20},{20,16},{24,28},{28,24},{1,5},{5... | collective-permute-start | bytes 6291464 | tf_op jit(solution)/shard_map/ppermute | solution.py:44
  773.0 34.5 %collective-permute-start.57 = (bf16[1024,512]{1,0:T(8,128)(2,1)}, bf16[1024,512]{1,0:T(8,128)(2,1)}, u32[]{:S(2)}, u32[]{:S(2)}) collective-permute-start(bf16[1024,512]{1,0:T(8,128)(2,1)} %bitcast.53), channel_id=1, source_target_pairs={{0,8},{4,12},{8,0},{12,4},{16,24},{20,28},{24,16},{28,20},{1,9},{5... | collective-permute-start | bytes 3145736 | tf_op jit(solution)/shard_map/ppermute | solution.py:44
  774.7 35.1 %collective-permute-start.59 = (bf16[1024,512]{1,0:T(8,128)(2,1)}, bf16[1024,512]{1,0:T(8,128)(2,1)}, u32[]{:S(2)}, u32[]{:S(2)}) collective-permute-start(bf16[1024,512]{1,0:T(8,128)(2,1)} %bitcast.53), channel_id=1, source_target_pairs={{0,16},{4,20},{8,24},{12,28},{16,0},{20,4},{24,8},{28,12},{1,17},{... | collective-permute-start | bytes 3145736 | tf_op jit(solution)/shard_map/ppermute | solution.py:44
  803.5 46.2 %collective-permute-start.90 = (bf16[512,2048]{1,0:T(8,128)(2,1)}, bf16[512,2048]{1,0:T(8,128)(2,1)}, u32[]{:S(2)}, u32[]{:S(2)}) collective-permute-start(bf16[512,2048]{1,0:T(8,128)(2,1)} %convolution_convert_fusion.8), channel_id=1, source_target_pairs={{0,4},{4,0},{8,12},{12,8},{16,20},{20,16},{24,28},{28,24},{1,5},{5... | collective-permute-start | bytes 6291464 | tf_op jit(solution)/shard_map/ppermute | solution.py:44
  809.4 31.7 %collective-permute-start.58 = (bf16[1024,256]{1,0:T(8,128)(2,1)}, bf16[1024,256]{1,0:T(8,128)(2,1)}, u32[]{:S(2)}, u32[]{:S(2)}) collective-permute-start(bf16[1024,256]{1,0:T(8,128)(2,1)} %slice.908), channel_id=1, source_target_pairs={{0,16},{4,20},{8,24},{12,28},{16,0},{20,4},{24,8},{28,12},{1,17},{... | collective-permute-start | bytes 1572872 | tf_op jit(solution)/shard_map/ppermute | solution.py:44
  811.7 29.4 %collective-permute-start.60 = (bf16[1024,256]{1,0:T(8,128)(2,1)}, bf16[1024,256]{1,0:T(8,128)(2,1)}, u32[]{:S(2)}, u32[]{:S(2)}) collective-permute-start(bf16[1024,256]{1,0:T(8,128)(2,1)} %slice.909), channel_id=1, source_target_pairs={{0,8},{4,12},{8,0},{12,4},{16,24},{20,28},{24,16},{28,20},{1,9},{5... | collective-permute-start | bytes 1572872 | tf_op jit(solution)/shard_map/ppermute | solution.py:44
  841.0 31.2 %collective-permute-start.105 = (bf16[512,2048]{1,0:T(8,128)(2,1)S(1)}, bf16[512,2048]{1,0:T(8,128)(2,1)S(1)}, u32[]{:S(2)}, u32[]{:S(2)}) collective-permute-start(bf16[512,2048]{1,0:T(8,128)(2,1)S(1)} %convolution_convert_fusion.7), channel_id=1, source_target_pairs={{0,4},{4,0},{8,12},{12,8},{16,20},{20,16},{24,28},{28,24},{1,5},{5... | collective-permute-start | bytes 6291464 | tf_op jit(solution)/shard_map/ppermute | solution.py:44
  849.0 170.5 %collective-permute-start.61 = (bf16[4096,512]{1,0:T(8,128)(2,1)}, bf16[4096,512]{1,0:T(8,128)(2,1)}, u32[]{:S(2)}, u32[]{:S(2)}) collective-permute-start(bf16[4096,512]{1,0:T(8,128)(2,1)} %pad_maximum_fusion.1), channel_id=1, source_target_pairs={{0,4},{4,0},{8,12},{12,8},{16,20},{20,16},{24,28},{28,24},{1,5},{5... | collective-permute-start | bytes 12582920 | tf_op jit(solution)/shard_map/ppermute | solution.py:44
  856.1 35.3 %collective-permute-start.93 = (bf16[256,1024]{1,0:T(8,128)(2,1)}, bf16[256,1024]{1,0:T(8,128)(2,1)}, u32[]{:S(2)}, u32[]{:S(2)}) collective-permute-start(bf16[256,1024]{1,0:T(8,128)(2,1)} %get-tuple-element.170), channel_id=1, source_target_pairs={{0,16},{4,20},{8,24},{12,28},{16,0},{20,4},{24,8},{28,12},{1,17},{... | collective-permute-start | bytes 1572872 | tf_op jit(solution)/shard_map/ppermute | solution.py:44
  882.0 184.2 %reduce-scatter.5.cloned.1.call-start = ((), (), s32[]{:S(2)}) async-start(), calls=%async_computation.16 | async-start | bytes 3932160 | tf_op jit(solution)/shard_map/reduce_scatter | solution.py:612
  925.8 34.0 %collective-permute-start.111 = (bf16[2,128,512]{2,1,0:T(8,128)(2,1)S(1)}, bf16[2,128,512]{2,1,0:T(8,128)(2,1)S(1)}, u32[]{:S(2)}, u32[]{:S(2)}) collective-permute-start(bf16[2,128,512]{2,1,0:T(8,128)(2,1)S(1)} %get-tuple-element.204), channel_id=1, source_target_pairs={{0,2},{1,3},{2,0},{3,1},{4,6},{5,7},{6,4},{7,5},{8,10},{9,11},{10,... | collective-permute-start | bytes 786440 | tf_op jit(solution)/shard_map/ppermute | solution.py:49
  929.2 31.3 %collective-permute-start.112 = (bf16[2,128,512]{2,1,0:T(8,128)(2,1)S(1)}, bf16[2,128,512]{2,1,0:T(8,128)(2,1)S(1)}, u32[]{:S(2)}, u32[]{:S(2)}) collective-permute-start(bf16[2,128,512]{2,1,0:T(8,128)(2,1)S(1)} %get-tuple-element.201), channel_id=1, source_target_pairs={{0,3},{1,0},{2,1},{3,2},{4,7},{5,4},{6,5},{7,6},{8,11},{9,8},{10,9... | collective-permute-start | bytes 786440 | tf_op jit(solution)/shard_map/ppermute | solution.py:49
  961.2 33.2 %collective-permute-start.113 = (bf16[1024,512]{1,0:T(8,128)(2,1)}, bf16[1024,512]{1,0:T(8,128)(2,1)}, u32[]{:S(2)}, u32[]{:S(2)}) collective-permute-start(bf16[1024,512]{1,0:T(8,128)(2,1)} %bitcast.86), channel_id=1, source_target_pairs={{0,8},{4,12},{8,0},{12,4},{16,24},{20,28},{24,16},{28,20},{1,9},{5... | collective-permute-start | bytes 3145736 | tf_op jit(solution)/shard_map/ppermute | solution.py:44
  961.2 37.1 %collective-permute-start.115 = (bf16[1024,512]{1,0:T(8,128)(2,1)}, bf16[1024,512]{1,0:T(8,128)(2,1)}, u32[]{:S(2)}, u32[]{:S(2)}) collective-permute-start(bf16[1024,512]{1,0:T(8,128)(2,1)} %bitcast.86), channel_id=1, source_target_pairs={{0,16},{4,20},{8,24},{12,28},{16,0},{20,4},{24,8},{28,12},{1,17},{... | collective-permute-start | bytes 3145736 | tf_op jit(solution)/shard_map/ppermute | solution.py:44
  1018.9 76.6 %collective-permute-start.117 = (bf16[4096,512]{1,0:T(8,128)(2,1)}, bf16[4096,512]{1,0:T(8,128)(2,1)}, u32[]{:S(2)}, u32[]{:S(2)}) collective-permute-start(bf16[4096,512]{1,0:T(8,128)(2,1)} %pad_maximum_fusion.3), channel_id=1, source_target_pairs={{0,4},{4,0},{8,12},{12,8},{16,20},{20,16},{24,28},{28,24},{1,5},{5... | collective-permute-start | bytes 12582920 | tf_op jit(solution)/shard_map/ppermute | solution.py:44
  1026.5 29.7 %all-to-all-start.7 = ((bf16[256,8,256]{2,0,1:T(8,128)(2,1)}), bf16[256,8,256]{2,0,1:T(8,128)(2,1)S(1)}, u32[]{:S(2)}, u32[]{:S(2)}) async-start(bf16[256,8,256]{2,0,1:T(8,128)(2,1)} %bitcast.358), calls=%async_computation.11 | async-start | bytes 2097152 | tf_op jit(solution)/shard_map/all_to_all | solution.py:477
  1030.2 30.1 %collective-permute-start.118 = (f32[8,1920]{1,0:T(8,128)S(1)}, f32[8,1920]{1,0:T(8,128)S(1)}, u32[]{:S(2)}, u32[]{:S(2)}) collective-permute-start(f32[8,1920]{1,0:T(8,128)S(1)} %get-tuple-element.221), channel_id=1, source_target_pairs={{0,1},{1,2},{2,3},{3,0},{4,5},{5,6},{6,7},{7,4},{8,9},{9,10},{10,1... | collective-permute-start | bytes 184328 | tf_op jit(solution)/shard_map/ppermute | solution.py:49
  (245 other events, 3352.0 us)
Sparse Core Ops, SparseCore 0:
  78.5 83.8 all-gather.4
  191.7 27.9 all-gather.6
  290.0 102.0 all-gather.8
  394.1 91.5 all-gather.10
  581.2 88.8 reduce-scatter.8
  672.3 89.4 reduce-scatter.10
  882.1 30.3 reduce-scatter.6
  914.8 78.1 reduce-scatter.4

commit v2 on v1

--- a/solution.py
+++ b/solution.py
@@ -5,6 +5,7 @@
 from jax.experimental.pallas import tpu as pltpu
 from jax.sharding import PartitionSpec as P
 
+
 H = 32
 BLK = 128
 MAXLEN = 1024
@@ -53,45 +54,71 @@
     return lax.optimization_barrier((values, others))[0]
 
 
-def near_kinds():
+def near_order(bins):
     count = lax.axis_size("dp")
-    return [0, 2, 6, 4] if count == 8 else list(range(0, count, 2))
-
-
-def plane_gather(rows):
-    if lax.axis_size("dp") == 8:
-        half = rows.shape[1] // 2
+    if count == 8 and bins == 2:
+        return [(0, 0), (0, 1), (2, 1), (2, 0), (6, 0), (6, 1), (4, 1), (4, 0)]
+    return [(k, b) for k in range(0, count, 2) for b in range(bins)]
+
+
+def plane_gather(rows, bins):
+    if lax.axis_size("dp") == 8 and bins == 2:
+        half = rows.shape[0] // 2
         a = swap(rows, 2)
         b = swap(rows, 4)
-        corner = [swap(a[:, :half], 4), swap(b[:, half:], 2)]
-        pieces = [rows, a, jnp.concatenate(corner, axis=1), b]
+        c = swap(a[:half], 4)
+        d = swap(b[half:], 2)
+        pieces = [rows, a[half:], a[:half], c, d, b[half:], b[:half]]
     else:
-        pieces = [swap(rows, k) if k else rows for k in near_kinds()]
+        pieces = [swap(rows, k) if k else rows for k in range(0, lax.axis_size("dp"), 2)]
     near = jnp.concatenate(pieces, axis=0)
     return near, swap(near, 1)
 
 
-def plane_sum(near, far, weight, dim):
+def sum_pair(near, far, weight, dim):
+    other = swap(contract(far, weight, 1, dim).astype(bf16), 1)
+    return (contract(near, weight, 1, dim) + other.astype(f32)).astype(bf16)
+
+
+def sum_first(both, bins):
     count = lax.axis_size("dp")
-    step = near.shape[0] * 2 // count
-    other = swap(contract(far, weight, 1, dim).astype(bf16), 1)
-    both = (contract(near, weight, 1, dim) + other.astype(f32)).astype(bf16)
-    if count == 8:
-        half = both.shape[1] // 2
-        a = swap(both[step : 3 * step, :half], 2)
-        b = swap(both[2 * step :, half:], 4)
-        c = both[3 * step :, :half].astype(f32) + a[step:].astype(f32)
-        d = both[step : 2 * step, half:].astype(f32) + b[:step].astype(f32)
-        c = swap(c.astype(bf16), 4)
-        d = swap(d.astype(bf16), 2)
-        left = both[:step, :half].astype(f32) + a[:step].astype(f32) + c.astype(f32)
-        right = both[:step, half:].astype(f32) + b[step:].astype(f32) + d.astype(f32)
-        return jnp.concatenate([left, right], axis=1)
+    step = both.shape[0] * 2 // count
+    if count == 8 and bins == 2:
+        half = step // 2
+        return [swap(both[3 * half : 5 * half], 2), swap(both[5 * half : 7 * half], 4)]
+    return [swap(both[j * step : (j + 1) * step], 2 * j) for j in range(1, count // 2)]
+
+
+def sum_second(both, first, bins):
+    if lax.axis_size("dp") == 8 and bins == 2:
+        half = both.shape[0] // 8
+        a, b = [v.astype(f32) for v in first]
+        c = both[7 * half :].astype(f32) + a[half:]
+        d = both[2 * half : 3 * half].astype(f32) + b[:half]
+        return [swap(c.astype(bf16), 4), swap(d.astype(bf16), 2)]
+    return []
+
+
+def sum_last(both, first, second, bins):
+    count = lax.axis_size("dp")
+    step = both.shape[0] * 2 // count
+    if count == 8 and bins == 2:
+        half = step // 2
+        (a, b), (c, d) = [[v.astype(f32) for v in pair] for pair in (first, second)]
+        upper = both[:half].astype(f32) + a[:half] + c
+        lower = both[half:step].astype(f32) + b[half:] + d
+        return jnp.concatenate([upper, lower], axis=0)
     total = both[:step].astype(f32)
-    for j, k in enumerate(near_kinds()):
-        if k:
-            total = total + swap(both[j * step : (j + 1) * step], k).astype(f32)
+    for v in first:
+        total = total + v.astype(f32)
     return total
+
+
+def plane_sum(near, far, weight, dim, bins):
+    both = sum_pair(near, far, weight, dim)
+    first = sum_first(both, bins)
+    second = sum_second(both, first, bins)
+    return sum_last(both, first, second, bins)
 
 
 def small_gather(value):
@@ -104,58 +131,92 @@
     return jnp.take(value, jnp.arange(count, dtype=jnp.int32) ^ lax.axis_index("dp"), axis=0)
 
 
-def pick_blocks(near, far, owner, local, blocks):
-    rank = lax.axis_index("dp")
-    near = near.reshape(-1, BLK, near.shape[-1])
-    far = far.reshape(-1, BLK, far.shape[-1])
-    kinds = near_kinds()
-    piece = jnp.array([kinds.index(2 * j) for j in range(len(kinds))], jnp.int32)
-    k = owner ^ rank
-    at = piece[k // 2] * blocks + local
-    picked = []
-    for i in range(owner.shape[0]):
-        a = lax.dynamic_index_in_dim(near, at[i], 0, keepdims=True)
-        b = lax.dynamic_index_in_dim(far, at[i], 0, keepdims=True)
-        picked.append(jnp.where(k[i] % 2 == 0, a, b))
-    return jnp.concatenate(picked, axis=0)
-
-
-def to_bins(blocks, here):
+def pick_blocks(rows, wanted):
+    count = wanted.shape[0]
+
+    def body(table, source, out):
+        for i in range(count):
+            begin = pl.multiple_of(table[i] * BLK, BLK)
+            out[i * BLK : (i + 1) * BLK, :] = source[pl.ds(begin, BLK), :]
+
+    return pl.pallas_call(
+        body,
+        out_shape=jax.ShapeDtypeStruct((count * BLK, rows.shape[1]), rows.dtype),
+        in_specs=[smem(), vmem()],
+        out_specs=vmem(),
+        name="pick",
+    )(wanted, rows)
+
+
+def to_bins(pieces):
     count = lax.axis_size("tensor")
     z = lax.axis_index("tensor")
-    wide = blocks.shape[-1]
-    out = jnp.zeros((here, BLK, wide * count), blocks.dtype)
-    for r in range(count):
-        piece = lax.dynamic_slice_in_dim(blocks, ((z + r) % count) * here, here, 0)
+    wide = pieces[0].shape[-1]
+    out = jnp.zeros((pieces[0].shape[0], wide * count), pieces[0].dtype)
+    for r, piece in enumerate(pieces):
         if r:
             piece = turn(piece, r)
-        out = lax.dynamic_update_slice(out, piece, (0, 0, ((z - r) % count) * wide))
+        out = lax.dynamic_update_slice(out, piece, (0, ((z - r) % count) * wide))
     return out
 
 
 def from_bins(rows):
     count = lax.axis_size("tensor")
     z = lax.axis_index("tensor")
-    here = rows.shape[0]
     wide = rows.shape[-1] // count
-    out = jnp.zeros((here * count, BLK, wide), rows.dtype)
+    pieces = []
     for r in range(count):
-        piece = lax.dynamic_slice_in_dim(rows, ((z + r) % count) * wide, wide, 2)
-        if r:
-            piece = turn(piece, r)
-        out = lax.dynamic_update_slice(out, piece, (((z - r) % count) * here, 0, 0))
-    return out
+        piece = lax.dynamic_slice_in_dim(rows, ((z + r) % count) * wide, wide, 1)
+        pieces.append(turn(piece, r) if r else piece)
+    return jnp.concatenate(pieces, axis=0)
 
 
 def contract(a, b, left, right):
     return lax.dot_general(a, b, (((left,), (right,)), ((), ())), preferred_element_type=f32)
 
 
-def attend_kernel(heads, head_size, where, slopes, near, far, out_near, out_far, qkv, mixed):
+def spread_blocks(bin_block):
+    count = lax.axis_size("dp")
+    edges = count * count
+    levels = count.bit_length() - 1
+    assert count == 1 << levels and bin_block.shape == (edges,)
+
+    def body(bin_column, bin_row, color):
+        column = lax.broadcasted_iota(jnp.int32, (edges, 1), 0)
+        row = lax.broadcasted_iota(jnp.int32, (1, edges), 1)
+        here_column, here_row = column, row
+        there_column, there_row = bin_column[...], bin_row[...]
+        for level in range(levels):
+            half = 1 << (levels - level - 1)
+            here = jnp.where((here_column ^ 1) == here_row, 1.0, 0.0).astype(bf16)
+            there = jnp.where((there_column ^ 1) == there_row, 1.0, 0.0).astype(bf16)
+            hop = contract(here, there, 1, 0).astype(bf16)
+            least_column, least_row = column.astype(f32), row.astype(f32)
+            for _ in range(2 * levels - 1):
+                least_column = jnp.minimum(least_column, contract(hop, least_column.astype(bf16), 1, 0))
+                least_row = jnp.minimum(least_row, contract(least_row.astype(bf16), hop, 1, 0))
+                hop = contract(hop, hop, 1, 0).astype(bf16)
+            bit_column = least_column > contract(here, least_column.astype(bf16), 1, 0)
+            bit_row = least_row > contract(least_row.astype(bf16), here, 1, 0)
+
+            def refine(key, bit):
+                low = key & (2 * half - 1)
+                return key - low + jnp.where(bit, half, 0) + (low >> 1)
+
+            here_column, here_row = refine(here_column, bit_column), refine(here_row, bit_row)
+            there_column, there_row = refine(there_column, bit_column), refine(there_row, bit_row)
+        color[...] = here_row & (count - 1)
+
+    color = pl.pallas_call(
+        body, out_shape=jax.ShapeDtypeStruct((1, edges), jnp.int32), name="spread_blocks"
+    )(bin_block.reshape(edges, 1), bin_block.reshape(1, edges))
+    return color.reshape(count, count)
+
+
+def attend_kernel(bins, heads, head_size, order, where, slopes, near, far, out_near, out_far, qkv, mixed):
     width = heads * head_size
-    blocks = near.shape[0] // BLK
-    for j in range(2 * blocks):
-        source, i = (near, j) if j < blocks else (far, j - blocks)
+    for j, b in enumerate(order):
+        source, i = (near, j) if j < len(order) // 2 else (far, j - len(order) // 2)
         at = pl.multiple_of(where[j] * BLK, BLK)
         for part in range(3):
             for h in range(heads):
@@ -163,11 +224,11 @@
                 piece = source[i * BLK : (i + 1) * BLK, lo : lo + head_size]
                 if part == 0:
                     piece = (piece.astype(f32) * 0.125).astype(bf16)
-                qkv[part, h, pl.ds(at, BLK), :] = piece
-    slots = 2 * blocks * BLK
+                qkv[part, b * heads + h, pl.ds(at, BLK), :] = piece
+    slots = qkv.shape[2]
 
     def one_head(h, carry):
-        slope = slopes[h]
+        slope = slopes[h % heads]
         for t in range(slots // TILE):
             lo, hi = t * TILE, (t + 1) * TILE
             query = qkv[0, h, lo:hi, :]
@@ -186,23 +247,23 @@
             mixed[h, lo:hi, :] = result.astype(bf16)
         return carry
 
-    lax.fori_loop(0, heads, one_head, 0)
-    for j in range(2 * blocks):
-        target, i = (out_near, j) if j < blocks else (out_far, j - blocks)
+    lax.fori_loop(0, bins * heads, one_head, 0)
+    for j, b in enumerate(order):
+        target, i = (out_near, j) if j < len(order) // 2 else (out_far, j - len(order) // 2)
         at = pl.multiple_of(where[j] * BLK, BLK)
         for h in range(heads):
             target[i * BLK : (i + 1) * BLK, h * head_size : (h + 1) * head_size] = mixed[
-                h, pl.ds(at, BLK), :
+                b * heads + h, pl.ds(at, BLK), :
             ]
 
 
 def attend_back_kernel(
-    heads, head_size, where, slopes, near, far, grad_near, grad_far, out_near, out_far, qkvg, sums, parts
+    bins, heads, head_size, order, where, slopes, near, far, grad_near, grad_far, out_near, out_far, qkvg, sums, parts
 ):
     width = heads * head_size
-    blocks = near.shape[0] // BLK
-    for j in range(2 * blocks):
-        source, grad, i = (near, grad_near, j) if j < blocks else (far, grad_far, j - blocks)
+    for j, b in enumerate(order):
+        near_half = j < len(order) // 2
+        source, grad, i = (near, grad_near, j) if near_half else (far, grad_far, j - len(order) // 2)
         at = pl.multiple_of(where[j] * BLK, BLK)
         for part in range(4):
             for h in range(heads):
@@ -213,11 +274,11 @@
                     piece = grad[i * BLK : (i + 1) * BLK, h * head_size : (h + 1) * head_size]
                 if part == 0:
                     piece = (piece.astype(f32) * 0.125).astype(bf16)
-                qkvg[part, h, pl.ds(at, BLK), :] = piece
-    slots = 2 * blocks * BLK
+                qkvg[part, b * heads + h, pl.ds(at, BLK), :] = piece
+    slots = qkvg.shape[2]
 
     def one_head(h, carry):
-        slope = slopes[h]
+        slope = slopes[h % heads]
         sums[...] = jnp.zeros_like(sums)
         for t in range(slots // TILE):
             lo, hi = t * TILE, (t + 1) * TILE
@@ -247,14 +308,16 @@
         parts[2, h] = sums[1].astype(bf16)
         return carry
 
-    lax.fori_loop(0, heads, one_head, 0)
-    for j in range(2 * blocks):
-        target, i = (out_near, j) if j < blocks else (out_far, j - blocks)
+    lax.fori_loop(0, bins * heads, one_head, 0)
+    for j, b in enumerate(order):
+        target, i = (out_near, j) if j < len(order) // 2 else (out_far, j - len(order) // 2)
         at = pl.multiple_of(where[j] * BLK, BLK)
         for part in range(3):
             for h in range(heads):
                 lo = part * width + h * head_size
-                target[i * BLK : (i + 1) * BLK, lo : lo + head_size] = parts[part, h, pl.ds(at, BLK), :]
+                target[i * BLK : (i + 1) * BLK, lo : lo + head_size] = parts[
+                    part, b * heads + h, pl.ds(at, BLK), :
+                ]
 
 
 def smem():
@@ -265,13 +328,14 @@
     return pl.BlockSpec(memory_space=pltpu.VMEM)
 
 
-def attend_one(near, far, where, slopes, heads, head_size):
-    slots = 2 * near.shape[0]
+def attend_one(near, far, order, where, slopes, heads, head_size):
+    bins = max(order) + 1
+    slots = 2 * near.shape[0] // bins
     width = heads * head_size
     half = jax.ShapeDtypeStruct((near.shape[0], width), bf16)
 
     def body(*refs):
-        attend_kernel(heads, head_size, *refs)
+        attend_kernel(bins, heads, head_size, order, *refs)
 
     return pl.pallas_call(
         body,
@@ -279,22 +343,26 @@
         in_specs=[smem(), smem(), vmem(), vmem()],
         out_specs=(vmem(), vmem()),
         scratch_shapes=[
-            pltpu.VMEM((3, heads, slots, head_size), bf16),
-            pltpu.VMEM((heads, slots, head_size), bf16),
+            pltpu.VMEM((3, bins * heads, slots, head_size), bf16),
+            pltpu.VMEM((bins * heads, slots, head_size), bf16),
         ],
         cost_estimate=pl.CostEstimate(
-            flops=2 * slots * slots * width, transcendentals=slots * slots * heads // 2, bytes_accessed=8 * slots * width
+            flops=2 * bins * slots * slots * width,
+            transcendentals=bins * slots * slots * heads // 2,
+            bytes_accessed=8 * bins * slots * width,
         ),
         name="attend",
     )(where, slopes, near, far)
 
 
-def attend_one_back(near, far, grad_near, grad_far, where, slopes, heads, head_size):
-    slots = 2 * near.shape[0]
+def attend_one_back(near, far, grad_near, grad_far, order, where, slopes, heads, head_size):
+    bins = max(order) + 1
+    slots = 2 * near.shape[0] // bins
+    width = heads * head_size
     half = jax.ShapeDtypeStruct(near.shape, bf16)
 
     def body(*refs):
-        attend_back_kernel(heads, head_size, *refs)
+        attend_back_kernel(bins, heads, head_size, order, *refs)
 
     return pl.pallas_call(
         body,
@@ -302,22 +370,17 @@
         in_specs=[smem(), smem(), vmem(), vmem(), vmem(), vmem()],
         out_specs=(vmem(), vmem()),
         scratch_shapes=[
-            pltpu.VMEM((4, heads, slots, head_size), bf16),
+            pltpu.VMEM((4, bins * heads, slots, head_size), bf16),
             pltpu.VMEM((2, slots, head_size), f32),
-            pltpu.VMEM((3, heads, slots, head_size), bf16),
+            pltpu.VMEM((3, bins * heads, slots, head_size), bf16),
         ],
         cost_estimate=pl.CostEstimate(
-            flops=5 * slots * slots * heads * head_size,
-            transcendentals=slots * slots * heads // 2,
-            bytes_accessed=16 * slots * heads * head_size,
+            flops=5 * bins * slots * slots * width,
+            transcendentals=bins * slots * slots * heads // 2,
+            bytes_accessed=16 * bins * slots * width,
         ),
         name="attend_back",
     )(where, slopes, near, far, grad_near, grad_far)
-
-
-def reorder(near, far, order):
-    pieces = jnp.concatenate([near, far], axis=0).reshape(-1, BLK, near.shape[-1])
-    return jnp.take(pieces, order, axis=0).reshape(-1, near.shape[-1])
 
 
 def block_view(query, keys, values, segment, place, valid, slopes, heads, head_size):
@@ -423,7 +486,7 @@
     nz = lax.axis_size("tensor")
     p = lax.axis_index("dp")
     z = lax.axis_index("tensor")
-    bin_slots, columns = tokens.shape
+    bin_slots, _ = tokens.shape
     blocks = bin_slots // BLK
     assert blocks == n and n % nz == 0 and n % 2 == 0
     here = n // nz
@@ -439,7 +502,7 @@
 
     small = [first_gain, first_shift, out_bias, second_gain, second_shift, down_bias]
     small = small + [attention_bias.reshape(-1), up_bias.reshape(-1)]
-    small = small + [t.astype(bf16) for t in (source_block, target_block, block_fill, block_start)]
+    small = small + [t.astype(bf16) for t in (target_block, block_fill, block_start)]
     packed = small_gather(jnp.concatenate(small))
     at = 6 * shard
     vectors = packed[:, :at].reshape(n, 6, shard).transpose(1, 0, 2).reshape(6, 1, d).astype(f32)
@@ -451,8 +514,8 @@
     size = up_bias.size
     up_z = packed[:, at : at + size].reshape(n, up_bias.shape[0], up_bias.shape[1])
     up_z = up_z.transpose(1, 0, 2).reshape(n, units)
-    tables = packed[:, at + size :].reshape(n, 4, blocks).transpose(1, 0, 2).astype(jnp.int32)
-    source, target, fill, start = [tables[i] for i in range(4)]
+    tables = packed[:, at + size :].reshape(n, 3, blocks).transpose(1, 0, 2).astype(jnp.int32)
+    target, fill, start = [tables[i] for i in range(3)]
     if even_heads:
         bias_z = lax.dynamic_slice_in_dim(bias_z, p * (width // nz), width // nz, 1)
         head_ids = jnp.arange(nz, dtype=jnp.int32)[:, None] * heads_z + p * (heads_z // n)
@@ -479,28 +542,54 @@
     def over_bins(value, axis):
         return lax.all_gather(value, "tensor", axis=axis, tiled=True)
 
-    wanted = lax.dynamic_index_in_dim(source, p, 1, keepdims=False)
-    near, far = plane_gather(tokens)
-    out_weight, up_weight, down_weight, cotangent = after(
-        (attention_out, up_weight, down_weight, cotangent), (near, far)
-    )
-    rows_in = to_bins(pick_blocks(near, far, wanted // blocks, wanted % blocks, blocks), here)
-    near, far = plane_gather(after(cotangent, rows_in))
-    grad_in = to_bins(pick_blocks(near, far, wanted // blocks, wanted % blocks, blocks), here)
-
     if even_heads:
         in_rows = over_bins(spread_out(attention_in.transpose(0, 2, 1), 1, 2), 1)
-        out_rows = over_bins(spread_out(out_weight, 0, 1), 0)
     else:
         in_rows = spread_out(over_bins(attention_in, 2).transpose(0, 2, 1), 1, 2)
-        out_rows = spread_out(over_bins(out_weight, 0), 0, 1)
     in_rows = in_rows.reshape(3 * width, d)
+    first_bin = z * here
+    ranks = jnp.arange(n, dtype=jnp.int32)
+    color = spread_blocks(target.reshape(-1))
+    match = color[:, :, None] == ranks[None, None, :]
+    held = jnp.sum(jnp.where(match, target[:, :, None], 0), axis=1)
+    color = lax.dynamic_index_in_dim(color, p, 0, keepdims=False)
+    leave = jnp.sum(jnp.where(color[:, None] == ranks[None, :], ranks[:, None], 0), axis=0)
+    held_bin = lax.dynamic_index_in_dim(held // blocks, p, 1, keepdims=False)
+    held_by = jnp.sum(jnp.where(held_bin[:, None] == ranks[None, :], ranks[:, None], 0), axis=0)
+
+    ahead = (first_bin + ranks) % n
+    at_ahead = held_by[ahead]
+    behind = (first_bin + here - 1 - ranks // here * here) % n
+    behind = behind - (here - 1) + ranks % here
+    place_of = jnp.sum(jnp.where(behind[None, :] == held_bin[:, None], ranks[None, :], 0), axis=1)
+
+    def bring(rows):
+        rows = spread_out(pick_blocks(rows, leave), 0, 0)
+        return pick_blocks(rows, at_ahead)
+
+    def bring_on(rows):
+        return to_bins(jnp.split(rows, nz, axis=0))
+
+    def take_back(rows):
+        return spread_out(pick_blocks(from_bins(rows), place_of), 0, 0)
+
+    rows_in = bring(tokens)
+    cotangent = after(cotangent, rows_in)
+    rows_in = bring_on(rows_in)
+    if even_heads:
+        out_rows = over_bins(spread_out(attention_out, 0, 1), 0)
+    else:
+        out_rows = spread_out(over_bins(attention_out, 0), 0, 1)
     up_part = over_bins(spread_out(up_weight, 1, 0), 1)
     down_part = over_bins(spread_out(down_weight, 0, 1), 0)
-
-    first_bin = z * here
-    kinds = near_kinds() + [k + 1 for k in near_kinds()]
-    where = jnp.array(kinds, jnp.int32) ^ p
+    grad_in = bring(cotangent)
+
+    gathered = near_order(here)
+    gathered = gathered + [(k + 1, b) for k, b in gathered]
+    order = [b for _, b in gathered]
+    of_bin = [held // blocks == first_bin + g for g in range(here)]
+    slot_of = jnp.stack([jnp.sum(jnp.where(match, held % blocks, 0), axis=0) for match in of_bin])
+    where = slot_of[jnp.array(order), jnp.array([k for k, _ in gathered], jnp.int32) ^ p]
     single = bin_slots == MAXLEN
     offset = jnp.arange(bin_slots, dtype=jnp.int32) % BLK
     block_of = jnp.arange(bin_slots, dtype=jnp.int32) // BLK
@@ -511,102 +600,107 @@
         segment = spread(bin_start)
         valid = offset < spread(bin_fill)
         place = (block_of - segment) * BLK + offset
-        valid_rows = jnp.arange(BLK, dtype=jnp.int32) < lax.dynamic_index_in_dim(bin_fill, p, 0)
-        return segment, place, valid, valid_rows[:, None]
-
-    inverse = [kinds.index(k) for k in range(n)]
-    order = jnp.array(inverse, jnp.int32)[jnp.arange(n, dtype=jnp.int32) ^ p]
-
-    def split_rows(rows):
-        back = jnp.take(rows.reshape(n, BLK, -1), where, axis=0).reshape(rows.shape)
-        return back[: bin_slots // 2], back[bin_slots // 2 :]
-
-    def attend(near, far, g):
+        slot = lax.dynamic_index_in_dim(slot_of[g], p, 0, keepdims=False)
+        valid_rows = jnp.arange(BLK, dtype=jnp.int32) < lax.dynamic_index_in_dim(bin_fill, slot, 0)
+        return segment, place, valid, valid_rows
+
+    sort_key = where + n * jnp.array(order, jnp.int32)
+    unsorted = jnp.argsort(sort_key)
+
+    def by_bin(near, far):
+        rows = jnp.concatenate([near, far], axis=0).reshape(here * n, BLK, -1)
+        return jnp.take(rows, unsorted, axis=0).reshape(here, bin_slots, -1)
+
+    def as_gathered(rows):
+        rows = jnp.take(rows.reshape(here * n, BLK, -1), sort_key, axis=0)
+        rows = rows.reshape(here * bin_slots, -1)
+        return rows[: here * bin_slots // 2], rows[here * bin_slots // 2 :]
+
+    def attend(near, far):
         if single:
-            return attend_one(near, far, where, slopes, heads, head_size)
-        segment, place, valid, _ = bin_tables(g)
-        rows = reorder(near, far, order)
-        query, keys, values = rows[:, :width], rows[:, width : 2 * width], rows[:, 2 * width :]
-        return split_rows(
-            attend_any(query, keys, values, segment, place, valid, slopes, heads, head_size)
-        )
-
-    def attend_back(near, far, grad_near, grad_far, g):
+            return attend_one(near, far, order, where, slopes, heads, head_size)
+        rows = by_bin(near, far)
+        mixed = []
+        for g in range(here):
+            query, keys, values = jnp.split(rows[g], 3, axis=1)
+            tables = bin_tables(g)[:3]
+            mixed.append(attend_any(query, keys, values, *tables, slopes, heads, head_size))
+        return as_gathered(jnp.stack(mixed))
+
+    def attend_back(near, far, grad_near, grad_far):
         if single:
-            return attend_one_back(near, far, grad_near, grad_far, where, slopes, heads, head_size)
-        segment, place, valid, _ = bin_tables(g)
-        rows = reorder(near, far, order)
-        grad = reorder(grad_near, grad_far, order)
-        query, keys, values = rows[:, :width], rows[:, width : 2 * width], rows[:, 2 * width :]
-        return split_rows(
-            attend_any_back(query, keys, values, grad, segment, place, valid, slopes, heads, head_size)
-        )
-
-    streams = []
-    for g in range(here):
-        s = {}
-        s["valid"] = bin_tables(g)[3]
-        s["x"] = rows_in[g].astype(f32)
-        s["grad"] = jnp.where(s["valid"], grad_in[g].astype(f32), 0.0)
-        s["unit_one"], s["scale_one"] = normalize(s["x"])
-        norm_one = (s["unit_one"] * gain_one + shift_one).astype(bf16)
-        s["one"] = plane_gather(norm_one)
-        s["qkv"] = [(contract(v, in_rows, 1, 1) + qkv_bias).astype(bf16) for v in s["one"]]
-        s["att"] = attend(*s["qkv"], g)
-        resid = s["x"] + plane_sum(*s["att"], out_rows, 0) + out_shift
-        s["unit_two"], s["scale_two"] = normalize(resid)
-        norm_two = (s["unit_two"] * gain_two + shift_two).astype(bf16)
-        s["two"] = plane_gather(norm_two)
-        s["hidden"], s["slope"] = [], []
-        for v in s["two"]:
-            before = jnp.dot(v, up_part, preferred_element_type=f32) + up_shift
-            share = 0.5 * (1.0 + lax.erf(before * root_half))
-            s["hidden"].append((before * share).astype(bf16))
-            density = jnp.exp(-0.5 * before * before) * density_scale
-            s["slope"].append((share + before * density).astype(bf16))
-        s["resid"] = resid
-        s["branch"] = plane_gather(s["grad"].astype(bf16))
-        streams.append(s)
+            return attend_one_back(near, far, grad_near, grad_far, order, where, slopes, heads, head_size)
+        rows = by_bin(near, far)
+        grad = by_bin(grad_near, grad_far)
+        grads = []
+        for g in range(here):
+            query, keys, values = jnp.split(rows[g], 3, axis=1)
+            tables = bin_tables(g)[:3]
+            grads.append(
+                attend_any_back(query, keys, values, grad[g], *tables, slopes, heads, head_size)
+            )
+        return as_gathered(jnp.stack(grads))
+
+    valid = jnp.concatenate([bin_tables(g)[3] for g in range(here)])[:, None]
+    x = rows_in.astype(f32)
+    unit_one, scale_one = normalize(x)
+    one = plane_gather((unit_one * gain_one + shift_one).astype(bf16), here)
+    one = after(one, grad_in)
+    grad_in = bring_on(grad_in)
+    qkv = [(contract(v, in_rows, 1, 1) + qkv_bias).astype(bf16) for v in one]
+    att = attend(*after(qkv, grad_in))
+    grad = jnp.where(valid, grad_in.astype(f32), 0.0)
+    branch = plane_gather(grad.astype(bf16), here)
+    resid = x + plane_sum(*att, out_rows, 0, here) + out_shift
+    unit_two, scale_two = normalize(resid)
+    norm_two = (unit_two * gain_two + shift_two).astype(bf16)
+    two = plane_gather(norm_two, here)
+    hidden, slope = [], []
+    for v in two:
+        before = jnp.dot(v, up_part, preferred_element_type=f32) + up_shift
+        share = 0.5 * (1.0 + lax.erf(before * root_half))
+        hidden.append((before * share).astype(bf16))
+        density = jnp.exp(-0.5 * before * before) * density_scale
+        slope.append((share + before * density).astype(bf16))
 
     def pairs_sum(left, right):
-        a = jnp.concatenate([v for s in streams for v in s[left]], axis=0)
-        b = jnp.concatenate([v for s in streams for v in s[right]], axis=0)
-        return contract(a, b, 0, 0)
-
-    down_grad = pairs_sum("hidden", "branch").astype(bf16)
-    branches = after([s["branch"] for s in streams], down_grad)
-    down_grad = lax.psum_scatter(down_grad, "tensor", scatter_dimension=0, tiled=True)
+        a = jnp.concatenate(left, axis=0)
+        b = jnp.concatenate(right, axis=0)
+        return contract(a, b, 0, 0).astype(bf16)
+
+    down_sum = pairs_sum(hidden, branch)
+    down_grad = lax.psum_scatter(down_sum, "tensor", scatter_dimension=0, tiled=True)
     down_grad = spread_out(down_grad, 1, 0).astype(f32)
-    for s, branch in zip(streams, branches):
-        s["before"] = [
-            (contract(v, down_part, 1, 1) * slope.astype(f32)).astype(bf16)
-            for v, slope in zip(branch, s["slope"])
-        ]
-    up_grad = pairs_sum("two", "before").astype(bf16)
-    up_grad = lax.psum_scatter(up_grad, "tensor", scatter_dimension=1, tiled=True)
+    grad_before = [
+        (contract(v, down_part, 1, 1) * w.astype(f32)).astype(bf16) for v, w in zip(branch, slope)
+    ]
+    up_sum = pairs_sum(two, grad_before)
+    up_grad = lax.psum_scatter(up_sum, "tensor", scatter_dimension=1, tiled=True)
     up_grad = spread_out(up_grad, 0, 1).astype(f32)
-    up_bias_grad = sum(jnp.sum(v.astype(f32), axis=0) for s in streams for v in s["before"])
-    for g, s in enumerate(streams):
-        grad_two = plane_sum(*s["before"], up_part, 1)
-        s["gain_two"] = jnp.sum(grad_two * s["unit_two"], axis=0)
-        s["shift_two"] = jnp.sum(grad_two, axis=0)
-        s["grad_resid"] = s["grad"] + norm_back(grad_two, s["unit_two"], s["scale_two"], gain_two)
-        s["attn"] = plane_gather(s["grad_resid"].astype(bf16))
-        grad_att = [contract(v, out_rows, 1, 1).astype(bf16) for v in s["attn"]]
-        s["grad_qkv"] = attend_back(*s["qkv"], *grad_att, g)
-    results = []
-    for s in streams:
-        result = s["resid"] + plane_sum(*s["hidden"], down_part, 0) + down_shift
-        results.append(jnp.where(s["valid"], result, 0.0).astype(bf16))
-    output = from_bins(jnp.stack(results))
-    out_grad = pairs_sum("att", "attn").astype(bf16)
+    up_bias_grad = sum(jnp.sum(v.astype(f32), axis=0) for v in grad_before)
+    grad_two = plane_sum(*grad_before, up_part, 1, here)
+    grad_resid = grad + norm_back(grad_two, unit_two, scale_two, gain_two)
+    attn = plane_gather(after(grad_resid.astype(bf16), down_sum), here)
+    out_grad = pairs_sum(att, attn)
+    grad_att = [contract(v, out_rows, 1, 1).astype(bf16) for v in attn]
+    both_out = sum_pair(*after(hidden, attn), down_part, 0)
+    first_out = sum_first(both_out, here)
+    grad_att = after(grad_att, (up_sum, out_grad, down_grad, both_out))
+    grad_qkv = attend_back(*qkv, *grad_att)
+    grad_qkv, first_out = lax.optimization_barrier((grad_qkv, first_out))
+    second_out = sum_second(both_out, first_out, here)
     if even_heads:
         out_grad = lax.psum_scatter(out_grad, "tensor", scatter_dimension=0, tiled=True)
         out_grad = spread_out(out_grad, 1, 0).astype(f32)
     else:
         out_grad = spread_out(out_grad, 1, 0)
         out_grad = lax.psum_scatter(out_grad, "tensor", scatter_dimension=0, tiled=True).astype(f32)
-    in_grad = pairs_sum("grad_qkv", "one").astype(bf16).reshape(3, width, d)
+    both_one = sum_pair(*grad_qkv, in_rows, 0)
+    first_one = sum_first(both_one, here)
+    result = resid + sum_last(both_out, first_out, second_out, here) + down_shift
+    result = jnp.where(valid, result, 0.0).astype(bf16)
+    output = pick_blocks(take_back(result), color)
+    in_grad = pairs_sum(grad_qkv, one).reshape(3, width, d)
     if even_heads:
         in_grad = in_grad.reshape(3, nz, width // nz, d).transpose(1, 0, 2, 3).reshape(-1, d)
         in_grad = lax.psum_scatter(in_grad, "tensor", scatter_dimension=0, tiled=True)
@@ -615,38 +709,23 @@
         in_grad = spread_out(in_grad, 2, 1)
         in_grad = lax.psum_scatter(in_grad, "tensor", scatter_dimension=1, tiled=True)
     in_grad = in_grad.transpose(0, 2, 1).astype(f32)
-    bias_grad = sum(jnp.sum(v.astype(f32), axis=0) for s in streams for v in s["grad_qkv"])
+    bias_grad = sum(jnp.sum(v.astype(f32), axis=0) for v in grad_qkv)
     bias_grad = jnp.stack([bias_grad[:width], bias_grad[2 * width :]])
-
-    input_rows = []
-    for s in streams:
-        grad_one = plane_sum(*s["grad_qkv"], in_rows, 0)
-        s["gain_one"] = jnp.sum(grad_one * s["unit_one"], axis=0)
-        s["shift_one"] = jnp.sum(grad_one, axis=0)
-        grad_x = s["grad_resid"] + norm_back(grad_one, s["unit_one"], s["scale_one"], gain_one)
-        input_rows.append(grad_x.astype(bf16))
-    input_grad = from_bins(jnp.stack(input_rows))
-
-    wanted = lax.dynamic_index_in_dim(target, p, 0, keepdims=False)
-
-    def to_anchor(blocks_here):
-        near, far = plane_gather(blocks_here.reshape(n * BLK, columns))
-        return pick_blocks(near, far, wanted % blocks, wanted // blocks, n).reshape(bin_slots, columns)
-
-    output = to_anchor(output)
-    input_grad = to_anchor(input_grad)
-
-    def over_streams(name):
-        return sum(s[name] for s in streams)
+    first_one = after(first_one, result)
+    second_one = sum_second(both_one, first_one, here)
+    grad_one = sum_last(both_one, first_one, second_one, here)
+    input_rows = grad_resid + norm_back(grad_one, unit_one, scale_one, gain_one)
+    input_grad = take_back(after(input_rows.astype(bf16), (up_grad, out_grad)))
+    input_grad = pick_blocks(after(input_grad, in_grad), color)
 
     vectors = jnp.stack(
         [
-            over_streams("gain_one"),
-            over_streams("shift_one"),
-            sum(jnp.sum(s["grad_resid"], axis=0) for s in streams),
-            over_streams("gain_two"),
-            over_streams("shift_two"),
-            sum(jnp.sum(s["grad"], axis=0) for s in streams),
+            jnp.sum(grad_one * unit_one, axis=0),
+            jnp.sum(grad_one, axis=0),
+            jnp.sum(grad_resid, axis=0),
+            jnp.sum(grad_two * unit_two, axis=0),
+            jnp.sum(grad_two, axis=0),
+            jnp.sum(grad, axis=0),
         ]
     ).reshape(6, n, shard).transpose(1, 0, 2).reshape(n, -1)
     if even_heads:

time: 1130 us -> 993 us (0.88)
  other arithmetic: 144 us -> 52.9 us
  waiting for transfers between devices: 346 us -> 429 us
  starting transfers between devices: 211 us -> 129 us
  between operations: 79.9 us -> 20.1 us
  Pallas kernels: 58.5 us -> 78.2 us
    concatenate x20 -> x4, other arithmetic: 68.5 us -> 2.1 us  [the longest x2 2.08 us: from_bins(): return jnp.concatenate(pieces, axis=0)]
    ppermute x18, starting transfers between devices: 75.7 us -> 22.8 us  [turn(): lax.ppermute(value, 'tensor', [(i, (i + r) % count) for i in range(count)])]
    all_gather x4, waiting for transfers between devices: 0.03 us -> 51.6 us  [over_bins(): return lax.all_gather(value, 'tensor', axis=axis, tiled=True)]
    ppermute x110 -> x50, starting transfers between devices: 106 us -> 59.3 us  [swap(): return lax.ppermute(value, 'dp', [(i, i ^ k) for i in range(count)])]
    all_to_all x8 -> x12, waiting for transfers between devices: 17.3 us -> 63.2 us  [spread_out(): lax.all_to_all(value, 'dp', split_axis=split, concat_axis=join, tiled=True)]
    unnamed x40 -> x8, other arithmetic: 39.4 us -> 5.39 us
    pallas_call x0 -> x9, Pallas kernels: none -> 22.3 us  [the longest x8 18.2 us: pick_blocks(): pl.pallas_call(body, out_shape=jax.ShapeDtypeStruct((count * BLK, rows.sh...]
    ppermute x110 -> x50, waiting for transfers between devices: 243 us -> 222 us  [swap(): return lax.ppermute(value, 'dp', [(i, i ^ k) for i in range(count)])]
  transfers between devices with their start and end apart: 144 -> 88, of which waited for: 58 -> 42; matrix products, arithmetic and copies ran while one was open for 34% -> 27% of each run, Pallas kernels for 5% -> 7%
where the time goes in v2:
time: 993 us; the launch traced here: 985 us
  waiting for transfers between devices  429 us (43%)
  matrix products  145 us (15%)
  local copies, waits for them, and re-layouts  131 us (13%)
  starting transfers between devices  129 us (13%)
  Pallas kernels  78.2 us (8%)
  other arithmetic  52.9 us (5%)
  between operations  20.1 us (2%)
    ppermute x50, waiting for transfers between devices, swap(): return lax.ppermute(value, 'dp', [(i, i ^ k) for i in range(count)])  222 us
    dot_general x18, matrix products, contract(): lax.dot_general(a, b, (((left,), (right,)), ((), ())), preferred_element_...  126 us
    ppermute x18, waiting for transfers between devices, turn(): lax.ppermute(value, 'tensor', [(i, (i + r) % count) for i in range(count)])  81.6 us
    unnamed x169, local copies, waits for them, and re-layouts  65.4 us
    all_to_all x12, waiting for transfers between devices, spread_out(): lax.all_to_all(value, 'dp', split_axis=split, concat_axis=join, tiled=True)  63.2 us
    ppermute x50, starting transfers between devices, swap(): return lax.ppermute(value, 'dp', [(i, i ^ k) for i in range(count)])  59.3 us
    all_gather x4, waiting for transfers between devices, over_bins(): return lax.all_gather(value, 'tensor', axis=axis, tiled=True)  51.6 us
    all_to_all x12, starting transfers between devices, spread_out(): lax.all_to_all(value, 'dp', split_axis=split, concat_axis=join, tiled=True)  46.8 us
  transfers between devices with their start and end apart: 88, of which 42 were waited for; matrix products, arithmetic and copies ran while one was open for 27% of the time, Pallas kernels for 7%

profile of v2, /device:TPU:0, one launch (start us, length us, event | category | flops | bytes accessed | tf_op | source)
XLA Modules:
  0.0 984.7 jit_solution(994568444416461481)
XLA Ops:
  10.7 4.1 concatenate.108
  26.7 4.1 spread_blocks.1
  35.6 4.2 all-to-all-start
  42.0 13.2 %all-to-all-done = bf16[8,128,512]{2,1,0:T(8,128)(2,1)S(1)} async-done(((bf16[8,128,512]{2,1,0:T(8,128)(2,1)}), bf16[8,128,512]{2,1,0:T(8,128)(2,1)S(1)}, u32[]{:S(2)}, u32[]{:S(2)}) %all-to-all-start) | async-done | bytes 1048608 | tf_op jit(solution)/shard_map/all_to_all | solution.py:540
  65.2 5.8 collective-permute-done.3
  71.1 12.9 %collective-permute-done.4 = bf16[256,512]{1,0:T(8,128)(2,1)S(1)} collective-permute-done((bf16[256,512]{1,0:T(8,128)(2,1)S(1)}, bf16[256,512]{1,0:T(8,128)(2,1)S(1)}, u32[]{:S(2)}, u32[]{:S(2)}) %collective-permute-start.4) | collective-permute-done | bytes 262176 | tf_op jit(solution)/shard_map/ppermute | solution.py:50
  97.0 17.4 %collective-permute-done.6 = bf16[256,2048]{1,0:T(8,128)(2,1)} collective-permute-done((bf16[256,2048]{1,0:T(8,128)(2,1)}, bf16[256,2048]{1,0:T(8,128)(2,1)}, u32[]{:S(2)}, u32[]{:S(2)}) %collective-permute-start.6) | collective-permute-done | bytes 1048608 | tf_op jit(solution)/shard_map/ppermute | solution.py:45
  118.9 13.6 %collective-permute-done.8 = bf16[256,2048]{1,0:T(8,128)(2,1)S(1)} collective-permute-done((bf16[256,2048]{1,0:T(8,128)(2,1)}, bf16[256,2048]{1,0:T(8,128)(2,1)S(1)}, u32[]{:S(2)}, u32[]{:S(2)}) %collective-permute-start.8) | collective-permute-done | bytes 1048608 | tf_op jit(solution)/shard_map/ppermute | solution.py:45
  135.9 7.3 collective-permute-done.7
  152.4 3.6 all-to-all-start.1
  159.5 11.8 %all-to-all-done.1 = bf16[8,128,512]{2,1,0:T(8,128)(2,1)S(1)} async-done(((bf16[8,128,512]{2,1,0:T(8,128)(2,1)}), bf16[8,128,512]{2,1,0:T(8,128)(2,1)S(1)}, u32[]{:S(2)}, u32[]{:S(2)}) %all-to-all-start.1) | async-done | bytes 1048608 | tf_op jit(solution)/shard_map/all_to_all | solution.py:540
  185.0 10.2 %collective-permute-done.14 = bf16[256,512]{1,0:T(8,128)(2,1)} collective-permute-done((bf16[256,512]{1,0:T(8,128)(2,1)S(1)}, bf16[256,512]{1,0:T(8,128)(2,1)}, u32[]{:S(2)}, u32[]{:S(2)}) %collective-permute-start.14) | collective-permute-done | bytes 262176 | tf_op jit(solution)/shard_map/ppermute | solution.py:50
  196.2 16.7 %collective-permute-done.15 = bf16[256,512]{1,0:T(8,128)(2,1)} collective-permute-done((bf16[256,512]{1,0:T(8,128)(2,1)S(1)}, bf16[256,512]{1,0:T(8,128)(2,1)}, u32[]{:S(2)}, u32[]{:S(2)}) %collective-permute-start.15) | collective-permute-done | bytes 262176 | tf_op jit(solution)/shard_map/ppermute | solution.py:50
  214.9 8.1 add_convert_fusion.5.refs_2_
  223.0 7.0 add_convert_fusion.4.refs_3_
  230.1 19.4 %attend.1 = (bf16[1024,256]{1,0:T(8,128)(2,1)}, bf16[1024,256]{1,0:T(8,128)(2,1)}) custom-call(s32[16]{0:T(128)} %gather_fusion.2, f32[4]{0:T(128)} %multiply_exponential_fusion.refs_1_, bf16[1024,768]{1,0:T(8,128)(2,1)} %add_convert_fusion.5.refs_2_, bf16[1024,768]{1,0:T(8,128)(2,1)} %add_convert_fusion.4.refs_3_), custom_call_target="tpu_custom_call" | custom-call | flops 1073741824 | bytes 4194304 | tf_op jit(solution)/shard_map/attend/pallas_call | solution.py:340
  252.3 7.1 collective-permute-done.17
  279.8 22.4 %all-to-all-done.4 = bf16[256,8,256]{0,2,1:T(8,128)(2,1)S(1)} async-done(((bf16[256,8,256]{0,2,1:T(8,128)(2,1)}), bf16[256,8,256]{0,2,1:T(8,128)(2,1)S(1)}, u32[]{:S(2)}, u32[]{:S(2)}) %all-to-all-start.4) | async-done | bytes 1048608 | tf_op jit(solution)/shard_map/all_to_all | solution.py:540
  311.3 9.7 collective-permute-done.19
  325.6 4.2 all-to-all-start.5
  334.2 13.6 %collective-permute-done.29 = bf16[256,2048]{1,0:T(8,128)(2,1)} collective-permute-done((bf16[256,2048]{1,0:T(8,128)(2,1)}, bf16[256,2048]{1,0:T(8,128)(2,1)}, u32[]{:S(2)}, u32[]{:S(2)}) %collective-permute-start.29) | collective-permute-done | bytes 1048608 | tf_op jit(solution)/shard_map/ppermute | solution.py:45
  357.0 15.5 %collective-permute-done.27 = bf16[256,2048]{1,0:T(8,128)(2,1)S(1)} collective-permute-done((bf16[256,2048]{1,0:T(8,128)(2,1)}, bf16[256,2048]{1,0:T(8,128)(2,1)S(1)}, u32[]{:S(2)}, u32[]{:S(2)}) %collective-permute-start.27) | collective-permute-done | bytes 1048608 | tf_op jit(solution)/shard_map/ppermute | solution.py:45
  379.3 24.8 %collective-permute-done.22 = bf16[256,2048]{1,0:T(8,128)(2,1)S(1)} collective-permute-done((bf16[256,2048]{1,0:T(8,128)(2,1)}, bf16[256,2048]{1,0:T(8,128)(2,1)S(1)}, u32[]{:S(2)}, u32[]{:S(2)}) %collective-permute-start.22) | collective-permute-done | bytes 1048608 | tf_op jit(solution)/shard_map/ppermute | solution.py:45
  433.1 9.9 %fusion.128 = f32[1024,1024]{1,0:T(8,128)} fusion(bf16[1024,2048]{1,0:T(8,128)(2,1)} %collective-permute-done.26, bf16[2048,1024]{1,0:T(8,128)(2,1)} %all-gather.9.cloned.1.call-done), kind=kOutput, calls=%fused_computation.345 | convolution fusion | flops 4294967296 | bytes 12582912 | tf_op jit(solution)/shard_map/dot_general | solution.py:660
  443.0 51.5 %all-gather.11.cloned.1.call-done = bf16[1024,2048]{0,1:T(8,128)(2,1)} async-done(((bf16[256,2048]{0,1:T(8,128)(2,1)}), bf16[1024,2048]{0,1:T(8,128)(2,1)}) %all-gather.11.cloned.1.call-update) | async-done | bytes 4194320 | tf_op jit(solution)/shard_map/all_gather | solution.py:543
  494.6 9.8 convert_reduce_fusion
  505.8 4.8 convolution_convert_fusion.3
  510.6 8.6 multiply_convert_fusion.3
  519.2 10.0 %convert_reduce_fusion.1 = (f32[1024]{0:T(1024)S(1)}, bf16[1024,1024]{1,0:T(8,128)(2,1)}) fusion(f32[1024,1024]{1,0:T(8,128)S(1)} %get-tuple-element.278, f32[1024]{0:T(1024)S(1)} %bitcast.227, bf16[1024,2048]{1,0:T(8,128)(2,1)} %slice_dynamic-update-slice_fusion.7, bf16[1024,2048]{0,1:T(8,128)(2,1)S(1)} %copy-done.43), kind=kOutput, calls=%fused_computation.32 | convolution fusion | flops 4310694912 | bytes 14688256 | tf_op jit(solution)/shard_map/dot_general | solution.py:175
  531.3 7.3 add_convert_fusion.2
  541.8 22.5 %collective-permute-done.33 = bf16[256,2048]{1,0:T(8,128)(2,1)S(1)} collective-permute-done((bf16[256,2048]{1,0:T(8,128)(2,1)S(1)}, bf16[256,2048]{1,0:T(8,128)(2,1)S(1)}, u32[]{:S(2)}, u32[]{:S(2)}) %collective-permute-start.33) | collective-permute-done | bytes 1048608 | tf_op jit(solution)/shard_map/ppermute | solution.py:45
  569.5 8.9 collective-permute-done.34
  581.4 11.3 %fusion.25 = bf16[1024,2048]{1,0:T(8,128)(2,1)} fusion(bf16[2048,2048]{1,0:T(8,128)(2,1)S(1)} %constant_dynamic-update-slice_fusion.15, bf16[1024,1024]{1,0:T(8,128)(2,1)S(1)} %copy-done.52, bf16[1024,1024]{1,0:T(8,128)(2,1)S(1)} %get-tuple-element.44), kind=kOutput, calls=%fused_computation.44 | convolution fusion | flops 8600420352 | bytes 16777216 | tf_op jit(solution)/shard_map/dot_general | solution.py:175
  602.5 19.5 %collective-permute-done.37 = bf16[256,2048]{1,0:T(8,128)(2,1)} collective-permute-done((bf16[256,2048]{1,0:T(8,128)(2,1)S(1)}, bf16[256,2048]{1,0:T(8,128)(2,1)}, u32[]{:S(2)}, u32[]{:S(2)}) %collective-permute-start.37) | collective-permute-done | bytes 1048608 | tf_op jit(solution)/shard_map/ppermute | solution.py:45
  628.5 8.9 collective-permute-done.38
  647.2 11.4 %fusion.22 = bf16[2048,1024]{1,0:T(8,128)(2,1)} fusion(bf16[2048,2048]{1,0:T(8,128)(2,1)S(1)} %constant_dynamic-update-slice_fusion.26, bf16[1024,1024]{1,0:T(8,128)(2,1)S(1)} %copy-done.54, bf16[1024,1024]{1,0:T(8,128)(2,1)S(1)} %copy-done.55), kind=kOutput, calls=%fused_computation.39 | convolution fusion | flops 8600420352 | bytes 16777216 | tf_op jit(solution)/shard_map/dot_general | solution.py:175
  658.7 9.3 convolution_convert_fusion.2
  668.5 5.4 reduce-scatter.5.cloned.1.call-done
  676.2 3.7 all-to-all-start.6
  679.9 4.6 convolution_convert_fusion.6.refs_4_
  684.5 10.8 %all-to-all-done.6 = bf16[256,8,256]{2,0,1:T(8,128)(2,1)S(1)} async-done(((bf16[256,8,256]{2,0,1:T(8,128)(2,1)}), bf16[256,8,256]{2,0,1:T(8,128)(2,1)S(1)}, u32[]{:S(2)}, u32[]{:S(2)}) %all-to-all-start.6) | async-done | bytes 1048608 | tf_op jit(solution)/shard_map/all_to_all | solution.py:540
  696.8 4.8 convolution_convert_fusion.5.refs_5_
  701.6 6.7 add_convert_fusion.1
  717.4 36.5 %attend_back.1 = (bf16[1024,768]{1,0:T(8,128)(2,1)}, bf16[1024,768]{1,0:T(8,128)(2,1)}) custom-call(s32[16]{0:T(128)} %gather_fusion.2, f32[4]{0:T(128)} %multiply_exponential_fusion.refs_1_, bf16[1024,768]{1,0:T(8,128)(2,1)} %add_convert_fusion.5.refs_2_, bf16[1024,768]{1,0:T(8,128)(2,1)} %add_convert_fusion.4.refs_3_, ...), custom_call_target="tpu_custom_call" | custom-call | flops 2684354560 | bytes 8388608 | tf_op jit(solution)/shard_map/attend_back/pallas_call | solution.py:367
  754.0 8.2 convolution_convert_fusion.1
  762.2 3.9 all-to-all-start.8
  766.1 10.3 %fusion.28 = bf16[768,2048]{1,0:T(8,128)(2,1)S(1)} fusion(bf16[1024,2048]{1,0:T(8,128)(2,1)} %collective-permute-done.10, bf16[1024,2048]{1,0:T(8,128)(2,1)} %slice_dynamic-update-slice_fusion, bf16[1024,768]{1,0:T(8,128)(2,1)} %get-tuple-element.53, bf16[1024,768]{1,0:T(8,128)(2,1)} %get-tuple-element.52), kind=kOutput, calls=%fused_computation.45 | convolution fusion | flops 6467092480 | bytes 14680064 | tf_op jit(solution)/shard_map/dot_general | solution.py:175
  785.4 4.9 reduce-scatter.9.cloned.1.call-done
  792.0 4.0 all-to-all-start.9
  797.7 5.1 all-to-all-done.9
  807.8 5.3 add_convert_fusion
  815.4 6.6 collective-permute-done.46
  823.6 14.6 %collective-permute-done.52 = bf16[256,2048]{1,0:T(8,128)(2,1)S(1)} collective-permute-done((bf16[256,2048]{1,0:T(8,128)(2,1)S(1)}, bf16[256,2048]{1,0:T(8,128)(2,1)S(1)}, u32[]{:S(2)}, u32[]{:S(2)}) %collective-permute-start.52) | collective-permute-done | bytes 1048608 | tf_op jit(solution)/shard_map/ppermute | solution.py:45
  838.2 4.7 collective-permute-done.51
  848.5 8.3 collective-permute-done.53
  864.9 4.5 collective-permute-done.49
  869.5 14.7 %collective-permute-done.48 = bf16[256,512]{1,0:T(8,128)(2,1)S(1)} collective-permute-done((bf16[256,512]{1,0:T(8,128)(2,1)S(1)}, bf16[256,512]{1,0:T(8,128)(2,1)S(1)}, u32[]{:S(2)}, u32[]{:S(2)}) %collective-permute-start.48) | collective-permute-done | bytes 262176 | tf_op jit(solution)/shard_map/ppermute | solution.py:50
  887.5 4.2 all-to-all-start.7
  891.8 4.2 copy.142
  896.0 4.3 reshape.561
  912.6 4.1 all-to-all-start.11
  920.6 16.6 %collective-permute-done.56 = bf16[256,512]{1,0:T(8,128)(2,1)S(1)} collective-permute-done((bf16[256,512]{1,0:T(8,128)(2,1)S(1)}, bf16[256,512]{1,0:T(8,128)(2,1)S(1)}, u32[]{:S(2)}, u32[]{:S(2)}) %collective-permute-start.56) | collective-permute-done | bytes 262176 | tf_op jit(solution)/shard_map/ppermute | solution.py:50
  940.5 4.4 all-to-all-start.10
  951.7 8.1 collective-permute-done.67
  (520 shorter events, 300.7 us)
Async XLA Ops:
  35.6 19.6 %all-to-all-start = ((bf16[8,128,512]{2,1,0:T(8,128)(2,1)}), bf16[8,128,512]{2,1,0:T(8,128)(2,1)S(1)}, u32[]{:S(2)}, u32[]{:S(2)}) async-start(bf16[8,128,512]{2,1,0:T(8,128)(2,1)} %bitcast.171), calls=%async_computation | async-start | bytes 2097152 | tf_op jit(solution)/shard_map/all_to_all | solution.py:540
  61.6 22.5 %collective-permute-start.5 = (bf16[256,512]{1,0:T(8,128)(2,1)S(1)}, bf16[256,512]{1,0:T(8,128)(2,1)S(1)}, u32[]{:S(2)}, u32[]{:S(2)}) collective-permute-start(bf16[256,512]{1,0:T(8,128)(2,1)S(1)} %get-tuple-element.232), channel_id=1, source_target_pairs={{0,3},{1,0},{2,1},{3,2},{4,7},{5,4},{6,5},{7,6},{8,11},{9,8},{10,9... | collective-permute-start | bytes 786440 | tf_op jit(solution)/shard_map/ppermute | solution.py:50
  63.8 20.2 %collective-permute-start.4 = (bf16[256,512]{1,0:T(8,128)(2,1)S(1)}, bf16[256,512]{1,0:T(8,128)(2,1)S(1)}, u32[]{:S(2)}, u32[]{:S(2)}) collective-permute-start(bf16[256,512]{1,0:T(8,128)(2,1)S(1)} %get-tuple-element.233), channel_id=1, source_target_pairs={{0,2},{1,3},{2,0},{3,1},{4,6},{5,7},{6,4},{7,5},{8,10},{9,11},{10,... | collective-permute-start | bytes 786440 | tf_op jit(solution)/shard_map/ppermute | solution.py:50
  86.6 27.8 %collective-permute-start.6 = (bf16[256,2048]{1,0:T(8,128)(2,1)}, bf16[256,2048]{1,0:T(8,128)(2,1)}, u32[]{:S(2)}, u32[]{:S(2)}) collective-permute-start(bf16[256,2048]{1,0:T(8,128)(2,1)} %get-tuple-element.179), channel_id=1, source_target_pairs={{0,8},{4,12},{8,0},{12,4},{16,24},{20,28},{24,16},{28,20},{1,9},{5... | collective-permute-start | bytes 3145736 | tf_op jit(solution)/shard_map/ppermute | solution.py:45
  91.5 43.3 %all-to-all-start.2 = ((bf16[3,512,256]{2,0,1:T(4,128)(2,1)}), bf16[3,512,256]{2,0,1:T(4,128)(2,1)S(1)}, u32[]{:S(2)}, u32[]{:S(2)}) async-start(bf16[3,512,256]{2,0,1:T(4,128)(2,1)} %bitcast.18), calls=%async_computation.2 | async-start | bytes 2097152 | tf_op jit(solution)/shard_map/all_to_all | solution.py:540
  95.0 119.9 %all-gather.5.cloned.1.call-start = ((), (), s32[]{:S(2)}) async-start(), calls=%async_computation.16 | async-start | bytes 3932160 | tf_op jit(solution)/shard_map/all_gather | solution.py:543
  95.1 37.3 %collective-permute-start.8 = (bf16[256,2048]{1,0:T(8,128)(2,1)}, bf16[256,2048]{1,0:T(8,128)(2,1)S(1)}, u32[]{:S(2)}, u32[]{:S(2)}) collective-permute-start(bf16[256,2048]{1,0:T(8,128)(2,1)} %get-tuple-element.179), channel_id=1, source_target_pairs={{0,16},{4,20},{8,24},{12,28},{16,0},{20,4},{24,8},{28,12},{1,17},{... | collective-permute-start | bytes 3145736 | tf_op jit(solution)/shard_map/ppermute | solution.py:45
  118.5 24.7 %collective-permute-start.7 = (bf16[128,2048]{1,0:T(8,128)(2,1)}, bf16[128,2048]{1,0:T(8,128)(2,1)}, u32[]{:S(2)}, u32[]{:S(2)}) collective-permute-start(bf16[128,2048]{1,0:T(8,128)(2,1)} %get-tuple-element.230), channel_id=1, source_target_pairs={{0,16},{4,20},{8,24},{12,28},{16,0},{20,4},{24,8},{28,12},{1,17},{... | collective-permute-start | bytes 1572872 | tf_op jit(solution)/shard_map/ppermute | solution.py:45
  150.1 64.8 %collective-permute-start.10 = (bf16[1024,2048]{1,0:T(8,128)(2,1)}, bf16[1024,2048]{1,0:T(8,128)(2,1)}, u32[]{:S(2)}, u32[]{:S(2)}) collective-permute-start(bf16[1024,2048]{1,0:T(8,128)(2,1)} %slice_dynamic-update-slice_fusion), channel_id=1, source_target_pairs={{0,4},{4,0},{8,12},{12,8},{16,20},{20,16},{24,28},{28,24},{1,5},{5... | collective-permute-start | bytes 12582920 | tf_op jit(solution)/shard_map/ppermute | solution.py:45
  152.4 18.9 %all-to-all-start.1 = ((bf16[8,128,512]{2,1,0:T(8,128)(2,1)}), bf16[8,128,512]{2,1,0:T(8,128)(2,1)S(1)}, u32[]{:S(2)}, u32[]{:S(2)}) async-start(bf16[8,128,512]{2,1,0:T(8,128)(2,1)} %bitcast.176), calls=%async_computation.1 | async-start | bytes 2097152 | tf_op jit(solution)/shard_map/all_to_all | solution.py:540
  157.1 22.8 %collective-permute-start.13 = (bf16[384]{0:T(512)(128)(2,1)S(1)}, bf16[384]{0:T(512)(128)(2,1)S(1)}, u32[]{:S(2)}, u32[]{:S(2)}) collective-permute-start(bf16[384]{0:T(512)(128)(2,1)S(1)} %pad_maximum_fusion.12), channel_id=1, source_target_pairs={{0,3},{1,0},{2,1},{3,2},{4,7},{5,4},{6,5},{7,6},{8,11},{9,8},{10,9... | collective-permute-start | bytes 2312 | tf_op jit(solution)/shard_map/ppermute | solution.py:50
  158.8 21.0 %collective-permute-start.12 = (bf16[384]{0:T(512)(128)(2,1)S(1)}, bf16[384]{0:T(512)(128)(2,1)S(1)}, u32[]{:S(2)}, u32[]{:S(2)}) collective-permute-start(bf16[384]{0:T(512)(128)(2,1)S(1)} %pad_maximum_fusion.12), channel_id=1, source_target_pairs={{0,2},{1,3},{2,0},{3,1},{4,6},{5,7},{6,4},{7,5},{8,10},{9,11},{10,... | collective-permute-start | bytes 2312 | tf_op jit(solution)/shard_map/ppermute | solution.py:50
  158.8 20.9 %collective-permute-start.11 = (bf16[384]{0:T(512)(128)(2,1)S(1)}, bf16[384]{0:T(512)(128)(2,1)S(1)}, u32[]{:S(2)}, u32[]{:S(2)}) collective-permute-start(bf16[384]{0:T(512)(128)(2,1)S(1)} %pad_maximum_fusion.12), channel_id=1, source_target_pairs={{0,1},{1,2},{2,3},{3,0},{4,5},{5,6},{6,7},{7,4},{8,9},{9,10},{10,1... | collective-permute-start | bytes 2312 | tf_op jit(solution)/shard_map/ppermute | solution.py:50
  174.7 74.8 %all-gather.7.cloned.1.call-start = ((), (), s32[]{:S(2)}) async-start(), calls=%async_computation.17 | async-start | bytes 1310720 | tf_op jit(solution)/shard_map/all_gather | solution.py:543
  178.4 16.7 %collective-permute-start.14 = (bf16[256,512]{1,0:T(8,128)(2,1)S(1)}, bf16[256,512]{1,0:T(8,128)(2,1)}, u32[]{:S(2)}, u32[]{:S(2)}) collective-permute-start(bf16[256,512]{1,0:T(8,128)(2,1)S(1)} %get-tuple-element.228), channel_id=1, source_target_pairs={{0,1},{1,2},{2,3},{3,0},{4,5},{5,6},{6,7},{7,4},{8,9},{9,10},{10,1... | collective-permute-start | bytes 786440 | tf_op jit(solution)/shard_map/ppermute | solution.py:50
  180.0 32.9 %collective-permute-start.15 = (bf16[256,512]{1,0:T(8,128)(2,1)S(1)}, bf16[256,512]{1,0:T(8,128)(2,1)}, u32[]{:S(2)}, u32[]{:S(2)}) collective-permute-start(bf16[256,512]{1,0:T(8,128)(2,1)S(1)} %get-tuple-element.227), channel_id=1, source_target_pairs={{0,2},{1,3},{2,0},{3,1},{4,6},{5,7},{6,4},{7,5},{8,10},{9,11},{10,... | collective-permute-start | bytes 786440 | tf_op jit(solution)/shard_map/ppermute | solution.py:50
  182.4 31.5 %collective-permute-start.16 = (bf16[256,512]{1,0:T(8,128)(2,1)S(1)}, bf16[256,512]{1,0:T(8,128)(2,1)}, u32[]{:S(2)}, u32[]{:S(2)}) collective-permute-start(bf16[256,512]{1,0:T(8,128)(2,1)S(1)} %get-tuple-element.226), channel_id=1, source_target_pairs={{0,3},{1,0},{2,1},{3,2},{4,7},{5,4},{6,5},{7,6},{8,11},{9,8},{10,9... | collective-permute-start | bytes 786440 | tf_op jit(solution)/shard_map/ppermute | solution.py:50
  264.3 39.2 %collective-permute-start.18 = (bf16[256,2048]{1,0:T(8,128)(2,1)}, bf16[256,2048]{1,0:T(8,128)(2,1)}, u32[]{:S(2)}, u32[]{:S(2)}) collective-permute-start(bf16[256,2048]{1,0:T(8,128)(2,1)} %get-tuple-element.192), channel_id=1, source_target_pairs={{0,8},{4,12},{8,0},{12,4},{16,24},{20,28},{24,16},{28,20},{1,9},{5... | collective-permute-start | bytes 3145736 | tf_op jit(solution)/shard_map/ppermute | solution.py:45
  267.3 34.9 %all-to-all-start.4 = ((bf16[256,8,256]{0,2,1:T(8,128)(2,1)}), bf16[256,8,256]{0,2,1:T(8,128)(2,1)S(1)}, u32[]{:S(2)}, u32[]{:S(2)}) async-start(bf16[256,8,256]{0,2,1:T(8,128)(2,1)} %bitcast.180), calls=%async_computation.4 | async-start | bytes 2097152 | tf_op jit(solution)/shard_map/all_to_all | solution.py:540
  270.8 161.4 %all-gather.9.cloned.1.call-start = ((), (), s32[]{:S(2)}) async-start(), calls=%async_computation.18 | async-start | bytes 5242880 | tf_op jit(solution)/shard_map/all_gather | solution.py:543
  277.9 32.0 %collective-permute-start.20 = (bf16[256,2048]{1,0:T(8,128)(2,1)}, bf16[256,2048]{1,0:T(8,128)(2,1)}, u32[]{:S(2)}, u32[]{:S(2)}) collective-permute-start(bf16[256,2048]{1,0:T(8,128)(2,1)} %get-tuple-element.193), channel_id=1, source_target_pairs={{0,16},{4,20},{8,24},{12,28},{16,0},{20,4},{24,8},{28,12},{1,17},{... | collective-permute-start | bytes 3145736 | tf_op jit(solution)/shard_map/ppermute | solution.py:45
  306.2 14.9 %collective-permute-start.19 = (bf16[128,2048]{1,0:T(8,128)(2,1)S(1)}, bf16[128,2048]{1,0:T(8,128)(2,1)S(1)}, u32[]{:S(2)}, u32[]{:S(2)}) collective-permute-start(bf16[128,2048]{1,0:T(8,128)(2,1)S(1)} %fusion.69), channel_id=1, source_target_pairs={{0,16},{4,20},{8,24},{12,28},{16,0},{20,4},{24,8},{28,12},{1,17},{... | collective-permute-start | bytes 1572872 | tf_op jit(solution)/shard_map/ppermute | solution.py:45
  308.2 39.7 %collective-permute-start.29 = (bf16[256,2048]{1,0:T(8,128)(2,1)}, bf16[256,2048]{1,0:T(8,128)(2,1)}, u32[]{:S(2)}, u32[]{:S(2)}) collective-permute-start(bf16[256,2048]{1,0:T(8,128)(2,1)} %get-tuple-element.175), channel_id=1, source_target_pairs={{0,16},{4,20},{8,24},{12,28},{16,0},{20,4},{24,8},{28,12},{1,17},{... | collective-permute-start | bytes 3145736 | tf_op jit(solution)/shard_map/ppermute | solution.py:45
  323.8 29.2 %collective-permute-start.21 = (bf16[128,2048]{1,0:T(8,128)(2,1)}, bf16[128,2048]{1,0:T(8,128)(2,1)}, u32[]{:S(2)}, u32[]{:S(2)}) collective-permute-start(bf16[128,2048]{1,0:T(8,128)(2,1)} %get-tuple-element.191), channel_id=1, source_target_pairs={{0,8},{4,12},{8,0},{12,4},{16,24},{20,28},{24,16},{28,20},{1,9},{5... | collective-permute-start | bytes 1572872 | tf_op jit(solution)/shard_map/ppermute | solution.py:45
  325.6 82.5 %all-to-all-start.5 = ((bf16[8,256,256]{2,1,0:T(8,128)(2,1)}), bf16[8,256,256]{2,1,0:T(8,128)(2,1)}, u32[]{:S(2)}, u32[]{:S(2)}) async-start(bf16[8,256,256]{2,1,0:T(8,128)(2,1)} %bitcast.188), calls=%async_computation.5 | async-start | bytes 2097152 | tf_op jit(solution)/shard_map/all_to_all | solution.py:540
  329.8 164.7 %all-gather.11.cloned.1.call-start = ((), (), s32[]{:S(2)}) async-start(), calls=%async_computation.19 | async-start | bytes 5242880 | tf_op jit(solution)/shard_map/all_gather | solution.py:543
  329.9 42.6 %collective-permute-start.27 = (bf16[256,2048]{1,0:T(8,128)(2,1)}, bf16[256,2048]{1,0:T(8,128)(2,1)S(1)}, u32[]{:S(2)}, u32[]{:S(2)}) collective-permute-start(bf16[256,2048]{1,0:T(8,128)(2,1)} %get-tuple-element.175), channel_id=1, source_target_pairs={{0,8},{4,12},{8,0},{12,4},{16,24},{20,28},{24,16},{28,20},{1,9},{5... | collective-permute-start | bytes 3145736 | tf_op jit(solution)/shard_map/ppermute | solution.py:45
  349.7 64.4 %collective-permute-start.30 = (bf16[128,2048]{1,0:T(8,128)(2,1)}, bf16[128,2048]{1,0:T(8,128)(2,1)}, u32[]{:S(2)}, u32[]{:S(2)}) collective-permute-start(bf16[128,2048]{1,0:T(8,128)(2,1)} %slice.430), channel_id=1, source_target_pairs={{0,8},{4,12},{8,0},{12,4},{16,24},{20,28},{24,16},{28,20},{1,9},{5... | collective-permute-start | bytes 1572872 | tf_op jit(solution)/shard_map/ppermute | solution.py:45
  357.0 47.2 %collective-permute-start.22 = (bf16[256,2048]{1,0:T(8,128)(2,1)}, bf16[256,2048]{1,0:T(8,128)(2,1)S(1)}, u32[]{:S(2)}, u32[]{:S(2)}) collective-permute-start(bf16[256,2048]{1,0:T(8,128)(2,1)} %get-tuple-element.173), channel_id=1, source_target_pairs={{0,8},{4,12},{8,0},{12,4},{16,24},{20,28},{24,16},{28,20},{1,9},{5... | collective-permute-start | bytes 3145736 | tf_op jit(solution)/shard_map/ppermute | solution.py:45
  375.0 37.0 %collective-permute-start.28 = (bf16[128,2048]{1,0:T(8,128)(2,1)}, bf16[128,2048]{1,0:T(8,128)(2,1)}, u32[]{:S(2)}, u32[]{:S(2)}) collective-permute-start(bf16[128,2048]{1,0:T(8,128)(2,1)} %get-tuple-element.223), channel_id=1, source_target_pairs={{0,16},{4,20},{8,24},{12,28},{16,0},{20,4},{24,8},{28,12},{1,17},{... | collective-permute-start | bytes 1572872 | tf_op jit(solution)/shard_map/ppermute | solution.py:45
  376.8 33.6 %collective-permute-start.24 = (bf16[256,2048]{1,0:T(8,128)(2,1)}, bf16[256,2048]{1,0:T(8,128)(2,1)S(1)}, u32[]{:S(2)}, u32[]{:S(2)}) collective-permute-start(bf16[256,2048]{1,0:T(8,128)(2,1)} %get-tuple-element.173), channel_id=1, source_target_pairs={{0,16},{4,20},{8,24},{12,28},{16,0},{20,4},{24,8},{28,12},{1,17},{... | collective-permute-start | bytes 3145736 | tf_op jit(solution)/shard_map/ppermute | solution.py:45
  410.4 263.6 %reduce-scatter.5.cloned.1.call-start = ((), (), s32[]{:S(2)}) async-start(), calls=%async_computation.20 | async-start | bytes 5242880 | tf_op jit(solution)/shard_map/reduce_scatter | solution.py:672
  431.7 62.8 %collective-permute-start.31 = (bf16[1024,2048]{1,0:T(8,128)(2,1)}, bf16[1024,2048]{1,0:T(8,128)(2,1)}, u32[]{:S(2)}, u32[]{:S(2)}) collective-permute-start(bf16[1024,2048]{1,0:T(8,128)(2,1)} %slice_dynamic-update-slice_fusion.7), channel_id=1, source_target_pairs={{0,4},{4,0},{8,12},{12,8},{16,20},{20,16},{24,28},{28,24},{1,5},{5... | collective-permute-start | bytes 12582920 | tf_op jit(solution)/shard_map/ppermute | solution.py:45
  510.6 18.7 %collective-permute-start.32 = (bf16[1024,2048]{1,0:T(8,128)(2,1)S(1)}, bf16[1024,2048]{1,0:T(8,128)(2,1)S(1)}, u32[]{:S(2)}, u32[]{:S(2)}) collective-permute-start(bf16[1024,2048]{1,0:T(8,128)(2,1)S(1)} %convolution_convert_fusion.3), channel_id=1, source_target_pairs={{0,4},{4,0},{8,12},{12,8},{16,20},{20,16},{24,28},{28,24},{1,5},{5... | collective-permute-start | bytes 12582920 | tf_op jit(solution)/shard_map/ppermute | solution.py:45
  538.8 25.5 %collective-permute-start.33 = (bf16[256,2048]{1,0:T(8,128)(2,1)S(1)}, bf16[256,2048]{1,0:T(8,128)(2,1)S(1)}, u32[]{:S(2)}, u32[]{:S(2)}) collective-permute-start(bf16[256,2048]{1,0:T(8,128)(2,1)S(1)} %get-tuple-element.188), channel_id=1, source_target_pairs={{0,8},{4,12},{8,0},{12,4},{16,24},{20,28},{24,16},{28,20},{1,9},{5... | collective-permute-start | bytes 3145736 | tf_op jit(solution)/shard_map/ppermute | solution.py:45
  540.3 28.9 %collective-permute-start.35 = (bf16[256,2048]{1,0:T(8,128)(2,1)S(1)}, bf16[256,2048]{1,0:T(8,128)(2,1)S(1)}, u32[]{:S(2)}, u32[]{:S(2)}) collective-permute-start(bf16[256,2048]{1,0:T(8,128)(2,1)S(1)} %get-tuple-element.189), channel_id=1, source_target_pairs={{0,16},{4,20},{8,24},{12,28},{16,0},{20,4},{24,8},{28,12},{1,17},{... | collective-permute-start | bytes 3145736 | tf_op jit(solution)/shard_map/ppermute | solution.py:45
  598.1 23.9 %collective-permute-start.37 = (bf16[256,2048]{1,0:T(8,128)(2,1)S(1)}, bf16[256,2048]{1,0:T(8,128)(2,1)}, u32[]{:S(2)}, u32[]{:S(2)}) collective-permute-start(bf16[256,2048]{1,0:T(8,128)(2,1)S(1)} %convert_element_type.401), channel_id=1, source_target_pairs={{0,8},{4,12},{8,0},{12,4},{16,24},{20,28},{24,16},{28,20},{1,9},{5... | collective-permute-start | bytes 3145736 | tf_op jit(solution)/shard_map/ppermute | solution.py:45
  599.8 162.4 %reduce-scatter.7.cloned.1.call-start = ((), (), s32[]{:S(2)}) async-start(), calls=%async_computation.21 | async-start | bytes 5242880 | tf_op jit(solution)/shard_map/reduce_scatter | solution.py:678
  599.9 27.4 %collective-permute-start.39 = (bf16[256,2048]{1,0:T(8,128)(2,1)S(1)}, bf16[256,2048]{1,0:T(8,128)(2,1)S(1)}, u32[]{:S(2)}, u32[]{:S(2)}) collective-permute-start(bf16[256,2048]{1,0:T(8,128)(2,1)S(1)} %convert_element_type.401), channel_id=1, source_target_pairs={{0,16},{4,20},{8,24},{12,28},{16,0},{20,4},{24,8},{28,12},{1,17},{... | collective-permute-start | bytes 3145736 | tf_op jit(solution)/shard_map/ppermute | solution.py:45
  643.7 15.0 %collective-permute-start.41 = (bf16[1024,2048]{1,0:T(8,128)(2,1)}, bf16[1024,2048]{1,0:T(8,128)(2,1)}, u32[]{:S(2)}, u32[]{:S(2)}) collective-permute-start(bf16[1024,2048]{1,0:T(8,128)(2,1)} %slice_dynamic-update-slice_fusion.3), channel_id=1, source_target_pairs={{0,4},{4,0},{8,12},{12,8},{16,20},{20,16},{24,28},{28,24},{1,5},{5... | collective-permute-start | bytes 12582920 | tf_op jit(solution)/shard_map/ppermute | solution.py:45
  668.1 33.6 %collective-permute-start.42 = (bf16[1024,2048]{1,0:T(8,128)(2,1)}, bf16[1024,2048]{1,0:T(8,128)(2,1)}, u32[]{:S(2)}, u32[]{:S(2)}) collective-permute-start(bf16[1024,2048]{1,0:T(8,128)(2,1)} %convolution_convert_fusion.2), channel_id=1, source_target_pairs={{0,4},{4,0},{8,12},{12,8},{16,20},{20,16},{24,28},{28,24},{1,5},{5... | collective-permute-start | bytes 12582920 | tf_op jit(solution)/shard_map/ppermute | solution.py:45
  676.2 19.0 %all-to-all-start.6 = ((bf16[256,8,256]{2,0,1:T(8,128)(2,1)}), bf16[256,8,256]{2,0,1:T(8,128)(2,1)S(1)}, u32[]{:S(2)}, u32[]{:S(2)}) async-start(bf16[256,8,256]{2,0,1:T(8,128)(2,1)} %bitcast.181), calls=%async_computation.7 | async-start | bytes 2097152 | tf_op jit(solution)/shard_map/all_to_all | solution.py:540
  679.9 110.4 %reduce-scatter.9.cloned.1.call-start = ((), (), s32[]{:S(2)}) async-start(), calls=%async_computation.22 | async-start | bytes 1310720 | tf_op jit(solution)/shard_map/reduce_scatter | solution.py:693
  710.1 43.8 %collective-permute-start.44 = (bf16[256,2048]{1,0:T(8,128)(2,1)}, bf16[256,2048]{1,0:T(8,128)(2,1)S(1)}, u32[]{:S(2)}, u32[]{:S(2)}) collective-permute-start(bf16[256,2048]{1,0:T(8,128)(2,1)} %get-tuple-element.185), channel_id=1, source_target_pairs={{0,16},{4,20},{8,24},{12,28},{16,0},{20,4},{24,8},{28,12},{1,17},{... | collective-permute-start | bytes 3145736 | tf_op jit(solution)/shard_map/ppermute | solution.py:45
  710.7 43.3 %collective-permute-start.43 = (bf16[256,2048]{1,0:T(8,128)(2,1)}, bf16[256,2048]{1,0:T(8,128)(2,1)}, u32[]{:S(2)}, u32[]{:S(2)}) collective-permute-start(bf16[256,2048]{1,0:T(8,128)(2,1)} %get-tuple-element.186), channel_id=1, source_target_pairs={{0,8},{4,12},{8,0},{12,4},{16,24},{20,28},{24,16},{28,20},{1,9},{5... | collective-permute-start | bytes 3145736 | tf_op jit(solution)/shard_map/ppermute | solution.py:45
  762.1 45.6 %collective-permute-start.50 = (bf16[1024,2048]{1,0:T(8,128)(2,1)}, bf16[1024,2048]{1,0:T(8,128)(2,1)}, u32[]{:S(2)}, u32[]{:S(2)}) collective-permute-start(bf16[1024,2048]{1,0:T(8,128)(2,1)} %convolution_convert_fusion.1), channel_id=1, source_target_pairs={{0,4},{4,0},{8,12},{12,8},{16,20},{20,16},{24,28},{28,24},{1,5},{5... | collective-permute-start | bytes 12582920 | tf_op jit(solution)/shard_map/ppermute | solution.py:45
  762.2 29.8 %all-to-all-start.8 = ((bf16[8,256,256]{2,1,0:T(8,128)(2,1)}), bf16[8,256,256]{2,1,0:T(8,128)(2,1)S(1)}, u32[]{:S(2)}, u32[]{:S(2)}) async-start(bf16[8,256,256]{2,1,0:T(8,128)(2,1)} %bitcast.189), calls=%async_computation.10 | async-start | bytes 2097152 | tf_op jit(solution)/shard_map/all_to_all | solution.py:540
  766.1 125.7 %reduce-scatter.11.cloned.1.call-start = ((), (), s32[]{:S(2)}) async-start(), calls=%async_computation.23 | async-start | bytes 3932160 | tf_op jit(solution)/shard_map/reduce_scatter | solution.py:706
  783.0 21.7 %collective-permute-start.45 = (bf16[128,2048]{1,0:T(8,128)(2,1)}, bf16[128,2048]{1,0:T(8,128)(2,1)}, u32[]{:S(2)}, u32[]{:S(2)}) collective-permute-start(bf16[128,2048]{1,0:T(8,128)(2,1)} %fusion.61), channel_id=1, source_target_pairs={{0,16},{4,20},{8,24},{12,28},{16,0},{20,4},{24,8},{28,12},{1,17},{... | collective-permute-start | bytes 1572872 | tf_op jit(solution)/shard_map/ppermute | solution.py:45
  807.2 14.9 %collective-permute-start.46 = (bf16[128,2048]{1,0:T(8,128)(2,1)S(1)}, bf16[128,2048]{1,0:T(8,128)(2,1)S(1)}, u32[]{:S(2)}, u32[]{:S(2)}) collective-permute-start(bf16[128,2048]{1,0:T(8,128)(2,1)S(1)} %get-tuple-element.184), channel_id=1, source_target_pairs={{0,8},{4,12},{8,0},{12,4},{16,24},{20,28},{24,16},{28,20},{1,9},{5... | collective-permute-start | bytes 1572872 | tf_op jit(solution)/shard_map/ppermute | solution.py:45
  813.3 24.9 %collective-permute-start.52 = (bf16[256,2048]{1,0:T(8,128)(2,1)S(1)}, bf16[256,2048]{1,0:T(8,128)(2,1)S(1)}, u32[]{:S(2)}, u32[]{:S(2)}) collective-permute-start(bf16[256,2048]{1,0:T(8,128)(2,1)S(1)} %get-tuple-element.181), channel_id=1, source_target_pairs={{0,16},{4,20},{8,24},{12,28},{16,0},{20,4},{24,8},{28,12},{1,17},{... | collective-permute-start | bytes 3145736 | tf_op jit(solution)/shard_map/ppermute | solution.py:45
  813.9 29.0 %collective-permute-start.51 = (bf16[256,2048]{1,0:T(8,128)(2,1)S(1)}, bf16[256,2048]{1,0:T(8,128)(2,1)S(1)}, u32[]{:S(2)}, u32[]{:S(2)}) collective-permute-start(bf16[256,2048]{1,0:T(8,128)(2,1)S(1)} %get-tuple-element.182), channel_id=1, source_target_pairs={{0,8},{4,12},{8,0},{12,4},{16,24},{20,28},{24,16},{28,20},{1,9},{5... | collective-permute-start | bytes 3145736 | tf_op jit(solution)/shard_map/ppermute | solution.py:45
  859.7 40.7 %collective-permute-start.54 = (bf16[128,2048]{1,0:T(8,128)(2,1)}, bf16[128,2048]{1,0:T(8,128)(2,1)}, u32[]{:S(2)}, u32[]{:S(2)}) collective-permute-start(bf16[128,2048]{1,0:T(8,128)(2,1)} %get-tuple-element.180), channel_id=1, source_target_pairs={{0,8},{4,12},{8,0},{12,4},{16,24},{20,28},{24,16},{28,20},{1,9},{5... | collective-permute-start | bytes 1572872 | tf_op jit(solution)/shard_map/ppermute | solution.py:45
  862.7 21.5 %collective-permute-start.48 = (bf16[256,512]{1,0:T(8,128)(2,1)S(1)}, bf16[256,512]{1,0:T(8,128)(2,1)S(1)}, u32[]{:S(2)}, u32[]{:S(2)}) collective-permute-start(bf16[256,512]{1,0:T(8,128)(2,1)S(1)} %get-tuple-element.201), channel_id=1, source_target_pairs={{0,2},{1,3},{2,0},{3,1},{4,6},{5,7},{6,4},{7,5},{8,10},{9,11},{10,... | collective-permute-start | bytes 786440 | tf_op jit(solution)/shard_map/ppermute | solution.py:50
  862.9 21.3 %collective-permute-start.47 = (bf16[256,512]{1,0:T(8,128)(2,1)S(1)}, bf16[256,512]{1,0:T(8,128)(2,1)S(1)}, u32[]{:S(2)}, u32[]{:S(2)}) collective-permute-start(bf16[256,512]{1,0:T(8,128)(2,1)S(1)} %get-tuple-element.202), channel_id=1, source_target_pairs={{0,1},{1,2},{2,3},{3,0},{4,5},{5,6},{6,7},{7,4},{8,9},{9,10},{10,1... | collective-permute-start | bytes 786440 | tf_op jit(solution)/shard_map/ppermute | solution.py:50
  887.5 25.1 %all-to-all-start.7 = ((bf16[8,128,512]{2,1,0:T(8,128)(2,1)}), bf16[8,128,512]{2,1,0:T(8,128)(2,1)}, u32[]{:S(2)}, u32[]{:S(2)}) async-start(bf16[8,128,512]{2,1,0:T(8,128)(2,1)} %bitcast.175), calls=%async_computation.8 | async-start | bytes 2097152 | tf_op jit(solution)/shard_map/all_to_all | solution.py:540
  908.0 29.2 %collective-permute-start.56 = (bf16[256,512]{1,0:T(8,128)(2,1)S(1)}, bf16[256,512]{1,0:T(8,128)(2,1)S(1)}, u32[]{:S(2)}, u32[]{:S(2)}) collective-permute-start(bf16[256,512]{1,0:T(8,128)(2,1)S(1)} %get-tuple-element.197), channel_id=1, source_target_pairs={{0,2},{1,3},{2,0},{3,1},{4,6},{5,7},{6,4},{7,5},{8,10},{9,11},{10,... | collective-permute-start | bytes 786440 | tf_op jit(solution)/shard_map/ppermute | solution.py:50
  910.6 26.6 %collective-permute-start.55 = (bf16[256,512]{1,0:T(8,128)(2,1)S(1)}, bf16[256,512]{1,0:T(8,128)(2,1)S(1)}, u32[]{:S(2)}, u32[]{:S(2)}) collective-permute-start(bf16[256,512]{1,0:T(8,128)(2,1)S(1)} %get-tuple-element.198), channel_id=1, source_target_pairs={{0,1},{1,2},{2,3},{3,0},{4,5},{5,6},{6,7},{7,4},{8,9},{9,10},{10,1... | collective-permute-start | bytes 786440 | tf_op jit(solution)/shard_map/ppermute | solution.py:50
  912.6 27.9 %all-to-all-start.11 = ((bf16[8,2,24576]{2,1,0:T(2,128)(2,1)}), bf16[8,2,24576]{2,1,0:T(2,128)(2,1)S(1)}, u32[]{:S(2)}, u32[]{:S(2)}) async-start(bf16[8,2,24576]{2,1,0:T(2,128)(2,1)} %reshape.561), calls=%async_computation.15 | async-start | bytes 1572864 | tf_op jit(solution)/shard_map/all_to_all | solution.py:540
  916.7 28.2 %collective-permute-start.58 = (f32[8,1920]{1,0:T(8,128)S(1)}, f32[8,1920]{1,0:T(8,128)S(1)}, u32[]{:S(2)}, u32[]{:S(2)}) collective-permute-start(f32[8,1920]{1,0:T(8,128)S(1)} %get-tuple-element.252), channel_id=1, source_target_pairs={{0,1},{1,2},{2,3},{3,0},{4,5},{5,6},{6,7},{7,4},{8,9},{9,10},{10,1... | collective-permute-start | bytes 184328 | tf_op jit(solution)/shard_map/ppermute | solution.py:50
  916.8 28.1 %collective-permute-start.59 = (f32[8,1920]{1,0:T(8,128)S(1)}, f32[8,1920]{1,0:T(8,128)S(1)}, u32[]{:S(2)}, u32[]{:S(2)}) collective-permute-start(f32[8,1920]{1,0:T(8,128)S(1)} %get-tuple-element.253), channel_id=1, source_target_pairs={{0,2},{1,3},{2,0},{3,1},{4,6},{5,7},{6,4},{7,5},{8,10},{9,11},{10,... | collective-permute-start | bytes 184328 | tf_op jit(solution)/shard_map/ppermute | solution.py:50
  919.2 25.7 %collective-permute-start.60 = (f32[8,1920]{1,0:T(8,128)S(1)}, f32[8,1920]{1,0:T(8,128)S(1)}, u32[]{:S(2)}, u32[]{:S(2)}) collective-permute-start(f32[8,1920]{1,0:T(8,128)S(1)} %get-tuple-element.254), channel_id=1, source_target_pairs={{0,3},{1,0},{2,1},{3,2},{4,7},{5,4},{6,5},{7,6},{8,11},{9,8},{10,9... | collective-permute-start | bytes 184328 | tf_op jit(solution)/shard_map/ppermute | solution.py:50
  940.5 33.6 %all-to-all-start.10 = ((bf16[8,128,512]{2,1,0:T(8,128)(2,1)}), bf16[8,128,512]{2,1,0:T(8,128)(2,1)S(1)}, u32[]{:S(2)}, u32[]{:S(2)}) async-start(bf16[8,128,512]{2,1,0:T(8,128)(2,1)} %bitcast.172), calls=%async_computation.13 | async-start | bytes 2097152 | tf_op jit(solution)/shard_map/all_to_all | solution.py:540
  948.2 14.5 %collective-permute-start.66 = (f32[1920]{0:T(1024)S(1)}, f32[1920]{0:T(1024)S(1)}, u32[]{:S(2)}, u32[]{:S(2)}) collective-permute-start(f32[1920]{0:T(1024)S(1)} %get-tuple-element.150), channel_id=1, source_target_pairs={{0,24},{4,28},{8,16},{12,20},{16,8},{20,12},{24,0},{28,4},{1,25},{... | collective-permute-start | bytes 23048 | tf_op jit(solution)/shard_map/ppermute | solution.py:45
  (86 other events, 1378.9 us)
Sparse Core Ops, SparseCore 0:
  136.1 78.7 all-gather.4
  217.0 27.9 all-gather.6
  303.6 83.9 all-gather.8
  410.5 84.0 all-gather.10
  600.0 73.9 reduce-scatter.4
  676.1 77.2 reduce-scatter.6
  762.3 27.9 reduce-scatter.8
  792.6 58.9 reduce-scatter.10

commit v3 on v2

--- a/solution.py
+++ b/solution.py
@@ -95,8 +95,12 @@
         a, b = [v.astype(f32) for v in first]
         c = both[7 * half :].astype(f32) + a[half:]
         d = both[2 * half : 3 * half].astype(f32) + b[:half]
-        return [swap(c.astype(bf16), 4), swap(d.astype(bf16), 2)]
+        return [c.astype(bf16), d.astype(bf16)]
     return []
+
+
+def swap_second(values):
+    return [swap(value, k) for value, k in zip(values, (4, 2))]
 
 
 def sum_last(both, first, second, bins):
@@ -117,7 +121,7 @@
 def plane_sum(near, far, weight, dim, bins):
     both = sum_pair(near, far, weight, dim)
     first = sum_first(both, bins)
-    second = sum_second(both, first, bins)
+    second = swap_second(sum_second(both, first, bins))
     return sum_last(both, first, second, bins)
 
 
@@ -160,15 +164,15 @@
     return out
 
 
-def from_bins(rows):
+def bin_pieces(rows):
     count = lax.axis_size("tensor")
     z = lax.axis_index("tensor")
     wide = rows.shape[-1] // count
-    pieces = []
-    for r in range(count):
-        piece = lax.dynamic_slice_in_dim(rows, ((z + r) % count) * wide, wide, 1)
-        pieces.append(turn(piece, r) if r else piece)
-    return jnp.concatenate(pieces, axis=0)
+    return [lax.dynamic_slice_in_dim(rows, ((z + r) % count) * wide, wide, 1) for r in range(count)]
+
+
+def from_bins(pieces):
+    return jnp.concatenate([turn(v, r) if r else v for r, v in enumerate(pieces)], axis=0)
 
 
 def contract(a, b, left, right):
@@ -570,9 +574,6 @@
     def bring_on(rows):
         return to_bins(jnp.split(rows, nz, axis=0))
 
-    def take_back(rows):
-        return spread_out(pick_blocks(from_bins(rows), place_of), 0, 0)
-
     rows_in = bring(tokens)
     cotangent = after(cotangent, rows_in)
     rows_in = bring_on(rows_in)
@@ -670,36 +671,43 @@
 
     down_sum = pairs_sum(hidden, branch)
     down_grad = lax.psum_scatter(down_sum, "tensor", scatter_dimension=0, tiled=True)
-    down_grad = spread_out(down_grad, 1, 0).astype(f32)
     grad_before = [
         (contract(v, down_part, 1, 1) * w.astype(f32)).astype(bf16) for v, w in zip(branch, slope)
     ]
     up_sum = pairs_sum(two, grad_before)
     up_grad = lax.psum_scatter(up_sum, "tensor", scatter_dimension=1, tiled=True)
-    up_grad = spread_out(up_grad, 0, 1).astype(f32)
     up_bias_grad = sum(jnp.sum(v.astype(f32), axis=0) for v in grad_before)
-    grad_two = plane_sum(*grad_before, up_part, 1, here)
+    both_two = sum_pair(*grad_before, up_part, 1)
+    first_two = sum_first(both_two, here)
+    second_two = swap_second(sum_second(both_two, first_two, here))
+    grad_two = sum_last(both_two, first_two, second_two, here)
     grad_resid = grad + norm_back(grad_two, unit_two, scale_two, gain_two)
-    attn = plane_gather(after(grad_resid.astype(bf16), down_sum), here)
+    attn = plane_gather(grad_resid.astype(bf16), here)
     out_grad = pairs_sum(att, attn)
     grad_att = [contract(v, out_rows, 1, 1).astype(bf16) for v in attn]
     both_out = sum_pair(*after(hidden, attn), down_part, 0)
     first_out = sum_first(both_out, here)
-    grad_att = after(grad_att, (up_sum, out_grad, down_grad, both_out))
+    grad_att = after(grad_att, (up_sum, out_grad, both_out))
     grad_qkv = attend_back(*qkv, *grad_att)
-    grad_qkv, first_out = lax.optimization_barrier((grad_qkv, first_out))
     second_out = sum_second(both_out, first_out, here)
-    if even_heads:
-        out_grad = lax.psum_scatter(out_grad, "tensor", scatter_dimension=0, tiled=True)
-        out_grad = spread_out(out_grad, 1, 0).astype(f32)
-    else:
-        out_grad = spread_out(out_grad, 1, 0)
-        out_grad = lax.psum_scatter(out_grad, "tensor", scatter_dimension=0, tiled=True).astype(f32)
+    grad_qkv, second_out = lax.optimization_barrier((grad_qkv, second_out))
+    second_out = swap_second(second_out)
     both_one = sum_pair(*grad_qkv, in_rows, 0)
     first_one = sum_first(both_one, here)
     result = resid + sum_last(both_out, first_out, second_out, here) + down_shift
     result = jnp.where(valid, result, 0.0).astype(bf16)
-    output = pick_blocks(take_back(result), color)
+    result_pieces = bin_pieces(result)
+    output = pick_blocks(from_bins(result_pieces), place_of)
+    output = pick_blocks(spread_out(output, 0, 0), color)
+    grad_qkv, up_grad, down_grad = after((grad_qkv, up_grad, down_grad), both_one)
+    down_grad = spread_out(down_grad, 1, 0).astype(f32)
+    up_grad = spread_out(up_grad, 0, 1).astype(f32)
+    if even_heads:
+        out_grad = lax.psum_scatter(out_grad, "tensor", scatter_dimension=0, tiled=True)
+        out_grad = spread_out(after(out_grad, both_one), 1, 0).astype(f32)
+    else:
+        out_grad = spread_out(out_grad, 1, 0)
+        out_grad = lax.psum_scatter(out_grad, "tensor", scatter_dimension=0, tiled=True).astype(f32)
     in_grad = pairs_sum(grad_qkv, one).reshape(3, width, d)
     if even_heads:
         in_grad = in_grad.reshape(3, nz, width // nz, d).transpose(1, 0, 2, 3).reshape(-1, d)
@@ -711,12 +719,12 @@
     in_grad = in_grad.transpose(0, 2, 1).astype(f32)
     bias_grad = sum(jnp.sum(v.astype(f32), axis=0) for v in grad_qkv)
     bias_grad = jnp.stack([bias_grad[:width], bias_grad[2 * width :]])
-    first_one = after(first_one, result)
-    second_one = sum_second(both_one, first_one, here)
+    first_one = after(first_one, result_pieces)
+    second_one = swap_second(sum_second(both_one, first_one, here))
     grad_one = sum_last(both_one, first_one, second_one, here)
     input_rows = grad_resid + norm_back(grad_one, unit_one, scale_one, gain_one)
-    input_grad = take_back(after(input_rows.astype(bf16), (up_grad, out_grad)))
-    input_grad = pick_blocks(after(input_grad, in_grad), color)
+    input_grad = pick_blocks(from_bins(bin_pieces(input_rows.astype(bf16))), place_of)
+    input_grad = pick_blocks(spread_out(input_grad, 0, 0), color)
 
     vectors = jnp.stack(
         [

time: 993 us -> 1010 us (1.017)
    reduce_scatter x1, waiting for transfers between devices: 5.44 us -> 34.5 us  [on_device(): lax.psum_scatter(down_sum, 'tensor', scatter_dimension=0, tiled=True)]
    ppermute x50, waiting for transfers between devices: 222 us -> 208 us  [swap(): return lax.ppermute(value, 'dp', [(i, i ^ k) for i in range(count)])]
    ppermute x18, waiting for transfers between devices: 81.6 us -> 70.4 us  [turn(): lax.ppermute(value, 'tensor', [(i, (i + r) % count) for i in range(count)])]
    unnamed x169 -> x157, local copies, waits for them, and re-layouts: 65.4 us -> 59.7 us
  transfers between devices with their start and end apart: 88 -> 88, of which waited for: 42 -> 41; matrix products, arithmetic and copies ran while one was open for 27% -> 27% of each run, Pallas kernels for 7% -> 7%
where the time goes in v3:
time: 1010 us; the launch traced here: 997 us
  waiting for transfers between devices  427 us (42%)
  matrix products  143 us (14%)
  starting transfers between devices  134 us (13%)
  local copies, waits for them, and re-layouts  133 us (13%)
  Pallas kernels  78.1 us (8%)
  other arithmetic  61.7 us (6%)
  between operations  19.7 us (2%)
    ppermute x50, waiting for transfers between devices, swap(): return lax.ppermute(value, 'dp', [(i, i ^ k) for i in range(count)])  208 us
    dot_general x18, matrix products, contract(): lax.dot_general(a, b, (((left,), (right,)), ((), ())), preferred_element_...  127 us
    all_to_all x12, waiting for transfers between devices, spread_out(): lax.all_to_all(value, 'dp', split_axis=split, concat_axis=join, tiled=True)  70.5 us
    ppermute x18, waiting for transfers between devices, turn(): lax.ppermute(value, 'tensor', [(i, (i + r) % count) for i in range(count)])  70.4 us
    ppermute x50, starting transfers between devices, swap(): return lax.ppermute(value, 'dp', [(i, i ^ k) for i in range(count)])  60 us
    unnamed x157, local copies, waits for them, and re-layouts  59.7 us
    all_to_all x12, starting transfers between devices, spread_out(): lax.all_to_all(value, 'dp', split_axis=split, concat_axis=join, tiled=True)  46.4 us
    all_gather x4, waiting for transfers between devices, over_bins(): return lax.all_gather(value, 'tensor', axis=axis, tiled=True)  43.3 us
  transfers between devices with their start and end apart: 88, of which 41 were waited for; matrix products, arithmetic and copies ran while one was open for 27% of the time, Pallas kernels for 7%

profile of v3, /device:TPU:0, one launch (start us, length us, event | category | flops | bytes accessed | tf_op | source)
XLA Modules:
  0.0 996.9 jit_solution(16756374254976436063)
XLA Ops:
  10.7 4.1 concatenate.108
  26.7 4.1 spread_blocks.1
  35.6 4.2 all-to-all-start
  42.0 13.2 %all-to-all-done = bf16[8,128,512]{2,1,0:T(8,128)(2,1)S(1)} async-done(((bf16[8,128,512]{2,1,0:T(8,128)(2,1)}), bf16[8,128,512]{2,1,0:T(8,128)(2,1)S(1)}, u32[]{:S(2)}, u32[]{:S(2)}) %all-to-all-start) | async-done | bytes 1048608 | tf_op jit(solution)/shard_map/all_to_all | solution.py:544
  65.2 5.8 collective-permute-done.3
  71.1 12.9 %collective-permute-done.4 = bf16[256,512]{1,0:T(8,128)(2,1)S(1)} collective-permute-done((bf16[256,512]{1,0:T(8,128)(2,1)S(1)}, bf16[256,512]{1,0:T(8,128)(2,1)S(1)}, u32[]{:S(2)}, u32[]{:S(2)}) %collective-permute-start.4) | collective-permute-done | bytes 262176 | tf_op jit(solution)/shard_map/ppermute | solution.py:50
  86.6 3.5 collective-permute-start.6
  91.5 3.6 all-to-all-start.2
  97.0 17.4 %collective-permute-done.6 = bf16[256,2048]{1,0:T(8,128)(2,1)} collective-permute-done((bf16[256,2048]{1,0:T(8,128)(2,1)}, bf16[256,2048]{1,0:T(8,128)(2,1)}, u32[]{:S(2)}, u32[]{:S(2)}) %collective-permute-start.6) | collective-permute-done | bytes 1048608 | tf_op jit(solution)/shard_map/ppermute | solution.py:45
  118.8 13.6 %collective-permute-done.8 = bf16[256,2048]{1,0:T(8,128)(2,1)S(1)} collective-permute-done((bf16[256,2048]{1,0:T(8,128)(2,1)}, bf16[256,2048]{1,0:T(8,128)(2,1)S(1)}, u32[]{:S(2)}, u32[]{:S(2)}) %collective-permute-start.8) | collective-permute-done | bytes 1048608 | tf_op jit(solution)/shard_map/ppermute | solution.py:45
  135.9 7.3 collective-permute-done.7
  152.3 3.6 all-to-all-start.1
  159.4 11.8 %all-to-all-done.1 = bf16[8,128,512]{2,1,0:T(8,128)(2,1)S(1)} async-done(((bf16[8,128,512]{2,1,0:T(8,128)(2,1)}), bf16[8,128,512]{2,1,0:T(8,128)(2,1)S(1)}, u32[]{:S(2)}, u32[]{:S(2)}) %all-to-all-start.1) | async-done | bytes 1048608 | tf_op jit(solution)/shard_map/all_to_all | solution.py:544
  171.2 3.4 all-to-all-start.3
  185.2 9.9 collective-permute-done.14
  196.1 16.7 %collective-permute-done.15 = bf16[256,512]{1,0:T(8,128)(2,1)} collective-permute-done((bf16[256,512]{1,0:T(8,128)(2,1)S(1)}, bf16[256,512]{1,0:T(8,128)(2,1)}, u32[]{:S(2)}, u32[]{:S(2)}) %collective-permute-start.15) | collective-permute-done | bytes 262176 | tf_op jit(solution)/shard_map/ppermute | solution.py:50
  214.9 8.0 add_convert_fusion.5.refs_2_
  223.0 7.0 add_convert_fusion.4.refs_3_
  230.0 19.1 %attend.1 = (bf16[1024,256]{1,0:T(8,128)(2,1)}, bf16[1024,256]{1,0:T(8,128)(2,1)}) custom-call(s32[16]{0:T(128)} %gather_fusion.2, f32[4]{0:T(128)} %multiply_exponential_fusion.refs_1_, bf16[1024,768]{1,0:T(8,128)(2,1)} %add_convert_fusion.5.refs_2_, bf16[1024,768]{1,0:T(8,128)(2,1)} %add_convert_fusion.4.refs_3_), custom_call_target="tpu_custom_call" | custom-call | flops 1073741824 | bytes 4194304 | tf_op jit(solution)/shard_map/attend/pallas_call | solution.py:344
  251.9 7.1 collective-permute-done.17
  267.0 3.6 all-to-all-start.4
  279.5 22.4 %all-to-all-done.4 = bf16[256,8,256]{0,2,1:T(8,128)(2,1)S(1)} async-done(((bf16[256,8,256]{0,2,1:T(8,128)(2,1)}), bf16[256,8,256]{0,2,1:T(8,128)(2,1)S(1)}, u32[]{:S(2)}, u32[]{:S(2)}) %all-to-all-start.4) | async-done | bytes 1048608 | tf_op jit(solution)/shard_map/all_to_all | solution.py:544
  311.1 9.7 collective-permute-done.19
  325.3 4.2 all-to-all-start.5
  333.9 13.6 %collective-permute-done.29 = bf16[256,2048]{1,0:T(8,128)(2,1)} collective-permute-done((bf16[256,2048]{1,0:T(8,128)(2,1)}, bf16[256,2048]{1,0:T(8,128)(2,1)}, u32[]{:S(2)}, u32[]{:S(2)}) %collective-permute-start.29) | collective-permute-done | bytes 1048608 | tf_op jit(solution)/shard_map/ppermute | solution.py:45
  356.7 15.5 %collective-permute-done.27 = bf16[256,2048]{1,0:T(8,128)(2,1)S(1)} collective-permute-done((bf16[256,2048]{1,0:T(8,128)(2,1)}, bf16[256,2048]{1,0:T(8,128)(2,1)S(1)}, u32[]{:S(2)}, u32[]{:S(2)}) %collective-permute-start.27) | collective-permute-done | bytes 1048608 | tf_op jit(solution)/shard_map/ppermute | solution.py:45
  379.1 24.8 %collective-permute-done.22 = bf16[256,2048]{1,0:T(8,128)(2,1)S(1)} collective-permute-done((bf16[256,2048]{1,0:T(8,128)(2,1)}, bf16[256,2048]{1,0:T(8,128)(2,1)S(1)}, u32[]{:S(2)}, u32[]{:S(2)}) %collective-permute-start.22) | collective-permute-done | bytes 1048608 | tf_op jit(solution)/shard_map/ppermute | solution.py:45
  432.0 7.9 fusion.128
  442.0 9.1 multiply_convert_fusion.2
  451.1 43.2 %all-gather.11.cloned.1.call-done = bf16[1024,2048]{0,1:T(8,128)(2,1)} async-done(((bf16[256,2048]{0,1:T(8,128)(2,1)}), bf16[1024,2048]{0,1:T(8,128)(2,1)}) %all-gather.11.cloned.1.call-update) | async-done | bytes 4194320 | tf_op jit(solution)/shard_map/all_gather | solution.py:547
  494.3 9.6 convert_reduce_fusion
  504.0 4.8 convolution_convert_fusion.3
  508.9 9.3 convert_reduce_fusion.1
  518.2 6.9 add_convert_fusion.2
  528.3 22.6 %collective-permute-done.33 = bf16[256,2048]{1,0:T(8,128)(2,1)S(1)} collective-permute-done((bf16[256,2048]{1,0:T(8,128)(2,1)S(1)}, bf16[256,2048]{1,0:T(8,128)(2,1)S(1)}, u32[]{:S(2)}, u32[]{:S(2)}) %collective-permute-start.33) | collective-permute-done | bytes 1048608 | tf_op jit(solution)/shard_map/ppermute | solution.py:45
  553.1 11.7 %collective-permute-done.34 = bf16[128,2048]{1,0:T(8,128)(2,1)S(1)} collective-permute-done((bf16[128,2048]{1,0:T(8,128)(2,1)S(1)}, bf16[128,2048]{1,0:T(8,128)(2,1)S(1)}, u32[]{:S(2)}, u32[]{:S(2)}) %collective-permute-start.34) | collective-permute-done | bytes 524320 | tf_op jit(solution)/shard_map/ppermute | solution.py:45
  566.7 11.1 %collective-permute-done.36 = bf16[128,2048]{1,0:T(8,128)(2,1)S(1)} collective-permute-done((bf16[128,2048]{1,0:T(8,128)(2,1)S(1)}, bf16[128,2048]{1,0:T(8,128)(2,1)S(1)}, u32[]{:S(2)}, u32[]{:S(2)}) %collective-permute-start.36) | collective-permute-done | bytes 524320 | tf_op jit(solution)/shard_map/ppermute | solution.py:45
  585.6 19.0 %collective-permute-done.37 = bf16[256,2048]{1,0:T(8,128)(2,1)S(1)} collective-permute-done((bf16[256,2048]{1,0:T(8,128)(2,1)S(1)}, bf16[256,2048]{1,0:T(8,128)(2,1)S(1)}, u32[]{:S(2)}, u32[]{:S(2)}) %collective-permute-start.37) | collective-permute-done | bytes 1048608 | tf_op jit(solution)/shard_map/ppermute | solution.py:45
  611.9 5.3 collective-permute-done.38
  623.9 11.0 %fusion.22 = bf16[2048,1024]{1,0:T(8,128)(2,1)} fusion(bf16[2048,2048]{1,0:T(8,128)(2,1)S(1)} %constant_dynamic-update-slice_fusion.20, bf16[1024,1024]{1,0:T(8,128)(2,1)S(1)} %get-tuple-element.288, bf16[1024,1024]{1,0:T(8,128)(2,1)S(1)} %copy-done.51), kind=kOutput, calls=%fused_computation.39 | convolution fusion | flops 8600420352 | bytes 16777216 | tf_op jit(solution)/shard_map/dot_general | solution.py:179
  635.2 9.4 convolution_convert_fusion.2
  645.1 4.9 constant_dynamic-update-slice_fusion.38
  650.0 13.1 %fusion.25 = bf16[1024,2048]{1,0:T(8,128)(2,1)} fusion(bf16[2048,2048]{1,0:T(8,128)(2,1)} %constant_dynamic-update-slice_fusion.38, bf16[1024,1024]{1,0:T(8,128)(2,1)S(1)} %copy-done.50, bf16[1024,1024]{1,0:T(8,128)(2,1)S(1)} %copy-done.48), kind=kOutput, calls=%fused_computation.44 | convolution fusion | flops 8600420352 | bytes 16777216 | tf_op jit(solution)/shard_map/dot_general | solution.py:179
  664.3 4.4 convolution_convert_fusion.6.refs_4_
  668.8 4.5 convolution_convert_fusion.5.refs_5_
  673.2 6.8 add_convert_fusion.1
  690.6 36.6 %attend_back.1 = (bf16[1024,768]{1,0:T(8,128)(2,1)}, bf16[1024,768]{1,0:T(8,128)(2,1)}) custom-call(s32[16]{0:T(128)} %gather_fusion.2, f32[4]{0:T(128)} %multiply_exponential_fusion.refs_1_, bf16[1024,768]{1,0:T(8,128)(2,1)} %add_convert_fusion.5.refs_2_, bf16[1024,768]{1,0:T(8,128)(2,1)} %add_convert_fusion.4.refs_3_, ...), custom_call_target="tpu_custom_call" | custom-call | flops 2684354560 | bytes 8388608 | tf_op jit(solution)/shard_map/attend_back/pallas_call | solution.py:371
  730.0 4.0 fusion.60
  734.1 5.0 convolution_convert_fusion.1
  740.7 5.9 collective-permute-done.50
  746.6 9.2 add_convert_fusion
  755.7 34.5 %reduce-scatter.7.cloned.1.call-done = bf16[256,2048]{1,0:T(8,128)(2,1)} async-done(((bf16[1024,2048]{1,0:T(8,128)(2,1)}), bf16[256,2048]{1,0:T(8,128)(2,1)}) %reduce-scatter.7.cloned.1.call-update) | async-done | bytes 1048592 | tf_op jit(solution)/shard_map/reduce_scatter | solution.py:673
  790.3 10.1 %fusion.28 = bf16[768,2048]{1,0:T(8,128)(2,1)S(1)} fusion(bf16[1024,2048]{1,0:T(8,128)(2,1)} %collective-permute-done.10, bf16[1024,2048]{1,0:T(8,128)(2,1)} %slice_dynamic-update-slice_fusion, bf16[1024,768]{1,0:T(8,128)(2,1)} %get-tuple-element.58, bf16[1024,768]{1,0:T(8,128)(2,1)} %get-tuple-element.57), kind=kOutput, calls=%fused_computation.45 | convolution fusion | flops 6467092480 | bytes 14680064 | tf_op jit(solution)/shard_map/dot_general | solution.py:179
  817.2 12.9 %collective-permute-done.52 = bf16[256,2048]{1,0:T(8,128)(2,1)S(1)} collective-permute-done((bf16[256,2048]{1,0:T(8,128)(2,1)}, bf16[256,2048]{1,0:T(8,128)(2,1)S(1)}, u32[]{:S(2)}, u32[]{:S(2)}) %collective-permute-start.52) | collective-permute-done | bytes 1048608 | tf_op jit(solution)/shard_map/ppermute | solution.py:45
  846.5 3.9 all-to-all-start.6
  866.3 3.4 all-to-all-start.9
  872.0 7.8 all-to-all-done.9
  879.8 4.2 all-to-all-start.11
  889.1 10.3 %all-to-all-done.11 = bf16[256,8,256]{2,0,1:T(8,128)(2,1)} async-done(((bf16[256,8,256]{2,0,1:T(8,128)(2,1)}), bf16[256,8,256]{2,0,1:T(8,128)(2,1)}, u32[]{:S(2)}, u32[]{:S(2)}) %all-to-all-start.11) | async-done | bytes 1048608 | tf_op jit(solution)/shard_map/all_to_all | solution.py:544
  899.4 4.2 all-to-all-start.10
  913.5 4.7 collective-permute-done.57
  918.2 16.9 %collective-permute-done.56 = bf16[256,512]{1,0:T(8,128)(2,1)S(1)} collective-permute-done((bf16[256,512]{1,0:T(8,128)(2,1)S(1)}, bf16[256,512]{1,0:T(8,128)(2,1)S(1)}, u32[]{:S(2)}, u32[]{:S(2)}) %collective-permute-start.56) | collective-permute-done | bytes 262176 | tf_op jit(solution)/shard_map/ppermute | solution.py:50
  938.5 3.8 all-to-all-start.7
  966.6 4.2 all-to-all-start.8
  (506 shorter events, 310.6 us)
Async XLA Ops:
  35.6 19.6 %all-to-all-start = ((bf16[8,128,512]{2,1,0:T(8,128)(2,1)}), bf16[8,128,512]{2,1,0:T(8,128)(2,1)S(1)}, u32[]{:S(2)}, u32[]{:S(2)}) async-start(bf16[8,128,512]{2,1,0:T(8,128)(2,1)} %bitcast.174), calls=%async_computation | async-start | bytes 2097152 | tf_op jit(solution)/shard_map/all_to_all | solution.py:544
  61.6 22.5 %collective-permute-start.5 = (bf16[256,512]{1,0:T(8,128)(2,1)S(1)}, bf16[256,512]{1,0:T(8,128)(2,1)S(1)}, u32[]{:S(2)}, u32[]{:S(2)}) collective-permute-start(bf16[256,512]{1,0:T(8,128)(2,1)S(1)} %get-tuple-element.238), channel_id=1, source_target_pairs={{0,3},{1,0},{2,1},{3,2},{4,7},{5,4},{6,5},{7,6},{8,11},{9,8},{10,9... | collective-permute-start | bytes 786440 | tf_op jit(solution)/shard_map/ppermute | solution.py:50
  63.8 20.2 %collective-permute-start.4 = (bf16[256,512]{1,0:T(8,128)(2,1)S(1)}, bf16[256,512]{1,0:T(8,128)(2,1)S(1)}, u32[]{:S(2)}, u32[]{:S(2)}) collective-permute-start(bf16[256,512]{1,0:T(8,128)(2,1)S(1)} %get-tuple-element.239), channel_id=1, source_target_pairs={{0,2},{1,3},{2,0},{3,1},{4,6},{5,7},{6,4},{7,5},{8,10},{9,11},{10,... | collective-permute-start | bytes 786440 | tf_op jit(solution)/shard_map/ppermute | solution.py:50
  86.6 27.8 %collective-permute-start.6 = (bf16[256,2048]{1,0:T(8,128)(2,1)}, bf16[256,2048]{1,0:T(8,128)(2,1)}, u32[]{:S(2)}, u32[]{:S(2)}) collective-permute-start(bf16[256,2048]{1,0:T(8,128)(2,1)} %get-tuple-element.185), channel_id=1, source_target_pairs={{0,8},{4,12},{8,0},{12,4},{16,24},{20,28},{24,16},{28,20},{1,9},{5... | collective-permute-start | bytes 3145736 | tf_op jit(solution)/shard_map/ppermute | solution.py:45
  91.5 43.3 %all-to-all-start.2 = ((bf16[3,512,256]{2,0,1:T(4,128)(2,1)}), bf16[3,512,256]{2,0,1:T(4,128)(2,1)S(1)}, u32[]{:S(2)}, u32[]{:S(2)}) async-start(bf16[3,512,256]{2,0,1:T(4,128)(2,1)} %bitcast.18), calls=%async_computation.2 | async-start | bytes 2097152 | tf_op jit(solution)/shard_map/all_to_all | solution.py:544
  95.0 119.9 %all-gather.5.cloned.1.call-start = ((), (), s32[]{:S(2)}) async-start(), calls=%async_computation.16 | async-start | bytes 3932160 | tf_op jit(solution)/shard_map/all_gather | solution.py:547
  95.1 37.3 %collective-permute-start.8 = (bf16[256,2048]{1,0:T(8,128)(2,1)}, bf16[256,2048]{1,0:T(8,128)(2,1)S(1)}, u32[]{:S(2)}, u32[]{:S(2)}) collective-permute-start(bf16[256,2048]{1,0:T(8,128)(2,1)} %get-tuple-element.185), channel_id=1, source_target_pairs={{0,16},{4,20},{8,24},{12,28},{16,0},{20,4},{24,8},{28,12},{1,17},{... | collective-permute-start | bytes 3145736 | tf_op jit(solution)/shard_map/ppermute | solution.py:45
  118.4 24.8 %collective-permute-start.7 = (bf16[128,2048]{1,0:T(8,128)(2,1)}, bf16[128,2048]{1,0:T(8,128)(2,1)}, u32[]{:S(2)}, u32[]{:S(2)}) collective-permute-start(bf16[128,2048]{1,0:T(8,128)(2,1)} %get-tuple-element.236), channel_id=1, source_target_pairs={{0,16},{4,20},{8,24},{12,28},{16,0},{20,4},{24,8},{28,12},{1,17},{... | collective-permute-start | bytes 1572872 | tf_op jit(solution)/shard_map/ppermute | solution.py:45
  150.0 64.8 %collective-permute-start.10 = (bf16[1024,2048]{1,0:T(8,128)(2,1)}, bf16[1024,2048]{1,0:T(8,128)(2,1)}, u32[]{:S(2)}, u32[]{:S(2)}) collective-permute-start(bf16[1024,2048]{1,0:T(8,128)(2,1)} %slice_dynamic-update-slice_fusion), channel_id=1, source_target_pairs={{0,4},{4,0},{8,12},{12,8},{16,20},{20,16},{24,28},{28,24},{1,5},{5... | collective-permute-start | bytes 12582920 | tf_op jit(solution)/shard_map/ppermute | solution.py:45
  152.3 18.9 %all-to-all-start.1 = ((bf16[8,128,512]{2,1,0:T(8,128)(2,1)}), bf16[8,128,512]{2,1,0:T(8,128)(2,1)S(1)}, u32[]{:S(2)}, u32[]{:S(2)}) async-start(bf16[8,128,512]{2,1,0:T(8,128)(2,1)} %bitcast.176), calls=%async_computation.1 | async-start | bytes 2097152 | tf_op jit(solution)/shard_map/all_to_all | solution.py:544
  157.0 22.8 %collective-permute-start.13 = (bf16[384]{0:T(512)(128)(2,1)S(1)}, bf16[384]{0:T(512)(128)(2,1)S(1)}, u32[]{:S(2)}, u32[]{:S(2)}) collective-permute-start(bf16[384]{0:T(512)(128)(2,1)S(1)} %pad_maximum_fusion.12), channel_id=1, source_target_pairs={{0,3},{1,0},{2,1},{3,2},{4,7},{5,4},{6,5},{7,6},{8,11},{9,8},{10,9... | collective-permute-start | bytes 2312 | tf_op jit(solution)/shard_map/ppermute | solution.py:50
  158.7 21.0 %collective-permute-start.12 = (bf16[384]{0:T(512)(128)(2,1)S(1)}, bf16[384]{0:T(512)(128)(2,1)S(1)}, u32[]{:S(2)}, u32[]{:S(2)}) collective-permute-start(bf16[384]{0:T(512)(128)(2,1)S(1)} %pad_maximum_fusion.12), channel_id=1, source_target_pairs={{0,2},{1,3},{2,0},{3,1},{4,6},{5,7},{6,4},{7,5},{8,10},{9,11},{10,... | collective-permute-start | bytes 2312 | tf_op jit(solution)/shard_map/ppermute | solution.py:50
  158.8 20.9 %collective-permute-start.11 = (bf16[384]{0:T(512)(128)(2,1)S(1)}, bf16[384]{0:T(512)(128)(2,1)S(1)}, u32[]{:S(2)}, u32[]{:S(2)}) collective-permute-start(bf16[384]{0:T(512)(128)(2,1)S(1)} %pad_maximum_fusion.12), channel_id=1, source_target_pairs={{0,1},{1,2},{2,3},{3,0},{4,5},{5,6},{6,7},{7,4},{8,9},{9,10},{10,1... | collective-permute-start | bytes 2312 | tf_op jit(solution)/shard_map/ppermute | solution.py:50
  174.6 74.5 %all-gather.7.cloned.1.call-start = ((), (), s32[]{:S(2)}) async-start(), calls=%async_computation.17 | async-start | bytes 1310720 | tf_op jit(solution)/shard_map/all_gather | solution.py:547
  178.4 16.7 %collective-permute-start.14 = (bf16[256,512]{1,0:T(8,128)(2,1)S(1)}, bf16[256,512]{1,0:T(8,128)(2,1)}, u32[]{:S(2)}, u32[]{:S(2)}) collective-permute-start(bf16[256,512]{1,0:T(8,128)(2,1)S(1)} %get-tuple-element.234), channel_id=1, source_target_pairs={{0,1},{1,2},{2,3},{3,0},{4,5},{5,6},{6,7},{7,4},{8,9},{9,10},{10,1... | collective-permute-start | bytes 786440 | tf_op jit(solution)/shard_map/ppermute | solution.py:50
  179.9 32.9 %collective-permute-start.15 = (bf16[256,512]{1,0:T(8,128)(2,1)S(1)}, bf16[256,512]{1,0:T(8,128)(2,1)}, u32[]{:S(2)}, u32[]{:S(2)}) collective-permute-start(bf16[256,512]{1,0:T(8,128)(2,1)S(1)} %get-tuple-element.233), channel_id=1, source_target_pairs={{0,2},{1,3},{2,0},{3,1},{4,6},{5,7},{6,4},{7,5},{8,10},{9,11},{10,... | collective-permute-start | bytes 786440 | tf_op jit(solution)/shard_map/ppermute | solution.py:50
  182.3 31.5 %collective-permute-start.16 = (bf16[256,512]{1,0:T(8,128)(2,1)S(1)}, bf16[256,512]{1,0:T(8,128)(2,1)}, u32[]{:S(2)}, u32[]{:S(2)}) collective-permute-start(bf16[256,512]{1,0:T(8,128)(2,1)S(1)} %get-tuple-element.232), channel_id=1, source_target_pairs={{0,3},{1,0},{2,1},{3,2},{4,7},{5,4},{6,5},{7,6},{8,11},{9,8},{10,9... | collective-permute-start | bytes 786440 | tf_op jit(solution)/shard_map/ppermute | solution.py:50
  264.0 39.3 %collective-permute-start.18 = (bf16[256,2048]{1,0:T(8,128)(2,1)}, bf16[256,2048]{1,0:T(8,128)(2,1)}, u32[]{:S(2)}, u32[]{:S(2)}) collective-permute-start(bf16[256,2048]{1,0:T(8,128)(2,1)} %get-tuple-element.200), channel_id=1, source_target_pairs={{0,8},{4,12},{8,0},{12,4},{16,24},{20,28},{24,16},{28,20},{1,9},{5... | collective-permute-start | bytes 3145736 | tf_op jit(solution)/shard_map/ppermute | solution.py:45
  267.0 34.9 %all-to-all-start.4 = ((bf16[256,8,256]{0,2,1:T(8,128)(2,1)}), bf16[256,8,256]{0,2,1:T(8,128)(2,1)S(1)}, u32[]{:S(2)}, u32[]{:S(2)}) async-start(bf16[256,8,256]{0,2,1:T(8,128)(2,1)} %bitcast.181), calls=%async_computation.4 | async-start | bytes 2097152 | tf_op jit(solution)/shard_map/all_to_all | solution.py:544
  270.5 161.5 %all-gather.9.cloned.1.call-start = ((), (), s32[]{:S(2)}) async-start(), calls=%async_computation.18 | async-start | bytes 5242880 | tf_op jit(solution)/shard_map/all_gather | solution.py:547
  277.6 32.0 %collective-permute-start.20 = (bf16[256,2048]{1,0:T(8,128)(2,1)}, bf16[256,2048]{1,0:T(8,128)(2,1)}, u32[]{:S(2)}, u32[]{:S(2)}) collective-permute-start(bf16[256,2048]{1,0:T(8,128)(2,1)} %get-tuple-element.201), channel_id=1, source_target_pairs={{0,16},{4,20},{8,24},{12,28},{16,0},{20,4},{24,8},{28,12},{1,17},{... | collective-permute-start | bytes 3145736 | tf_op jit(solution)/shard_map/ppermute | solution.py:45
  305.9 14.9 %collective-permute-start.19 = (bf16[128,2048]{1,0:T(8,128)(2,1)S(1)}, bf16[128,2048]{1,0:T(8,128)(2,1)S(1)}, u32[]{:S(2)}, u32[]{:S(2)}) collective-permute-start(bf16[128,2048]{1,0:T(8,128)(2,1)S(1)} %fusion.69), channel_id=1, source_target_pairs={{0,16},{4,20},{8,24},{12,28},{16,0},{20,4},{24,8},{28,12},{1,17},{... | collective-permute-start | bytes 1572872 | tf_op jit(solution)/shard_map/ppermute | solution.py:45
  307.8 39.7 %collective-permute-start.29 = (bf16[256,2048]{1,0:T(8,128)(2,1)}, bf16[256,2048]{1,0:T(8,128)(2,1)}, u32[]{:S(2)}, u32[]{:S(2)}) collective-permute-start(bf16[256,2048]{1,0:T(8,128)(2,1)} %get-tuple-element.167), channel_id=1, source_target_pairs={{0,16},{4,20},{8,24},{12,28},{16,0},{20,4},{24,8},{28,12},{1,17},{... | collective-permute-start | bytes 3145736 | tf_op jit(solution)/shard_map/ppermute | solution.py:45
  323.4 29.2 %collective-permute-start.21 = (bf16[128,2048]{1,0:T(8,128)(2,1)}, bf16[128,2048]{1,0:T(8,128)(2,1)}, u32[]{:S(2)}, u32[]{:S(2)}) collective-permute-start(bf16[128,2048]{1,0:T(8,128)(2,1)} %get-tuple-element.199), channel_id=1, source_target_pairs={{0,8},{4,12},{8,0},{12,4},{16,24},{20,28},{24,16},{28,20},{1,9},{5... | collective-permute-start | bytes 1572872 | tf_op jit(solution)/shard_map/ppermute | solution.py:45
  325.3 82.5 %all-to-all-start.5 = ((bf16[8,256,256]{2,1,0:T(8,128)(2,1)}), bf16[8,256,256]{2,1,0:T(8,128)(2,1)}, u32[]{:S(2)}, u32[]{:S(2)}) async-start(bf16[8,256,256]{2,1,0:T(8,128)(2,1)} %bitcast.188), calls=%async_computation.5 | async-start | bytes 2097152 | tf_op jit(solution)/shard_map/all_to_all | solution.py:544
  329.5 164.8 %all-gather.11.cloned.1.call-start = ((), (), s32[]{:S(2)}) async-start(), calls=%async_computation.19 | async-start | bytes 5242880 | tf_op jit(solution)/shard_map/all_gather | solution.py:547
  329.7 42.6 %collective-permute-start.27 = (bf16[256,2048]{1,0:T(8,128)(2,1)}, bf16[256,2048]{1,0:T(8,128)(2,1)S(1)}, u32[]{:S(2)}, u32[]{:S(2)}) collective-permute-start(bf16[256,2048]{1,0:T(8,128)(2,1)} %get-tuple-element.167), channel_id=1, source_target_pairs={{0,8},{4,12},{8,0},{12,4},{16,24},{20,28},{24,16},{28,20},{1,9},{5... | collective-permute-start | bytes 3145736 | tf_op jit(solution)/shard_map/ppermute | solution.py:45
  349.4 64.5 %collective-permute-start.30 = (bf16[128,2048]{1,0:T(8,128)(2,1)}, bf16[128,2048]{1,0:T(8,128)(2,1)}, u32[]{:S(2)}, u32[]{:S(2)}) collective-permute-start(bf16[128,2048]{1,0:T(8,128)(2,1)} %slice.430), channel_id=1, source_target_pairs={{0,8},{4,12},{8,0},{12,4},{16,24},{20,28},{24,16},{28,20},{1,9},{5... | collective-permute-start | bytes 1572872 | tf_op jit(solution)/shard_map/ppermute | solution.py:45
  356.7 47.2 %collective-permute-start.22 = (bf16[256,2048]{1,0:T(8,128)(2,1)}, bf16[256,2048]{1,0:T(8,128)(2,1)S(1)}, u32[]{:S(2)}, u32[]{:S(2)}) collective-permute-start(bf16[256,2048]{1,0:T(8,128)(2,1)} %get-tuple-element.181), channel_id=1, source_target_pairs={{0,8},{4,12},{8,0},{12,4},{16,24},{20,28},{24,16},{28,20},{1,9},{5... | collective-permute-start | bytes 3145736 | tf_op jit(solution)/shard_map/ppermute | solution.py:45
  374.7 37.1 %collective-permute-start.28 = (bf16[128,2048]{1,0:T(8,128)(2,1)}, bf16[128,2048]{1,0:T(8,128)(2,1)}, u32[]{:S(2)}, u32[]{:S(2)}) collective-permute-start(bf16[128,2048]{1,0:T(8,128)(2,1)} %get-tuple-element.207), channel_id=1, source_target_pairs={{0,16},{4,20},{8,24},{12,28},{16,0},{20,4},{24,8},{28,12},{1,17},{... | collective-permute-start | bytes 1572872 | tf_op jit(solution)/shard_map/ppermute | solution.py:45
  376.6 33.6 %collective-permute-start.24 = (bf16[256,2048]{1,0:T(8,128)(2,1)}, bf16[256,2048]{1,0:T(8,128)(2,1)S(1)}, u32[]{:S(2)}, u32[]{:S(2)}) collective-permute-start(bf16[256,2048]{1,0:T(8,128)(2,1)} %get-tuple-element.181), channel_id=1, source_target_pairs={{0,16},{4,20},{8,24},{12,28},{16,0},{20,4},{24,8},{28,12},{1,17},{... | collective-permute-start | bytes 3145736 | tf_op jit(solution)/shard_map/ppermute | solution.py:45
  410.1 345.6 %reduce-scatter.5.cloned.1.call-start = ((), (), s32[]{:S(2)}) async-start(), calls=%async_computation.20 | async-start | bytes 5242880 | tf_op jit(solution)/shard_map/reduce_scatter | solution.py:678
  425.4 14.5 %collective-permute-start.26 = (bf16[1024,2048]{1,0:T(8,128)(2,1)}, bf16[1024,2048]{1,0:T(8,128)(2,1)}, u32[]{:S(2)}, u32[]{:S(2)}) collective-permute-start(bf16[1024,2048]{1,0:T(8,128)(2,1)} %slice_dynamic-update-slice_fusion.11), channel_id=1, source_target_pairs={{0,4},{4,0},{8,12},{12,8},{16,20},{20,16},{24,28},{28,24},{1,5},{5... | collective-permute-start | bytes 12582920 | tf_op jit(solution)/shard_map/ppermute | solution.py:45
  431.5 62.8 %collective-permute-start.31 = (bf16[1024,2048]{1,0:T(8,128)(2,1)}, bf16[1024,2048]{1,0:T(8,128)(2,1)}, u32[]{:S(2)}, u32[]{:S(2)}) collective-permute-start(bf16[1024,2048]{1,0:T(8,128)(2,1)} %slice_dynamic-update-slice_fusion.7), channel_id=1, source_target_pairs={{0,4},{4,0},{8,12},{12,8},{16,20},{20,16},{24,28},{28,24},{1,5},{5... | collective-permute-start | bytes 12582920 | tf_op jit(solution)/shard_map/ppermute | solution.py:45
  525.3 25.6 %collective-permute-start.33 = (bf16[256,2048]{1,0:T(8,128)(2,1)S(1)}, bf16[256,2048]{1,0:T(8,128)(2,1)S(1)}, u32[]{:S(2)}, u32[]{:S(2)}) collective-permute-start(bf16[256,2048]{1,0:T(8,128)(2,1)S(1)} %get-tuple-element.196), channel_id=1, source_target_pairs={{0,8},{4,12},{8,0},{12,4},{16,24},{20,28},{24,16},{28,20},{1,9},{5... | collective-permute-start | bytes 3145736 | tf_op jit(solution)/shard_map/ppermute | solution.py:45
  526.8 26.0 %collective-permute-start.35 = (bf16[256,2048]{1,0:T(8,128)(2,1)S(1)}, bf16[256,2048]{1,0:T(8,128)(2,1)S(1)}, u32[]{:S(2)}, u32[]{:S(2)}) collective-permute-start(bf16[256,2048]{1,0:T(8,128)(2,1)S(1)} %get-tuple-element.197), channel_id=1, source_target_pairs={{0,16},{4,20},{8,24},{12,28},{16,0},{20,4},{24,8},{28,12},{1,17},{... | collective-permute-start | bytes 3145736 | tf_op jit(solution)/shard_map/ppermute | solution.py:45
  581.5 23.0 %collective-permute-start.37 = (bf16[256,2048]{1,0:T(8,128)(2,1)S(1)}, bf16[256,2048]{1,0:T(8,128)(2,1)S(1)}, u32[]{:S(2)}, u32[]{:S(2)}) collective-permute-start(bf16[256,2048]{1,0:T(8,128)(2,1)S(1)} %get-tuple-element.179), channel_id=1, source_target_pairs={{0,8},{4,12},{8,0},{12,4},{16,24},{20,28},{24,16},{28,20},{1,9},{5... | collective-permute-start | bytes 3145736 | tf_op jit(solution)/shard_map/ppermute | solution.py:45
  583.0 24.8 %collective-permute-start.39 = (bf16[256,2048]{1,0:T(8,128)(2,1)S(1)}, bf16[256,2048]{1,0:T(8,128)(2,1)S(1)}, u32[]{:S(2)}, u32[]{:S(2)}) collective-permute-start(bf16[256,2048]{1,0:T(8,128)(2,1)S(1)} %get-tuple-element.179), channel_id=1, source_target_pairs={{0,16},{4,20},{8,24},{12,28},{16,0},{20,4},{24,8},{28,12},{1,17},{... | collective-permute-start | bytes 3145736 | tf_op jit(solution)/shard_map/ppermute | solution.py:45
  635.0 155.3 %reduce-scatter.7.cloned.1.call-start = ((), (), s32[]{:S(2)}) async-start(), calls=%async_computation.21 | async-start | bytes 5242880 | tf_op jit(solution)/shard_map/reduce_scatter | solution.py:673
  644.6 28.6 %collective-permute-start.42 = (bf16[1024,2048]{1,0:T(8,128)(2,1)}, bf16[1024,2048]{1,0:T(8,128)(2,1)}, u32[]{:S(2)}, u32[]{:S(2)}) collective-permute-start(bf16[1024,2048]{1,0:T(8,128)(2,1)} %convolution_convert_fusion.2), channel_id=1, source_target_pairs={{0,4},{4,0},{8,12},{12,8},{16,20},{20,16},{24,28},{28,24},{1,5},{5... | collective-permute-start | bytes 12582920 | tf_op jit(solution)/shard_map/ppermute | solution.py:45
  663.1 198.3 %reduce-scatter.11.cloned.1.call-start = ((), (), s32[]{:S(2)}) async-start(), calls=%async_computation.23 | async-start | bytes 1310720 | tf_op jit(solution)/shard_map/reduce_scatter | solution.py:706
  681.8 45.4 %collective-permute-start.43 = (bf16[256,2048]{1,0:T(8,128)(2,1)}, bf16[256,2048]{1,0:T(8,128)(2,1)}, u32[]{:S(2)}, u32[]{:S(2)}) collective-permute-start(bf16[256,2048]{1,0:T(8,128)(2,1)} %get-tuple-element.193), channel_id=1, source_target_pairs={{0,8},{4,12},{8,0},{12,4},{16,24},{20,28},{24,16},{28,20},{1,9},{5... | collective-permute-start | bytes 3145736 | tf_op jit(solution)/shard_map/ppermute | solution.py:45
  683.3 45.4 %collective-permute-start.44 = (bf16[256,2048]{1,0:T(8,128)(2,1)}, bf16[256,2048]{1,0:T(8,128)(2,1)S(1)}, u32[]{:S(2)}, u32[]{:S(2)}) collective-permute-start(bf16[256,2048]{1,0:T(8,128)(2,1)} %get-tuple-element.194), channel_id=1, source_target_pairs={{0,16},{4,20},{8,24},{12,28},{16,0},{20,4},{24,8},{28,12},{1,17},{... | collective-permute-start | bytes 3145736 | tf_op jit(solution)/shard_map/ppermute | solution.py:45
  739.1 220.3 %reduce-scatter.9.cloned.1.call-start = ((), (), s32[]{:S(2)}) async-start(), calls=%async_computation.22 | async-start | bytes 3932160 | tf_op jit(solution)/shard_map/reduce_scatter | solution.py:714
  739.2 69.1 %collective-permute-start.45 = (bf16[128,2048]{1,0:T(8,128)(2,1)}, bf16[128,2048]{1,0:T(8,128)(2,1)}, u32[]{:S(2)}, u32[]{:S(2)}) collective-permute-start(bf16[128,2048]{1,0:T(8,128)(2,1)} %get-tuple-element.51), channel_id=1, source_target_pairs={{0,16},{4,20},{8,24},{12,28},{16,0},{20,4},{24,8},{28,12},{1,17},{... | collective-permute-start | bytes 1572872 | tf_op jit(solution)/shard_map/ppermute | solution.py:45
  740.2 68.1 %collective-permute-start.46 = (bf16[128,2048]{1,0:T(8,128)(2,1)}, bf16[128,2048]{1,0:T(8,128)(2,1)}, u32[]{:S(2)}, u32[]{:S(2)}) collective-permute-start(bf16[128,2048]{1,0:T(8,128)(2,1)} %get-tuple-element.52), channel_id=1, source_target_pairs={{0,8},{4,12},{8,0},{12,4},{16,24},{20,28},{24,16},{28,20},{1,9},{5... | collective-permute-start | bytes 1572872 | tf_op jit(solution)/shard_map/ppermute | solution.py:45
  805.3 24.8 %collective-permute-start.52 = (bf16[256,2048]{1,0:T(8,128)(2,1)}, bf16[256,2048]{1,0:T(8,128)(2,1)S(1)}, u32[]{:S(2)}, u32[]{:S(2)}) collective-permute-start(bf16[256,2048]{1,0:T(8,128)(2,1)} %get-tuple-element.187), channel_id=1, source_target_pairs={{0,16},{4,20},{8,24},{12,28},{16,0},{20,4},{24,8},{28,12},{1,17},{... | collective-permute-start | bytes 3145736 | tf_op jit(solution)/shard_map/ppermute | solution.py:45
  806.8 24.6 %collective-permute-start.51 = (bf16[256,2048]{1,0:T(8,128)(2,1)}, bf16[256,2048]{1,0:T(8,128)(2,1)}, u32[]{:S(2)}, u32[]{:S(2)}) collective-permute-start(bf16[256,2048]{1,0:T(8,128)(2,1)} %get-tuple-element.188), channel_id=1, source_target_pairs={{0,8},{4,12},{8,0},{12,4},{16,24},{20,28},{24,16},{28,20},{1,9},{5... | collective-permute-start | bytes 3145736 | tf_op jit(solution)/shard_map/ppermute | solution.py:45
  812.2 29.8 %collective-permute-start.49 = (bf16[256,512]{1,0:T(8,128)(2,1)}, bf16[256,512]{1,0:T(8,128)(2,1)}, u32[]{:S(2)}, u32[]{:S(2)}) collective-permute-start(bf16[256,512]{1,0:T(8,128)(2,1)} %get-tuple-element.215), channel_id=1, source_target_pairs={{0,3},{1,0},{2,1},{3,2},{4,7},{5,4},{6,5},{7,6},{8,11},{9,8},{10,9... | collective-permute-start | bytes 786440 | tf_op jit(solution)/shard_map/ppermute | solution.py:50
  815.0 27.0 %collective-permute-start.48 = (bf16[256,512]{1,0:T(8,128)(2,1)}, bf16[256,512]{1,0:T(8,128)(2,1)}, u32[]{:S(2)}, u32[]{:S(2)}) collective-permute-start(bf16[256,512]{1,0:T(8,128)(2,1)} %get-tuple-element.216), channel_id=1, source_target_pairs={{0,2},{1,3},{2,0},{3,1},{4,6},{5,7},{6,4},{7,5},{8,10},{9,11},{10,... | collective-permute-start | bytes 786440 | tf_op jit(solution)/shard_map/ppermute | solution.py:50
  815.2 26.9 %collective-permute-start.47 = (bf16[256,512]{1,0:T(8,128)(2,1)}, bf16[256,512]{1,0:T(8,128)(2,1)}, u32[]{:S(2)}, u32[]{:S(2)}) collective-permute-start(bf16[256,512]{1,0:T(8,128)(2,1)} %get-tuple-element.217), channel_id=1, source_target_pairs={{0,1},{1,2},{2,3},{3,0},{4,5},{5,6},{6,7},{7,4},{8,9},{9,10},{10,1... | collective-permute-start | bytes 786440 | tf_op jit(solution)/shard_map/ppermute | solution.py:50
  834.8 20.5 %collective-permute-start.53 = (bf16[128,2048]{1,0:T(8,128)(2,1)}, bf16[128,2048]{1,0:T(8,128)(2,1)}, u32[]{:S(2)}, u32[]{:S(2)}) collective-permute-start(bf16[128,2048]{1,0:T(8,128)(2,1)} %fusion.57), channel_id=1, source_target_pairs={{0,16},{4,20},{8,24},{12,28},{16,0},{20,4},{24,8},{28,12},{1,17},{... | collective-permute-start | bytes 1572872 | tf_op jit(solution)/shard_map/ppermute | solution.py:45
  846.5 19.8 %all-to-all-start.6 = ((bf16[8,128,512]{2,1,0:T(8,128)(2,1)}), bf16[8,128,512]{2,1,0:T(8,128)(2,1)S(1)}, u32[]{:S(2)}, u32[]{:S(2)}) async-start(bf16[8,128,512]{2,1,0:T(8,128)(2,1)} %bitcast.177), calls=%async_computation.6 | async-start | bytes 2097152 | tf_op jit(solution)/shard_map/all_to_all | solution.py:544
  859.4 24.6 %collective-permute-start.54 = (bf16[128,2048]{1,0:T(8,128)(2,1)}, bf16[128,2048]{1,0:T(8,128)(2,1)}, u32[]{:S(2)}, u32[]{:S(2)}) collective-permute-start(bf16[128,2048]{1,0:T(8,128)(2,1)} %get-tuple-element.186), channel_id=1, source_target_pairs={{0,8},{4,12},{8,0},{12,4},{16,24},{20,28},{24,16},{28,20},{1,9},{5... | collective-permute-start | bytes 1572872 | tf_op jit(solution)/shard_map/ppermute | solution.py:45
  879.8 19.6 %all-to-all-start.11 = ((bf16[256,8,256]{2,0,1:T(8,128)(2,1)}), bf16[256,8,256]{2,0,1:T(8,128)(2,1)}, u32[]{:S(2)}, u32[]{:S(2)}) async-start(bf16[256,8,256]{2,0,1:T(8,128)(2,1)} %bitcast.161), calls=%async_computation.15 | async-start | bytes 2097152 | tf_op jit(solution)/shard_map/all_to_all | solution.py:544
  899.4 39.1 %all-to-all-start.10 = ((bf16[8,256,256]{2,1,0:T(8,128)(2,1)}), bf16[8,256,256]{2,1,0:T(8,128)(2,1)}, u32[]{:S(2)}, u32[]{:S(2)}) async-start(bf16[8,256,256]{2,1,0:T(8,128)(2,1)} %bitcast.189), calls=%async_computation.14 | async-start | bytes 2097152 | tf_op jit(solution)/shard_map/all_to_all | solution.py:544
  911.4 23.7 %collective-permute-start.56 = (bf16[256,512]{1,0:T(8,128)(2,1)S(1)}, bf16[256,512]{1,0:T(8,128)(2,1)S(1)}, u32[]{:S(2)}, u32[]{:S(2)}) collective-permute-start(bf16[256,512]{1,0:T(8,128)(2,1)S(1)} %get-tuple-element.212), channel_id=1, source_target_pairs={{0,2},{1,3},{2,0},{3,1},{4,6},{5,7},{6,4},{7,5},{8,10},{9,11},{10,... | collective-permute-start | bytes 786440 | tf_op jit(solution)/shard_map/ppermute | solution.py:50
  911.6 23.6 %collective-permute-start.55 = (bf16[256,512]{1,0:T(8,128)(2,1)S(1)}, bf16[256,512]{1,0:T(8,128)(2,1)S(1)}, u32[]{:S(2)}, u32[]{:S(2)}) collective-permute-start(bf16[256,512]{1,0:T(8,128)(2,1)S(1)} %get-tuple-element.213), channel_id=1, source_target_pairs={{0,1},{1,2},{2,3},{3,0},{4,5},{5,6},{6,7},{7,4},{8,9},{9,10},{10,1... | collective-permute-start | bytes 786440 | tf_op jit(solution)/shard_map/ppermute | solution.py:50
  938.5 28.1 %all-to-all-start.7 = ((bf16[8,128,512]{2,1,0:T(8,128)(2,1)}), bf16[8,128,512]{2,1,0:T(8,128)(2,1)S(1)}, u32[]{:S(2)}, u32[]{:S(2)}) async-start(bf16[8,128,512]{2,1,0:T(8,128)(2,1)} %bitcast.172), calls=%async_computation.7 | async-start | bytes 2097152 | tf_op jit(solution)/shard_map/all_to_all | solution.py:544
  951.6 14.6 %collective-permute-start.67 = (f32[1920]{0:T(1024)S(1)}, f32[1920]{0:T(1024)S(1)}, u32[]{:S(2)}, u32[]{:S(2)}) collective-permute-start(f32[1920]{0:T(1024)S(1)} %get-tuple-element.153), channel_id=1, source_target_pairs={{0,28},{4,24},{8,20},{12,16},{16,12},{20,8},{24,4},{28,0},{1,29},{... | collective-permute-start | bytes 23048 | tf_op jit(solution)/shard_map/ppermute | solution.py:45
  957.4 19.1 %collective-permute-start.66 = (f32[1920]{0:T(1024)S(1)}, f32[1920]{0:T(1024)S(1)}, u32[]{:S(2)}, u32[]{:S(2)}) collective-permute-start(f32[1920]{0:T(1024)S(1)} %get-tuple-element.154), channel_id=1, source_target_pairs={{0,24},{4,28},{8,16},{12,20},{16,8},{20,12},{24,0},{28,4},{1,25},{... | collective-permute-start | bytes 23048 | tf_op jit(solution)/shard_map/ppermute | solution.py:45
  957.8 18.8 %collective-permute-start.65 = (f32[1920]{0:T(1024)S(1)}, f32[1920]{0:T(1024)S(1)}, u32[]{:S(2)}, u32[]{:S(2)}) collective-permute-start(f32[1920]{0:T(1024)S(1)} %get-tuple-element.155), channel_id=1, source_target_pairs={{0,20},{4,16},{8,28},{12,24},{16,4},{20,0},{24,12},{28,8},{1,21},{... | collective-permute-start | bytes 23048 | tf_op jit(solution)/shard_map/ppermute | solution.py:45
  958.8 17.7 %collective-permute-start.64 = (f32[1920]{0:T(1024)S(1)}, f32[1920]{0:T(1024)S(1)}, u32[]{:S(2)}, u32[]{:S(2)}) collective-permute-start(f32[1920]{0:T(1024)S(1)} %get-tuple-element.156), channel_id=1, source_target_pairs={{0,16},{4,20},{8,24},{12,28},{16,0},{20,4},{24,8},{28,12},{1,17},{... | collective-permute-start | bytes 23048 | tf_op jit(solution)/shard_map/ppermute | solution.py:45
  966.6 16.8 %all-to-all-start.8 = ((bf16[8,2,24576]{2,1,0:T(2,128)(2,1)}), bf16[8,2,24576]{2,1,0:T(2,128)(2,1)}, u32[]{:S(2)}, u32[]{:S(2)}) async-start(bf16[8,2,24576]{2,1,0:T(2,128)(2,1)} %reshape.561), calls=%async_computation.11 | async-start | bytes 1572864 | tf_op jit(solution)/shard_map/all_to_all | solution.py:544
  (80 other events, 1208.8 us)
Sparse Core Ops, SparseCore 0:
  136.0 78.8 all-gather.4
  217.1 27.9 all-gather.6
  303.3 84.0 all-gather.8
  410.2 84.0 all-gather.10
  635.1 75.6 reduce-scatter.4
  712.9 77.2 reduce-scatter.6
  792.6 29.9 reduce-scatter.10
  824.8 68.3 reduce-scatter.8
